TPU v7x, 32 devices: a whole 2x2x4 slice. The times are simulated.
32 devices in a mesh: groups: 2 (over x), seq: 8 (over z, y), tp: 2 (over core).
Axes of the slice: x: 2, y: 2, z: 4, core: 2. Of those that a mesh axis runs over, the one named last changes fastest.
Arguments:
- queries: bfloat16 [4096, 8192], P(('groups', 'seq', 'tp')), parts along dimension 0, may hold values from -10 to 10
- keys: bfloat16 [4096, 1024], P(('groups', 'seq', 'tp')), parts along dimension 0, may hold values from -10 to 10
- values: bfloat16 [4096, 1024], P(('groups', 'seq', 'tp')), parts along dimension 0, may hold values from -6 to 6
- vertical_blocks: int32 [64, 2], replicated, may hold values from 0 to 15, as said below
- vertical_count: int32 [64], replicated, may hold values from 1 to 2, as said below
- slash_offsets: int32 [64, 2], replicated, may hold values from 1 to 15, as said below
- slash_count: int32 [64], replicated, may hold values from 1 to 2, as said below
Outputs:
- attention: bfloat16 [4096, 8192], P(('groups', 'seq', 'tp')), parts along dimension 0
There are 2 independent parts, one for each index of `groups`. A program takes and returns all parts, laid end to end along the dimension named above; an argument that names none is the same for every part. Nothing has to cross between parts.
Inputs may be any that keep to these rules, and one draw needn't show every extreme that they name: `vertical_blocks`: the 2 entries of one head are distinct. `vertical_count`: some head uses all 2 entries. `slash_offsets`: the 2 entries of one head are distinct. `slash_count`: some head uses all 2 entries.
All inputs are finite; a program needn't handle non-finite values.
Results may differ from a plain program's by a relative error of at most 0.0037.
Values may be sent and summed in bfloat16 or wider, within the bound.
No kernel may reach another device: no remote copies, remote signals or barrier semaphores. Data moves between devices by JAX's collectives and lax.ppermute only.
A program may use at most 128 MiB of HBM per device.

v0:
```python
import jax
import jax.numpy as jnp
import numpy as np
from jax import lax
from jax.sharding import PartitionSpec as P

QUERY_HEADS = 64
KEY_VALUE_HEADS = 8
HEAD_SIZE = 128
MASK_BLOCK_SIZE = 128


def head_attend(
    query_blocks,
    block_index,
    row_offset,
    key_blocks,
    value_blocks,
    verticals,
    vertical_live,
    slash_list,
    slash_live,
):
    query_rows = query_blocks.shape[1]
    scaling = query_blocks.shape[2] ** (-0.5)
    total_block_count = key_blocks.shape[0]
    block_width = key_blocks.shape[1]
    block_total = block_index.shape[0]
    vertical_entries = jnp.arange(verticals.shape[0])
    slash_entries = jnp.arange(slash_list.shape[0])
    member = jnp.any(
        (jnp.arange(total_block_count)[:, None] == verticals[None, :])
        & (vertical_entries < vertical_live)[None, :],
        axis=1,
    )
    vertical_active = (block_index[:, None] > verticals[None, :]) & (
        vertical_entries < vertical_live
    )[None, :]
    targets = block_index[:, None] - slash_list[None, :]
    safe_targets = jnp.clip(targets, 0, total_block_count - 1)
    slash_active = (
        (targets >= 0)
        & (slash_entries < slash_live)[None, :]
        & jnp.logical_not(jnp.take(member, safe_targets))
    )
    tile_index = jnp.concatenate(
        [
            block_index[:, None],
            jnp.broadcast_to(verticals[None, :], (block_total, verticals.shape[0])),
            safe_targets,
        ],
        axis=1,
    )
    tile_active = jnp.concatenate(
        [jnp.ones((block_total, 1), bool), vertical_active, slash_active], axis=1
    )
    tile_keys = jnp.take(key_blocks, tile_index, axis=0)
    tile_values = jnp.take(value_blocks, tile_index, axis=0)
    scores = (
        jnp.einsum("nqd,ntkd->nqtk", query_blocks, tile_keys, preferred_element_type=jnp.float32)
        * scaling
    )
    query_pos = row_offset + jnp.arange(query_rows)
    causal = query_pos[:, None] >= jnp.arange(block_width)[None, :]
    off_diagonal = (jnp.arange(tile_index.shape[1]) > 0)[None, None, :, None]
    allowed = tile_active[:, None, :, None] & (causal[None, :, None, :] | off_diagonal)
    scores = jnp.where(allowed, scores, -jnp.inf)
    peak = jnp.max(scores, axis=(2, 3))
    weights = jnp.exp(scores - peak[:, :, None, None])
    total = jnp.sum(weights, axis=(2, 3))
    rounded = weights.astype(jnp.bfloat16)
    numerator = jnp.einsum(
        "nqtk,ntkd->nqd", rounded, tile_values, preferred_element_type=jnp.float32
    )
    return (numerator / total[..., None]).astype(jnp.bfloat16)


def shards(queries, keys, values, vertical_blocks, vertical_count, slash_offsets, slash_count):
    local_token_count = queries.shape[0]
    seq_ranks = lax.axis_size("seq")
    core_count = lax.axis_size("tp")
    core_index = lax.axis_index("tp")
    rank_index = lax.axis_index("seq")
    heads_rank = QUERY_HEADS // seq_ranks
    heads_per_group = QUERY_HEADS // KEY_VALUE_HEADS
    kv_rank = max(1, heads_rank // heads_per_group)
    query_width = heads_rank * HEAD_SIZE
    kv_width = kv_rank * HEAD_SIZE
    key_value_lookup = (
        (
            np.arange(seq_ranks)[:, None] * heads_rank // heads_per_group
            + np.arange(kv_rank)[None, :]
        )
        .reshape(-1)
        .astype(np.int32)
    )
    key_selection = jnp.take(
        keys.reshape(local_token_count, KEY_VALUE_HEADS, HEAD_SIZE), key_value_lookup, axis=1
    ).reshape(local_token_count, seq_ranks * kv_width)
    value_selection = jnp.take(
        values.reshape(local_token_count, KEY_VALUE_HEADS, HEAD_SIZE), key_value_lookup, axis=1
    ).reshape(local_token_count, seq_ranks * kv_width)
    per_shard = local_token_count // MASK_BLOCK_SIZE
    total_block_count = seq_ranks * core_count * per_shard
    query_got, key_portion, value_part = (
        lax.all_to_all(queries, "seq", split_axis=1, concat_axis=0, tiled=True),
        lax.all_to_all(key_selection, "seq", split_axis=1, concat_axis=0, tiled=True),
        lax.all_to_all(value_selection, "seq", split_axis=1, concat_axis=0, tiled=True),
    )
    key_rows, value_rows = (
        lax.all_gather(
            key_portion.reshape(seq_ranks, 1, local_token_count, kv_width), "tp", axis=1, tiled=True
        ),
        lax.all_gather(
            value_part.reshape(seq_ranks, 1, local_token_count, kv_width), "tp", axis=1, tiled=True
        ),
    )
    local_blocks = seq_ranks * per_shard
    query_rows = MASK_BLOCK_SIZE
    row_offset = 0
    block_order = jnp.arange(local_blocks, dtype=jnp.int32)
    block_index = (
        block_order // per_shard * core_count + core_index
    ) * per_shard + block_order % per_shard
    key_blocks_all = key_rows.reshape(total_block_count, MASK_BLOCK_SIZE, kv_rank, HEAD_SIZE)
    value_blocks_all = value_rows.reshape(total_block_count, MASK_BLOCK_SIZE, kv_rank, HEAD_SIZE)
    query_all = query_got.reshape(local_blocks, query_rows, heads_rank, HEAD_SIZE)
    results = []
    for head_slot in range(heads_rank):
        head = rank_index * heads_rank + head_slot
        kv_slot = head // heads_per_group - rank_index * heads_rank // heads_per_group
        key_blocks = lax.dynamic_index_in_dim(key_blocks_all, kv_slot, 2, False)
        value_blocks = lax.dynamic_index_in_dim(value_blocks_all, kv_slot, 2, False)
        results.append(
            head_attend(
                query_all[:, :, head_slot],
                block_index,
                row_offset,
                key_blocks,
                value_blocks,
                lax.dynamic_index_in_dim(vertical_blocks, head, 0, False),
                lax.dynamic_index_in_dim(vertical_count, head, 0, False),
                lax.dynamic_index_in_dim(slash_offsets, head, 0, False),
                lax.dynamic_index_in_dim(slash_count, head, 0, False),
            )
        )
    attended = jnp.stack(results, axis=2).reshape(local_blocks * query_rows, query_width)
    return lax.all_to_all(attended, "seq", split_axis=0, concat_axis=1, tiled=True)


def solution(mesh):
    return jax.shard_map(
        shards,
        mesh=mesh,
        in_specs=(
            P(("groups", "seq", "tp"), None),
            P(("groups", "seq", "tp"), None),
            P(("groups", "seq", "tp"), None),
            P(),
            P(),
            P(),
            P(),
        ),
        out_specs=P(("groups", "seq", "tp"), None),
        check_vma=False,
    )
```

profile of v0, /device:TPU:0, one launch (start us, length us, event | category | flops | bytes accessed | tf_op | source)
XLA Modules:
  0.0 186.8 jit_solution(7677651605231621368)
XLA Ops:
  4.8 7.3 %all-to-all-start = ((bf16[128,8,128]{2,0,1:T(8,128)(2,1)}), bf16[128,8,128]{2,0,1:T(8,128)(2,1)S(1)}, u32[]{:S(2)}, u32[]{:S(2)}) async-start(bf16[128,8,128]{2,0,1:T(8,128)(2,1)} %get-tuple-element.123), calls=%async_computation | async-start | bytes 524288 | tf_op jit(solution)/shard_map/all_to_all | solution.py:107
  19.0 2.1 %all-to-all-done = bf16[128,8,128]{2,0,1:T(8,128)(2,1)S(1)} async-done(((bf16[128,8,128]{2,0,1:T(8,128)(2,1)}), bf16[128,8,128]{2,0,1:T(8,128)(2,1)S(1)}, u32[]{:S(2)}, u32[]{:S(2)}) %all-to-all-start) | async-done | bytes 262176 | tf_op jit(solution)/shard_map/all_to_all | solution.py:107
  21.1 4.0 %all-to-all-start.2 = ((bf16[128,8,128]{2,0,1:T(8,128)(2,1)}), bf16[128,8,128]{2,0,1:T(8,128)(2,1)S(1)}, u32[]{:S(2)}, u32[]{:S(2)}) async-start(bf16[128,8,128]{2,0,1:T(8,128)(2,1)} %get-tuple-element.122), calls=%async_computation.2 | async-start | bytes 524288 | tf_op jit(solution)/shard_map/all_to_all | solution.py:108
  25.0 2.4 %copy.77 = bf16[128,8192]{0,1:T(8,128)(2,1)} copy(bf16[128,8192]{1,0:T(8,128)(2,1)S(1)} %copy-done.7) | data formatting | bytes 4194304 | tf_op args[0]
  27.8 5.7 %all-to-all-done.2 = bf16[128,8,128]{2,0,1:T(8,128)(2,1)S(1)} async-done(((bf16[128,8,128]{2,0,1:T(8,128)(2,1)}), bf16[128,8,128]{2,0,1:T(8,128)(2,1)S(1)}, u32[]{:S(2)}, u32[]{:S(2)}) %all-to-all-start.2) | async-done | bytes 262176 | tf_op jit(solution)/shard_map/all_to_all | solution.py:108
  33.5 4.3 %all-to-all-start.1 = ((bf16[128,8,1024]{0,2,1:T(8,128)(2,1)}), bf16[128,8,1024]{0,2,1:T(8,128)(2,1)}, u32[]{:S(2)}, u32[]{:S(2)}) async-start(bf16[128,8,1024]{0,2,1:T(8,128)(2,1)} %bitcast.7), calls=%async_computation.1 | async-start | bytes 4194304 | tf_op jit(solution)/shard_map/all_to_all | solution.py:106
  51.1 2.2 %all-gather = bf16[8,256,128]{2,1,0:T(8,128)(2,1)S(1)} all-gather(bf16[8,128,128]{2,1,0:T(8,128)(2,1)S(1)} %bitcast.293), channel_id=2, replica_groups=mesh['groups'=2,'seq'=8,'tp'=2] {'tp'}, dimensions={1}, use_global_device_ids=true | all-gather | bytes 786432 | tf_op jit(solution)/shard_map/all_gather | solution.py:111
  53.3 1.8 gather_fusion.2
  55.1 2.2 %all-gather.1 = bf16[8,256,128]{2,1,0:T(8,128)(2,1)S(1)} all-gather(bf16[8,128,128]{2,1,0:T(8,128)(2,1)S(1)} %bitcast.294), channel_id=3, replica_groups=mesh['groups'=2,'seq'=8,'tp'=2] {'tp'}, dimensions={1}, use_global_device_ids=true | all-gather | bytes 786432 | tf_op jit(solution)/shard_map/all_gather | solution.py:114
  58.1 1.8 gather_fusion.6
  60.0 1.9 %gather_fusion.7 = bf16[40,128,128]{2,1,0:T(8,128)(2,1)} fusion(bf16[16,128,128]{2,1,0:T(8,128)(2,1)S(1)} %bitcast.268, s32[1024]{0:T(1024)S(1)} %pad_clamp_fusion.13), kind=kCustom, calls=%fused_computation.13.clone | custom fusion | bytes 2621600 | tf_op jit(solution)/shard_map/jit(_take)/gather | solution.py:58
  61.9 1.9 %gather_fusion.9 = bf16[40,128,128]{2,1,0:T(8,128)(2,1)} fusion(bf16[16,128,128]{2,1,0:T(8,128)(2,1)S(1)} %bitcast.261, s32[1024]{0:T(1024)S(1)} %pad_clamp_fusion.11), kind=kCustom, calls=%fused_computation.14.clone | custom fusion | bytes 2621600 | tf_op jit(solution)/shard_map/jit(_take)/gather | solution.py:57
  63.8 1.9 gather_fusion.10
  65.6 1.9 %gather_fusion.12 = bf16[40,128,128]{2,1,0:T(8,128)(2,1)} fusion(bf16[16,128,128]{2,1,0:T(8,128)(2,1)S(1)} %bitcast.262, s32[1024]{0:T(1024)S(1)} %pad_clamp_fusion.9), kind=kCustom, calls=%fused_computation.16.clone | custom fusion | bytes 2621600 | tf_op jit(solution)/shard_map/jit(_take)/gather | solution.py:57
  67.6 1.9 %gather_fusion.13 = bf16[40,128,128]{2,1,0:T(8,128)(2,1)} fusion(bf16[16,128,128]{2,1,0:T(8,128)(2,1)S(1)} %bitcast.270, s32[1024]{0:T(1024)S(1)} %pad_clamp_fusion.9), kind=kCustom, calls=%fused_computation.17.clone | custom fusion | bytes 2621600 | tf_op jit(solution)/shard_map/jit(_take)/gather | solution.py:58
  69.4 1.9 %gather_fusion.15 = bf16[40,128,128]{2,1,0:T(8,128)(2,1)} fusion(bf16[16,128,128]{2,1,0:T(8,128)(2,1)S(1)} %bitcast.263, s32[1024]{0:T(1024)S(1)} %pad_clamp_fusion.7), kind=kCustom, calls=%fused_computation.18.clone | custom fusion | bytes 2621600 | tf_op jit(solution)/shard_map/jit(_take)/gather | solution.py:57
  71.3 1.9 gather_fusion.16
  73.2 1.9 %gather_fusion.18 = bf16[40,128,128]{2,1,0:T(8,128)(2,1)} fusion(bf16[16,128,128]{2,1,0:T(8,128)(2,1)S(1)} %bitcast.264, s32[1024]{0:T(1024)S(1)} %pad_clamp_fusion.5), kind=kCustom, calls=%fused_computation.20.clone | custom fusion | bytes 2621600 | tf_op jit(solution)/shard_map/jit(_take)/gather | solution.py:57
  75.1 1.9 %gather_fusion.19 = bf16[40,128,128]{2,1,0:T(8,128)(2,1)} fusion(bf16[16,128,128]{2,1,0:T(8,128)(2,1)S(1)} %bitcast.272, s32[1024]{0:T(1024)S(1)} %pad_clamp_fusion.5), kind=kCustom, calls=%fused_computation.21.clone | custom fusion | bytes 2621600 | tf_op jit(solution)/shard_map/jit(_take)/gather | solution.py:58
  78.8 1.9 %gather_fusion.22 = bf16[40,128,128]{2,1,0:T(8,128)(2,1)} fusion(bf16[16,128,128]{2,1,0:T(8,128)(2,1)S(1)} %bitcast.273, s32[1024]{0:T(1024)S(1)} %pad_clamp_fusion.3), kind=kCustom, calls=%fused_computation.23.clone | custom fusion | bytes 2621600 | tf_op jit(solution)/shard_map/jit(_take)/gather | solution.py:58
  82.5 1.9 %gather_fusion.25 = bf16[40,128,128]{2,1,0:T(8,128)(2,1)} fusion(bf16[16,128,128]{2,1,0:T(8,128)(2,1)S(1)} %bitcast.274, s32[1024]{0:T(1024)S(1)} %pad_clamp_fusion.1), kind=kCustom, calls=%fused_computation.25.clone | custom fusion | bytes 2621600 | tf_op jit(solution)/shard_map/jit(_take)/gather | solution.py:58
  95.6 2.0 %fusion.338 = (f32[8,128]{1,0:T(8,128)S(1)}, f32[8,128,5,128]{1,3,2,0:T(8,128)S(1)}) fusion(bf16[8,128,8,128]{1,3,2,0:T(8,128)(2,1)} %bitcast.9, bf16[8,5,128,128]{3,2,1,0:T(8,128)(2,1)} %bitcast.292, pred[8,5]{1,0:T(8,128)(4,1)S(1)} %get-tuple-element.50, pred[128,5,128]{0,2,1:T(8,128)(4,1)S(1)} %broadcast_or_fusion, pred[8,5]{1,0:T(8,128)(4,1)S(1)} %get-tuple-element.75), kind=kOutput, calls=%fused_computation.349 | convolution fusion | flops 171047936 | bytes 4280400 | tf_op jit(solution)/shard_map/nqd,ntkd->nqtk/dot_general | solution.py:60
  129.7 54.2 %all_to_all.61 = bf16[8,128,1024]{1,2,0:T(8,128)(2,1)S(1)} all-to-all(bf16[8,128,1024]{1,2,0:T(8,128)(2,1)S(1)} %bitcast.275), channel_id=1, replica_groups=mesh['groups'=2,'seq'=8,'tp'=2] {'seq'}, dimensions={0} | all-to-all | bytes 4194304 | tf_op jit(solution)/shard_map/all_to_all | solution.py:148
  183.9 2.9 %copy.105 = bf16[128,8192]{1,0:T(8,128)(2,1)} copy(bf16[128,8192]{0,1:T(8,128)(2,1)S(1)} %bitcast.276) | data formatting | bytes 4194304 | tf_op jit(solution)/shard_map/all_to_all | solution.py:148
  (193 shorter events, 72.4 us)
Async XLA Ops:
  2.7 9.5 %copy-start.24 = (s32[64]{0:T(128)S(1)}, s32[64]{0:T(128)}, u32[]{:S(2)}) copy-start(s32[64]{0:T(128)} %param.20) | copy-start | bytes 772
  2.7 9.5 %copy-start.25 = (s32[64]{0:T(128)S(1)}, s32[64]{0:T(128)}, u32[]{:S(2)}) copy-start(s32[64]{0:T(128)} %param.18) | copy-start | bytes 772
  2.7 10.9 %copy-start.22 = (s32[64,2]{0,1:T(2,128)S(1)}, s32[64,2]{0,1:T(2,128)}, u32[]{:S(2)}) copy-start(s32[64,2]{0,1:T(2,128)} %param.17) | copy-start | bytes 1540
  2.7 10.9 %copy-start.23 = (s32[64,2]{0,1:T(2,128)S(1)}, s32[64,2]{0,1:T(2,128)}, u32[]{:S(2)}) copy-start(s32[64,2]{0,1:T(2,128)} %param.19) | copy-start | bytes 1540
  3.9 21.1 %copy-start.7 = (bf16[128,8192]{1,0:T(8,128)(2,1)S(1)}, bf16[128,8192]{1,0:T(8,128)(2,1)}, u32[]{:S(2)}) copy-start(bf16[128,8192]{1,0:T(8,128)(2,1)} %param.14) | copy-start | bytes 6291460
  4.8 16.2 %all-to-all-start = ((bf16[128,8,128]{2,0,1:T(8,128)(2,1)}), bf16[128,8,128]{2,0,1:T(8,128)(2,1)S(1)}, u32[]{:S(2)}, u32[]{:S(2)}) async-start(bf16[128,8,128]{2,0,1:T(8,128)(2,1)} %get-tuple-element.123), calls=%async_computation | async-start | bytes 524288 | tf_op jit(solution)/shard_map/all_to_all | solution.py:107
  21.1 12.5 %all-to-all-start.2 = ((bf16[128,8,128]{2,0,1:T(8,128)(2,1)}), bf16[128,8,128]{2,0,1:T(8,128)(2,1)S(1)}, u32[]{:S(2)}, u32[]{:S(2)}) async-start(bf16[128,8,128]{2,0,1:T(8,128)(2,1)} %get-tuple-element.122), calls=%async_computation.2 | async-start | bytes 524288 | tf_op jit(solution)/shard_map/all_to_all | solution.py:108
  33.5 62.1 %all-to-all-start.1 = ((bf16[128,8,1024]{0,2,1:T(8,128)(2,1)}), bf16[128,8,1024]{0,2,1:T(8,128)(2,1)}, u32[]{:S(2)}, u32[]{:S(2)}) async-start(bf16[128,8,1024]{0,2,1:T(8,128)(2,1)} %bitcast.7), calls=%async_computation.1 | async-start | bytes 4194304 | tf_op jit(solution)/shard_map/all_to_all | solution.py:106
  84.4 1.4 copy-start
  85.9 1.5 copy-start.1
  87.4 1.5 copy-start.2
  88.8 1.5 copy-start.3
  90.3 1.5 copy-start.4
  91.8 1.4 copy-start.5
  93.2 1.4 copy-start.6
  97.7 1.3 copy-start.21
  99.0 1.3 copy-start.20
  101.9 1.3 copy-start.19
  104.9 1.3 copy-start.18
  107.9 1.3 copy-start.17
  110.9 1.3 copy-start.16
  113.9 1.3 copy-start.15
  116.9 1.3 copy-start.13
  119.8 1.3 copy-start.14
  (5 other events, 6.6 us)
where the time goes:
time: 188 us; the launch traced here: 187 us
  local copies, waits for them, and re-layouts  68.2 us (36%)
  blocking collectives  58.6 us (31%)
  matrix products  20.6 us (11%)
  starting transfers between devices  15.6 us (8%)
  other arithmetic  15.4 us (8%)
  waiting for transfers between devices  7.75 us (4%)
    all_to_all x1, blocking collectives, shards(): lax.all_to_all(attended, 'seq', split_axis=0, concat_axis=1, tiled=True)  54.2 us
    gather x16, local copies, waits for them, and re-layouts, head_attend(): tile_values = jnp.take(value_blocks, tile_index, axis=0)  25.1 us
    gather x8, local copies, waits for them, and re-layouts, head_attend(): tile_keys = jnp.take(key_blocks, tile_index, axis=0)  15 us
    unnamed x55, local copies, waits for them, and re-layouts  14.9 us
    dot_general x8, matrix products, head_attend(): jnp.einsum('nqd,ntkd->nqtk', query_blocks, tile_keys, preferred_element_t...  13.6 us
    all_to_all x1, starting transfers between devices, shards(): lax.all_to_all(key_selection, 'seq', split_axis=1, concat_axis=0, tiled=T...  7.31 us
    dot_general x8, matrix products, head_attend(): jnp.einsum('nqtk,ntkd->nqd', rounded, tile_values, preferred_element_type...  6.98 us
    gather x16, local copies, waits for them, and re-layouts, head_attend(): jnp.take(member, safe_targets)  6.08 us
  transfers between devices with their start and end apart: 3, of which 2 were waited for; matrix products, arithmetic and copies ran while one was open for 34% of the time, Pallas kernels for 0%

commit v1 on v0

v1 whole, which is shorter than its diff:
```python
import functools

import jax
import jax.numpy as jnp
from jax import lax
from jax.experimental import pallas as pl
from jax.experimental.pallas import tpu as pltpu
from jax.sharding import PartitionSpec as P

QUERY_HEADS = 64
KEY_VALUE_HEADS = 8
HEAD_SIZE = 128
MASK_BLOCK_SIZE = 128
GROUP = QUERY_HEADS // KEY_VALUE_HEADS
LOG2E = 1.4426950408889634


def attend_kernel(geometry, table, own_queries, sibling_queries, *refs):
    relay, columns, cores, kv_first, vertical_width, slash_width, offsets, pieces = geometry
    piece_refs = refs[: len(pieces)]
    own_out, sibling_out, key_rows, value_rows = refs[len(pieces) :]
    chip_rows = cores * MASK_BLOCK_SIZE
    step = pl.program_id(0)
    vertical_at, vertical_count_at, slash_at, slash_count_at, rank_at, core_at = offsets
    rank = table[rank_at]
    core = table[core_at]
    kv_head = core * (KEY_VALUE_HEADS // cores) + kv_first + step

    @pl.when(step == 0)
    def _():
        value_rows[:, HEAD_SIZE:] = jnp.ones((value_rows.shape[0], HEAD_SIZE), jnp.bfloat16)

    for ref, (chips, slots) in zip(piece_refs, pieces):
        for chip in range(chips):
            rows = pl.ds(slots[chip] * chip_rows, chip_rows)
            key_rows[rows, :] = ref[chip, 0, 0]
            value_rows[rows, :HEAD_SIZE] = ref[chip, 0, 1]

    causal = lax.broadcasted_iota(jnp.int32, (MASK_BLOCK_SIZE, MASK_BLOCK_SIZE), 0) >= lax.broadcasted_iota(
        jnp.int32, (MASK_BLOCK_SIZE, MASK_BLOCK_SIZE), 1
    )
    factor = HEAD_SIZE**-0.5 * LOG2E
    own_slot = 0 if relay else rank

    def row_of(block):
        chip = block // cores
        if relay:
            slot = (rank // columns - chip // columns) * columns + jnp.bitwise_xor(rank % columns, chip % columns)
        else:
            slot = chip
        return (slot * cores + jnp.bitwise_xor(block % cores, core)) * MASK_BLOCK_SIZE

    def unit(queries, block, diagonal_row, head):
        rows = [diagonal_row]
        active = [None]
        verticals = []
        for entry in range(vertical_width):
            vertical = table[vertical_at + head * vertical_width + entry]
            live = entry < table[vertical_count_at + head]
            verticals.append((vertical, live))
            use = live & (vertical < block)
            rows.append(row_of(jnp.where(use, vertical, block)))
            active.append(use)
        for entry in range(slash_width):
            target = block - table[slash_at + head * slash_width + entry]
            use = (entry < table[slash_count_at + head]) & (target >= 0)
            for vertical, live in verticals:
                use = use & jnp.logical_not(live & (vertical == target))
            rows.append(row_of(jnp.where(use, target, block)))
            active.append(use)
        rows = [pl.multiple_of(row, MASK_BLOCK_SIZE) for row in rows]
        keys = jnp.concatenate([key_rows[pl.ds(row, MASK_BLOCK_SIZE), :] for row in rows], axis=0)
        values = jnp.concatenate([value_rows[pl.ds(row, MASK_BLOCK_SIZE), :] for row in rows], axis=0)
        scores = lax.dot_general(queries, keys, (((1,), (1,)), ((), ())), preferred_element_type=jnp.float32)
        tiles = []
        for index, use in enumerate(active):
            tile = scores[:, index * MASK_BLOCK_SIZE : (index + 1) * MASK_BLOCK_SIZE]
            tiles.append(jnp.where(causal if use is None else use, tile, -jnp.inf))
        peak = functools.reduce(jnp.maximum, tiles)
        peak = jnp.max(peak, axis=1, keepdims=True)
        weights = [jnp.exp2((tile - peak) * factor).astype(jnp.bfloat16) for tile in tiles]
        sums = jnp.dot(jnp.concatenate(weights, axis=1), values, preferred_element_type=jnp.float32)
        return (sums[:, :HEAD_SIZE] / sums[:, HEAD_SIZE:]).astype(jnp.bfloat16)

    def head_pair(slot, carry):
        head = kv_head * GROUP + slot
        lanes = pl.ds(pl.multiple_of(slot * HEAD_SIZE, HEAD_SIZE), HEAD_SIZE)
        base = own_slot * chip_rows
        own_out[:, lanes] = unit(own_queries[:, lanes], rank * cores + core, base, head)
        sibling_out[:, lanes] = unit(
            sibling_queries[:, lanes], rank * cores + (cores - 1 - core), base + MASK_BLOCK_SIZE, head
        )
        return carry

    lax.fori_loop(0, GROUP, head_pair, 0, unroll=2)


def attend(table, geometry, queries, sibling_queries, pieces, kv_heads):
    _, _, cores, kv_first, _, _, offsets, layout = geometry
    tokens = queries.shape[0]
    width = GROUP * HEAD_SIZE
    core_at = offsets[-1]
    half = KEY_VALUE_HEADS // cores
    chip_rows = cores * MASK_BLOCK_SIZE
    rows = sum(chips for chips, _ in layout) * chip_rows

    def piece_spec(piece):
        return pl.BlockSpec((piece.shape[0], 1, 2, chip_rows, HEAD_SIZE), lambda g, t: (0, g, 0, 0, 0))

    return pl.pallas_call(
        functools.partial(attend_kernel, geometry),
        grid_spec=pltpu.PrefetchScalarGridSpec(
            num_scalar_prefetch=1,
            grid=(kv_heads,),
            in_specs=[
                pl.BlockSpec((tokens, width), lambda g, t: (0, t[core_at] * half + kv_first + g)),
                pl.BlockSpec((tokens, width), lambda g, t: (0, kv_first + g)),
            ]
            + [piece_spec(piece) for piece in pieces],
            out_specs=[
                pl.BlockSpec((tokens, width), lambda g, t: (0, g)),
                pl.BlockSpec((tokens, width), lambda g, t: (0, g)),
            ],
            scratch_shapes=[
                pltpu.VMEM((rows, HEAD_SIZE), jnp.bfloat16),
                pltpu.VMEM((rows, 2 * HEAD_SIZE), jnp.bfloat16),
            ],
        ),
        out_shape=[jax.ShapeDtypeStruct((tokens, kv_heads * width), jnp.bfloat16)] * 2,
        name="attend",
    )(table, queries, sibling_queries, *pieces)


def shards(queries, keys, values, vertical_blocks, vertical_count, slash_offsets, slash_count):
    tokens = queries.shape[0]
    ranks = lax.axis_size("seq")
    cores = lax.axis_size("tp")
    assert tokens == MASK_BLOCK_SIZE and cores == 2
    rank = lax.axis_index("seq")
    core = lax.axis_index("tp")
    columns = 2
    relay = ranks == 8
    lines = ranks // columns
    half = KEY_VALUE_HEADS // cores
    swap = [(0, 1), (1, 0)]

    parts = [vertical_blocks, vertical_count, slash_offsets, slash_count, rank, core]
    sizes = [part.size for part in parts]
    offsets = tuple(sum(sizes[:n]) for n in range(len(sizes)))
    table = jnp.concatenate([part.astype(jnp.int32).reshape(-1) for part in parts])
    common = (vertical_blocks.shape[1], slash_offsets.shape[1], offsets)

    def by_head(array):
        return array.reshape(tokens, cores, half, HEAD_SIZE).transpose(1, 2, 0, 3)

    stacked = jnp.stack([by_head(keys), by_head(values)], axis=2)
    own = lax.dynamic_index_in_dim(stacked, core, 0, False)
    other = lax.dynamic_index_in_dim(stacked, cores - 1 - core, 0, False)
    other = lax.ppermute(other, "tp", swap)
    local = jnp.concatenate([own, other], axis=2)[None]
    query_width = QUERY_HEADS // cores * HEAD_SIZE
    sibling_queries = lax.ppermute(
        lax.dynamic_slice_in_dim(queries, (cores - 1 - core) * query_width, query_width, 1), "tp", swap
    )

    if not relay:
        gathered = lax.all_gather(local[0], "seq", axis=0)
        geometry = (False, columns, cores, 0) + common + (((ranks, tuple(range(ranks))),),)
        own_out, sibling_out = attend(table, geometry, queries, sibling_queries, [gathered], half)
        sibling_out = lax.ppermute(sibling_out, "tp", swap)
    else:
        first = half - 1

        def along(array, step):
            pairs = [
                (line * columns + column, (line + 1) * columns + column)
                for line in range(step - 1, lines - 1)
                for column in range(columns)
            ]
            return lax.ppermute(array, "seq", pairs)

        def across(array, step):
            pairs = [
                (line * columns + column, line * columns + 1 - column)
                for line in range(step, lines)
                for column in range(columns)
            ]
            return lax.ppermute(array, "seq", pairs)

        a = [local[:, :first]]
        b_own = local[:, first:]
        b = [jnp.concatenate([b_own, across(b_own, 0)], axis=0)]
        for step in range(1, lines):
            a.append(along(a[-1], step))
        across_a = [across(a[step], step) for step in range(lines)]
        for step in range(1, lines):
            b.append(along(b[-1], step))
        layout_a = tuple((1, (step * columns,)) for step in range(lines)) + tuple(
            (1, (step * columns + 1,)) for step in range(lines)
        )
        layout_b = tuple((columns, (step * columns, step * columns + 1)) for step in range(lines))
        own_a, sibling_a = attend(
            table, (True, columns, cores, 0) + common + (layout_a,), queries, sibling_queries, a + across_a, first
        )
        sibling_a = lax.ppermute(sibling_a, "tp", swap)
        own_b, sibling_b = attend(
            table, (True, columns, cores, first) + common + (layout_b,), queries, sibling_queries, b, half - first
        )
        sibling_b = lax.ppermute(sibling_b, "tp", swap)
        own_out = jnp.concatenate([own_a, own_b], axis=1)
        sibling_out = jnp.concatenate([sibling_a, sibling_b], axis=1)
    low = jnp.where(core == 0, own_out, sibling_out)
    high = jnp.where(core == 0, sibling_out, own_out)
    return jnp.concatenate([low, high], axis=1)


def solution(mesh):
    return jax.shard_map(
        shards,
        mesh=mesh,
        in_specs=(
            P(("groups", "seq", "tp"), None),
            P(("groups", "seq", "tp"), None),
            P(("groups", "seq", "tp"), None),
            P(),
            P(),
            P(),
            P(),
        ),
        out_specs=P(("groups", "seq", "tp"), None),
        check_vma=False,
    )
```

time: 188 us -> 101 us (0.54)
  the two profiles are of different devices: /device:TPU:0 before, /device:TPU:31 now
where the time goes in v1:
time: 101 us
  waiting for transfers between devices  48.5 us (48%)
  starting transfers between devices  22.7 us (22%)
  Pallas kernels  21.4 us (21%)
  local copies, waits for them, and re-layouts  6.42 us (6%)
  other arithmetic  1.74 us (2%)
    ppermute x6, waiting for transfers between devices, along(): return lax.ppermute(array, 'seq', pairs)  30.1 us
    pallas_call x2, Pallas kernels, attend(): pl.pallas_call(functools.partial(attend_kernel, geometry), grid_spec=pltp...  21.4 us
    ppermute x5, waiting for transfers between devices, across(): return lax.ppermute(array, 'seq', pairs)  17 us
    ppermute x5, starting transfers between devices, across(): return lax.ppermute(array, 'seq', pairs)  7.94 us
    ppermute x6, starting transfers between devices, along(): return lax.ppermute(array, 'seq', pairs)  7.71 us
    ppermute x1, starting transfers between devices, shards(): sibling_a = lax.ppermute(sibling_a, 'tp', swap)  4.15 us
    reshape x2, local copies, waits for them, and re-layouts, by_head(): return array.reshape(tokens, cores, half, HEAD_SIZE).transpose(1, 2, 0, 3)  2.23 us
  transfers between devices with their start and end apart: 15, of which 9 were waited for; matrix products, arithmetic and copies ran while one was open for 3% of the time, Pallas kernels for 21%

profile of v1, /device:TPU:31, one launch (start us, length us, event | category | flops | bytes accessed | tf_op | source)
XLA Modules:
  0.0 101.0 jit_solution(486211995628364810)
XLA Ops:
  0.0 1.1 %reshape.23 = bf16[128,2,4,128]{3,2,1,0:T(4,128)(2,1)S(1)} reshape(bf16[128,1024]{1,0:T(8,128)(2,1)} %param.9) | data formatting | bytes 524288 | tf_op jit(solution)/shard_map/reshape | solution.py:154
  1.1 1.1 %reshape.22 = bf16[128,2,4,128]{3,2,1,0:T(4,128)(2,1)S(1)} reshape(bf16[128,1024]{1,0:T(8,128)(2,1)} %param.8) | data formatting | bytes 524288 | tf_op jit(solution)/shard_map/reshape | solution.py:154
  3.2 1.2 %collective-permute-done.1 = bf16[4,2,128,128]{3,2,1,0:T(8,128)(2,1)S(1)} collective-permute-done((bf16[4,2,128,128]{3,2,1,0:T(8,128)(2,1)S(1)}, bf16[4,2,128,128]{3,2,1,0:T(8,128)(2,1)S(1)}, u32[]{:S(2)}, u32[]{:S(2)}) %collective-permute-start.1) | collective-permute-done | bytes 262176 | tf_op jit(solution)/shard_map/ppermute | solution.py:159
  4.5 1.3 %collective-permute-start.2 = (bf16[1,3,2,256,128]{4,3,2,1,0:T(8,128)(2,1)S(1)}, bf16[1,3,2,256,128]{4,3,2,1,0:T(8,128)(2,1)S(1)}, u32[]{:S(2)}, u32[]{:S(2)}) collective-permute-start(bf16[1,3,2,256,128]{4,3,2,1,0:T(8,128)(2,1)S(1)} %slice.8.refs_0_), channel_id=1, source_target_pairs={{0,4},{2,6},{4,8},{6,10},{8,12},{10,14},{1,5},{3,7},{5,9},{7,11},{... | collective-permute-start | bytes 1179656 | tf_op jit(solution)/shard_map/ppermute | solution.py:180
  5.8 10.9 %collective-permute-done.2.refs_1_ = bf16[1,3,2,256,128]{4,3,2,1,0:T(8,128)(2,1)S(1)} collective-permute-done((bf16[1,3,2,256,128]{4,3,2,1,0:T(8,128)(2,1)S(1)}, bf16[1,3,2,256,128]{4,3,2,1,0:T(8,128)(2,1)S(1)}, u32[]{:S(2)}, u32[]{:S(2)}) %collective-permute-start.2) | collective-permute-done | bytes 393248 | tf_op jit(solution)/shard_map/ppermute | solution.py:180
  16.6 1.3 %collective-permute-start.3 = (bf16[1,3,2,256,128]{4,3,2,1,0:T(8,128)(2,1)S(1)}, bf16[1,3,2,256,128]{4,3,2,1,0:T(8,128)(2,1)}, u32[]{:S(2)}, u32[]{:S(2)}) collective-permute-start(bf16[1,3,2,256,128]{4,3,2,1,0:T(8,128)(2,1)S(1)} %collective-permute-done.2.refs_1_), channel_id=1, source_target_pairs={{4,8},{6,10},{8,12},{10,14},{5,9},{7,11},{9,13},{11,15},{20,24},{2... | collective-permute-start | bytes 1179656 | tf_op jit(solution)/shard_map/ppermute | solution.py:180
  19.0 1.2 %collective-permute-start = (bf16[128,4096]{1,0:T(8,128)(2,1)}, bf16[128,4096]{1,0:T(8,128)(2,1)S(1)}, u32[]{:S(2)}, u32[]{:S(2)}) collective-permute-start(bf16[128,4096]{1,0:T(8,128)(2,1)} %constant_dynamic-slice_fusion), channel_id=1, source_target_pairs={{0,1},{1,0},{2,3},{3,2},{4,5},{5,4},{6,7},{7,6},{8,9},{9,8},{10,11... | collective-permute-start | bytes 3145736 | tf_op jit(solution)/shard_map/ppermute | solution.py:162
  20.5 7.6 %collective-permute-done.3.refs_2_ = bf16[1,3,2,256,128]{4,3,2,1,0:T(8,128)(2,1)} collective-permute-done((bf16[1,3,2,256,128]{4,3,2,1,0:T(8,128)(2,1)S(1)}, bf16[1,3,2,256,128]{4,3,2,1,0:T(8,128)(2,1)}, u32[]{:S(2)}, u32[]{:S(2)}) %collective-permute-start.3) | collective-permute-done | bytes 393248 | tf_op jit(solution)/shard_map/ppermute | solution.py:180
  28.1 1.3 %collective-permute-start.4 = (bf16[1,3,2,256,128]{4,3,2,1,0:T(8,128)(2,1)}, bf16[1,3,2,256,128]{4,3,2,1,0:T(8,128)(2,1)}, u32[]{:S(2)}, u32[]{:S(2)}) collective-permute-start(bf16[1,3,2,256,128]{4,3,2,1,0:T(8,128)(2,1)} %collective-permute-done.3.refs_2_), channel_id=1, source_target_pairs={{8,12},{10,14},{9,13},{11,15},{24,28},{26,30},{25,29},{27,31}} | collective-permute-start | bytes 1179656 | tf_op jit(solution)/shard_map/ppermute | solution.py:180
  29.7 3.6 %collective-permute-done.9 = bf16[1,1,2,256,128]{4,3,2,1,0:T(8,128)(2,1)S(1)} collective-permute-done((bf16[1,1,2,256,128]{4,3,2,1,0:T(8,128)(2,1)S(1)}, bf16[1,1,2,256,128]{4,3,2,1,0:T(8,128)(2,1)S(1)}, u32[]{:S(2)}, u32[]{:S(2)}) %collective-permute-start.9) | collective-permute-done | bytes 131104 | tf_op jit(solution)/shard_map/ppermute | solution.py:188
  33.3 1.3 %collective-permute-start.10 = (bf16[2,1,2,256,128]{4,3,2,1,0:T(8,128)(2,1)S(1)}, bf16[2,1,2,256,128]{4,3,2,1,0:T(8,128)(2,1)}, u32[]{:S(2)}, u32[]{:S(2)}) collective-permute-start(bf16[2,1,2,256,128]{4,3,2,1,0:T(8,128)(2,1)S(1)} %pad_maximum_fusion.1.refs_0_), channel_id=1, source_target_pairs={{0,4},{2,6},{4,8},{6,10},{8,12},{10,14},{1,5},{3,7},{5,9},{7,11},{... | collective-permute-start | bytes 786440 | tf_op jit(solution)/shard_map/ppermute | solution.py:180
  34.6 2.1 %collective-permute-start.6 = (bf16[1,3,2,256,128]{4,3,2,1,0:T(8,128)(2,1)S(1)}, bf16[1,3,2,256,128]{4,3,2,1,0:T(8,128)(2,1)S(1)}, u32[]{:S(2)}, u32[]{:S(2)}) collective-permute-start(bf16[1,3,2,256,128]{4,3,2,1,0:T(8,128)(2,1)S(1)} %collective-permute-done.2.refs_1_), channel_id=1, source_target_pairs={{4,6},{6,4},{8,10},{10,8},{12,14},{14,12},{5,7},{7,5},{9,11},{11,9... | collective-permute-start | bytes 1179656 | tf_op jit(solution)/shard_map/ppermute | solution.py:188
  36.8 3.1 %collective-permute-start.7 = (bf16[1,3,2,256,128]{4,3,2,1,0:T(8,128)(2,1)}, bf16[1,3,2,256,128]{4,3,2,1,0:T(8,128)(2,1)S(1)}, u32[]{:S(2)}, u32[]{:S(2)}) collective-permute-start(bf16[1,3,2,256,128]{4,3,2,1,0:T(8,128)(2,1)} %collective-permute-done.3.refs_2_), channel_id=1, source_target_pairs={{8,10},{10,8},{12,14},{14,12},{9,11},{11,9},{13,15},{15,13},{24,26... | collective-permute-start | bytes 1179656 | tf_op jit(solution)/shard_map/ppermute | solution.py:188
  39.9 2.1 %collective-permute-start.8 = (bf16[1,3,2,256,128]{4,3,2,1,0:T(8,128)(2,1)}, bf16[1,3,2,256,128]{4,3,2,1,0:T(8,128)(2,1)}, u32[]{:S(2)}, u32[]{:S(2)}) collective-permute-start(bf16[1,3,2,256,128]{4,3,2,1,0:T(8,128)(2,1)} %collective-permute-done.4.refs_3_), channel_id=1, source_target_pairs={{12,14},{14,12},{13,15},{15,13},{28,30},{30,28},{29,31},{31,29}} | collective-permute-start | bytes 1179656 | tf_op jit(solution)/shard_map/ppermute | solution.py:188
  42.1 2.9 %collective-permute-done.10.refs_1_ = bf16[2,1,2,256,128]{4,3,2,1,0:T(8,128)(2,1)} collective-permute-done((bf16[2,1,2,256,128]{4,3,2,1,0:T(8,128)(2,1)S(1)}, bf16[2,1,2,256,128]{4,3,2,1,0:T(8,128)(2,1)}, u32[]{:S(2)}, u32[]{:S(2)}) %collective-permute-start.10) | collective-permute-done | bytes 262176 | tf_op jit(solution)/shard_map/ppermute | solution.py:180
  45.0 1.3 %collective-permute-start.11 = (bf16[2,1,2,256,128]{4,3,2,1,0:T(8,128)(2,1)}, bf16[2,1,2,256,128]{4,3,2,1,0:T(8,128)(2,1)}, u32[]{:S(2)}, u32[]{:S(2)}) collective-permute-start(bf16[2,1,2,256,128]{4,3,2,1,0:T(8,128)(2,1)} %collective-permute-done.10.refs_1_), channel_id=1, source_target_pairs={{4,8},{6,10},{8,12},{10,14},{5,9},{7,11},{9,13},{11,15},{20,24},{2... | collective-permute-start | bytes 786440 | tf_op jit(solution)/shard_map/ppermute | solution.py:180
  47.5 4.9 %collective-permute-done.7.refs_6_ = bf16[1,3,2,256,128]{4,3,2,1,0:T(8,128)(2,1)S(1)} collective-permute-done((bf16[1,3,2,256,128]{4,3,2,1,0:T(8,128)(2,1)}, bf16[1,3,2,256,128]{4,3,2,1,0:T(8,128)(2,1)S(1)}, u32[]{:S(2)}, u32[]{:S(2)}) %collective-permute-start.7) | collective-permute-done | bytes 393248 | tf_op jit(solution)/shard_map/ppermute | solution.py:188
  52.4 8.5 %collective-permute-done.8.refs_7_ = bf16[1,3,2,256,128]{4,3,2,1,0:T(8,128)(2,1)} collective-permute-done((bf16[1,3,2,256,128]{4,3,2,1,0:T(8,128)(2,1)}, bf16[1,3,2,256,128]{4,3,2,1,0:T(8,128)(2,1)}, u32[]{:S(2)}, u32[]{:S(2)}) %collective-permute-start.8) | collective-permute-done | bytes 393248 | tf_op jit(solution)/shard_map/ppermute | solution.py:188
  60.9 14.7 %attend.2 = (bf16[128,3072]{1,0:T(8,128)(2,1)}, bf16[128,3072]{1,0:T(8,128)(2,1)}) custom-call(s32[386]{0:T(512)} %concatenate.18.table, bf16[128,8192]{1,0:T(8,128)(2,1)} %own_queries.3, bf16[128,4096]{1,0:T(8,128)(2,1)} %copy-done.1, bf16[1,3,2,256,128]{4,3,2,1,0:T(8,128)(2,1)} %copy-done.2, bf16[1,3,2,256,128]{4,3,2,1,0:T(8,128)(2,1)} %copy-done.5, ...), custom_call_target="tpu_custom_call" | custom-call | tf_op jit(solution)/shard_map/attend/pallas_call | solution.py:110
  75.7 4.2 %collective-permute-start.13 = (bf16[128,3072]{1,0:T(8,128)(2,1)}, bf16[128,3072]{1,0:T(8,128)(2,1)S(1)}, u32[]{:S(2)}, u32[]{:S(2)}) collective-permute-start(bf16[128,3072]{1,0:T(8,128)(2,1)} %get-tuple-element.11), channel_id=1, source_target_pairs={{0,1},{1,0},{2,3},{3,2},{4,5},{5,4},{6,7},{7,6},{8,9},{9,8},{10,11... | collective-permute-start | bytes 2359304 | tf_op jit(solution)/shard_map/ppermute | solution.py:205
  79.8 1.3 %collective-permute-start.12 = (bf16[2,1,2,256,128]{4,3,2,1,0:T(8,128)(2,1)}, bf16[2,1,2,256,128]{4,3,2,1,0:T(8,128)(2,1)S(1)}, u32[]{:S(2)}, u32[]{:S(2)}) collective-permute-start(bf16[2,1,2,256,128]{4,3,2,1,0:T(8,128)(2,1)} %collective-permute-done.11.refs_2_), channel_id=1, source_target_pairs={{8,12},{10,14},{9,13},{11,15},{24,28},{26,30},{25,29},{27,31}} | collective-permute-start | bytes 786440 | tf_op jit(solution)/shard_map/ppermute | solution.py:180
  81.1 8.6 %collective-permute-done.12.refs_3_ = bf16[2,1,2,256,128]{4,3,2,1,0:T(8,128)(2,1)S(1)} collective-permute-done((bf16[2,1,2,256,128]{4,3,2,1,0:T(8,128)(2,1)}, bf16[2,1,2,256,128]{4,3,2,1,0:T(8,128)(2,1)S(1)}, u32[]{:S(2)}, u32[]{:S(2)}) %collective-permute-start.12) | collective-permute-done | bytes 262176 | tf_op jit(solution)/shard_map/ppermute | solution.py:180
  90.4 6.7 %attend.3 = (bf16[128,1024]{1,0:T(8,128)(2,1)}, bf16[128,1024]{1,0:T(8,128)(2,1)}) custom-call(s32[386]{0:T(512)} %concatenate.18.table, bf16[128,8192]{1,0:T(8,128)(2,1)} %own_queries.3, bf16[128,4096]{1,0:T(8,128)(2,1)} %copy-done.1, bf16[2,1,2,256,128]{4,3,2,1,0:T(8,128)(2,1)} %copy-done.3, bf16[2,1,2,256,128]{4,3,2,1,0:T(8,128)(2,1)} %collective-permute-done.10.refs_1_, ...), custom_call_target="tpu_custom_call" | custom-call | tf_op jit(solution)/shard_map/attend/pallas_call | solution.py:110
  99.5 1.5 %pad_maximum_fusion = bf16[128,8192]{1,0:T(8,128)(2,1)} fusion(bf16[128,4096]{1,0:T(8,128)(2,1)S(1)} %get-tuple-element.14, bf16[128,4096]{1,0:T(8,128)(2,1)S(1)} %get-tuple-element.13), kind=kLoop, calls=%fused_computation | loop fusion | flops 4194304 | bytes 4194304 | tf_op jit(solution)/shard_map/concatenate | solution.py:214
  (56 shorter events, 6.9 us)
Async XLA Ops:
  2.4 1.9 %collective-permute-start.1 = (bf16[4,2,128,128]{3,2,1,0:T(8,128)(2,1)S(1)}, bf16[4,2,128,128]{3,2,1,0:T(8,128)(2,1)S(1)}, u32[]{:S(2)}, u32[]{:S(2)}) collective-permute-start(bf16[4,2,128,128]{3,2,1,0:T(8,128)(2,1)S(1)} %get-tuple-element.16), channel_id=1, source_target_pairs={{0,1},{1,0},{2,3},{3,2},{4,5},{5,4},{6,7},{7,6},{8,9},{9,8},{10,11... | collective-permute-start | bytes 786440 | tf_op jit(solution)/shard_map/ppermute | solution.py:159
  4.4 41.9 %copy-start.10 = (s32[64,2]{0,1:T(2,128)S(1)}, s32[64,2]{0,1:T(2,128)}, u32[]{:S(2)}) copy-start(s32[64,2]{0,1:T(2,128)} %param.10) | copy-start | bytes 1540
  4.4 42.2 %copy-start.11 = (s32[64,2]{0,1:T(2,128)S(1)}, s32[64,2]{0,1:T(2,128)}, u32[]{:S(2)}) copy-start(s32[64,2]{0,1:T(2,128)} %param.12) | copy-start | bytes 1540
  4.4 42.4 %copy-start.12 = (s32[64]{0:T(128)S(1)}, s32[64]{0:T(128)}, u32[]{:S(2)}) copy-start(s32[64]{0:T(128)} %param.11) | copy-start | bytes 772
  4.4 42.4 %copy-start.13 = (s32[64]{0:T(128)S(1)}, s32[64]{0:T(128)}, u32[]{:S(2)}) copy-start(s32[64]{0:T(128)} %param.13) | copy-start | bytes 772
  4.4 56.5 %copy-start.2 = (bf16[1,3,2,256,128]{4,3,2,1,0:T(8,128)(2,1)}, bf16[1,3,2,256,128]{4,3,2,1,0:T(8,128)(2,1)S(1)}, u32[]{:S(2)}) copy-start(bf16[1,3,2,256,128]{4,3,2,1,0:T(8,128)(2,1)S(1)} %slice.8.refs_0_) | copy-start | bytes 1179652
  4.5 12.2 %collective-permute-start.2 = (bf16[1,3,2,256,128]{4,3,2,1,0:T(8,128)(2,1)S(1)}, bf16[1,3,2,256,128]{4,3,2,1,0:T(8,128)(2,1)S(1)}, u32[]{:S(2)}, u32[]{:S(2)}) collective-permute-start(bf16[1,3,2,256,128]{4,3,2,1,0:T(8,128)(2,1)S(1)} %slice.8.refs_0_), channel_id=1, source_target_pairs={{0,4},{2,6},{4,8},{6,10},{8,12},{10,14},{1,5},{3,7},{5,9},{7,11},{... | collective-permute-start | bytes 1179656 | tf_op jit(solution)/shard_map/ppermute | solution.py:180
  16.6 44.3 %copy-start.5 = (bf16[1,3,2,256,128]{4,3,2,1,0:T(8,128)(2,1)}, bf16[1,3,2,256,128]{4,3,2,1,0:T(8,128)(2,1)S(1)}, u32[]{:S(2)}) copy-start(bf16[1,3,2,256,128]{4,3,2,1,0:T(8,128)(2,1)S(1)} %collective-permute-done.2.refs_1_) | copy-start | bytes 1179652
  16.6 11.4 %collective-permute-start.3 = (bf16[1,3,2,256,128]{4,3,2,1,0:T(8,128)(2,1)S(1)}, bf16[1,3,2,256,128]{4,3,2,1,0:T(8,128)(2,1)}, u32[]{:S(2)}, u32[]{:S(2)}) collective-permute-start(bf16[1,3,2,256,128]{4,3,2,1,0:T(8,128)(2,1)S(1)} %collective-permute-done.2.refs_1_), channel_id=1, source_target_pairs={{4,8},{6,10},{8,12},{10,14},{5,9},{7,11},{9,13},{11,15},{20,24},{2... | collective-permute-start | bytes 1179656 | tf_op jit(solution)/shard_map/ppermute | solution.py:180
  19.0 28.5 %collective-permute-start = (bf16[128,4096]{1,0:T(8,128)(2,1)}, bf16[128,4096]{1,0:T(8,128)(2,1)S(1)}, u32[]{:S(2)}, u32[]{:S(2)}) collective-permute-start(bf16[128,4096]{1,0:T(8,128)(2,1)} %constant_dynamic-slice_fusion), channel_id=1, source_target_pairs={{0,1},{1,0},{2,3},{3,2},{4,5},{5,4},{6,7},{7,6},{8,9},{9,8},{10,11... | collective-permute-start | bytes 3145736 | tf_op jit(solution)/shard_map/ppermute | solution.py:162
  20.2 16.5 %collective-permute-start.5 = (bf16[1,3,2,256,128]{4,3,2,1,0:T(8,128)(2,1)S(1)}, bf16[1,3,2,256,128]{4,3,2,1,0:T(8,128)(2,1)S(1)}, u32[]{:S(2)}, u32[]{:S(2)}) collective-permute-start(bf16[1,3,2,256,128]{4,3,2,1,0:T(8,128)(2,1)S(1)} %slice.8.refs_0_), channel_id=1, source_target_pairs={{0,2},{2,0},{4,6},{6,4},{8,10},{10,8},{12,14},{14,12},{1,3},{3,1},... | collective-permute-start | bytes 1179656 | tf_op jit(solution)/shard_map/ppermute | solution.py:188
  28.1 11.9 %collective-permute-start.4 = (bf16[1,3,2,256,128]{4,3,2,1,0:T(8,128)(2,1)}, bf16[1,3,2,256,128]{4,3,2,1,0:T(8,128)(2,1)}, u32[]{:S(2)}, u32[]{:S(2)}) collective-permute-start(bf16[1,3,2,256,128]{4,3,2,1,0:T(8,128)(2,1)} %collective-permute-done.3.refs_2_), channel_id=1, source_target_pairs={{8,12},{10,14},{9,13},{11,15},{24,28},{26,30},{25,29},{27,31}} | collective-permute-start | bytes 1179656 | tf_op jit(solution)/shard_map/ppermute | solution.py:180
  29.4 3.9 %collective-permute-start.9 = (bf16[1,1,2,256,128]{4,3,2,1,0:T(8,128)(2,1)S(1)}, bf16[1,1,2,256,128]{4,3,2,1,0:T(8,128)(2,1)S(1)}, u32[]{:S(2)}, u32[]{:S(2)}) collective-permute-start(bf16[1,1,2,256,128]{4,3,2,1,0:T(8,128)(2,1)S(1)} %slice.9), channel_id=1, source_target_pairs={{0,2},{2,0},{4,6},{6,4},{8,10},{10,8},{12,14},{14,12},{1,3},{3,1},... | collective-permute-start | bytes 393224 | tf_op jit(solution)/shard_map/ppermute | solution.py:188
  33.3 56.4 %copy-start.3 = (bf16[2,1,2,256,128]{4,3,2,1,0:T(8,128)(2,1)}, bf16[2,1,2,256,128]{4,3,2,1,0:T(8,128)(2,1)S(1)}, u32[]{:S(2)}) copy-start(bf16[2,1,2,256,128]{4,3,2,1,0:T(8,128)(2,1)S(1)} %pad_maximum_fusion.1.refs_0_) | copy-start | bytes 786436
  33.3 11.7 %collective-permute-start.10 = (bf16[2,1,2,256,128]{4,3,2,1,0:T(8,128)(2,1)S(1)}, bf16[2,1,2,256,128]{4,3,2,1,0:T(8,128)(2,1)}, u32[]{:S(2)}, u32[]{:S(2)}) collective-permute-start(bf16[2,1,2,256,128]{4,3,2,1,0:T(8,128)(2,1)S(1)} %pad_maximum_fusion.1.refs_0_), channel_id=1, source_target_pairs={{0,4},{2,6},{4,8},{6,10},{8,12},{10,14},{1,5},{3,7},{5,9},{7,11},{... | collective-permute-start | bytes 786440 | tf_op jit(solution)/shard_map/ppermute | solution.py:180
  34.6 12.9 %collective-permute-start.6 = (bf16[1,3,2,256,128]{4,3,2,1,0:T(8,128)(2,1)S(1)}, bf16[1,3,2,256,128]{4,3,2,1,0:T(8,128)(2,1)S(1)}, u32[]{:S(2)}, u32[]{:S(2)}) collective-permute-start(bf16[1,3,2,256,128]{4,3,2,1,0:T(8,128)(2,1)S(1)} %collective-permute-done.2.refs_1_), channel_id=1, source_target_pairs={{4,6},{6,4},{8,10},{10,8},{12,14},{14,12},{5,7},{7,5},{9,11},{11,9... | collective-permute-start | bytes 1179656 | tf_op jit(solution)/shard_map/ppermute | solution.py:188
  36.8 24.1 %copy-start.6 = (bf16[1,3,2,256,128]{4,3,2,1,0:T(8,128)(2,1)}, bf16[1,3,2,256,128]{4,3,2,1,0:T(8,128)(2,1)S(1)}, u32[]{:S(2)}) copy-start(bf16[1,3,2,256,128]{4,3,2,1,0:T(8,128)(2,1)S(1)} %collective-permute-done.5.refs_4_) | copy-start | bytes 1179652
  36.8 15.6 %collective-permute-start.7 = (bf16[1,3,2,256,128]{4,3,2,1,0:T(8,128)(2,1)}, bf16[1,3,2,256,128]{4,3,2,1,0:T(8,128)(2,1)S(1)}, u32[]{:S(2)}, u32[]{:S(2)}) collective-permute-start(bf16[1,3,2,256,128]{4,3,2,1,0:T(8,128)(2,1)} %collective-permute-done.3.refs_2_), channel_id=1, source_target_pairs={{8,10},{10,8},{12,14},{14,12},{9,11},{11,9},{13,15},{15,13},{24,26... | collective-permute-start | bytes 1179656 | tf_op jit(solution)/shard_map/ppermute | solution.py:188
  39.9 21.0 %collective-permute-start.8 = (bf16[1,3,2,256,128]{4,3,2,1,0:T(8,128)(2,1)}, bf16[1,3,2,256,128]{4,3,2,1,0:T(8,128)(2,1)}, u32[]{:S(2)}, u32[]{:S(2)}) collective-permute-start(bf16[1,3,2,256,128]{4,3,2,1,0:T(8,128)(2,1)} %collective-permute-done.4.refs_3_), channel_id=1, source_target_pairs={{12,14},{14,12},{13,15},{15,13},{28,30},{30,28},{29,31},{31,29}} | collective-permute-start | bytes 1179656 | tf_op jit(solution)/shard_map/ppermute | solution.py:188
  45.0 34.8 %collective-permute-start.11 = (bf16[2,1,2,256,128]{4,3,2,1,0:T(8,128)(2,1)}, bf16[2,1,2,256,128]{4,3,2,1,0:T(8,128)(2,1)}, u32[]{:S(2)}, u32[]{:S(2)}) collective-permute-start(bf16[2,1,2,256,128]{4,3,2,1,0:T(8,128)(2,1)} %collective-permute-done.10.refs_1_), channel_id=1, source_target_pairs={{4,8},{6,10},{8,12},{10,14},{5,9},{7,11},{9,13},{11,15},{20,24},{2... | collective-permute-start | bytes 786440 | tf_op jit(solution)/shard_map/ppermute | solution.py:180
  75.7 23.4 %collective-permute-start.13 = (bf16[128,3072]{1,0:T(8,128)(2,1)}, bf16[128,3072]{1,0:T(8,128)(2,1)S(1)}, u32[]{:S(2)}, u32[]{:S(2)}) collective-permute-start(bf16[128,3072]{1,0:T(8,128)(2,1)} %get-tuple-element.11), channel_id=1, source_target_pairs={{0,1},{1,0},{2,3},{3,2},{4,5},{5,4},{6,7},{7,6},{8,9},{9,8},{10,11... | collective-permute-start | bytes 2359304 | tf_op jit(solution)/shard_map/ppermute | solution.py:205
  79.8 9.9 %collective-permute-start.12 = (bf16[2,1,2,256,128]{4,3,2,1,0:T(8,128)(2,1)}, bf16[2,1,2,256,128]{4,3,2,1,0:T(8,128)(2,1)S(1)}, u32[]{:S(2)}, u32[]{:S(2)}) collective-permute-start(bf16[2,1,2,256,128]{4,3,2,1,0:T(8,128)(2,1)} %collective-permute-done.11.refs_2_), channel_id=1, source_target_pairs={{8,12},{10,14},{9,13},{11,15},{24,28},{26,30},{25,29},{27,31}} | collective-permute-start | bytes 786440 | tf_op jit(solution)/shard_map/ppermute | solution.py:180
  81.1 16.9 %copy-start.4 = (bf16[128,3072]{1,0:T(8,128)(2,1)S(1)}, bf16[128,3072]{1,0:T(8,128)(2,1)}, u32[]{:S(2)}) copy-start(bf16[128,3072]{1,0:T(8,128)(2,1)} %get-tuple-element.9) | copy-start | bytes 2359300
  97.1 2.3 %collective-permute-start.14 = (bf16[128,1024]{1,0:T(8,128)(2,1)}, bf16[128,1024]{1,0:T(8,128)(2,1)S(1)}, u32[]{:S(2)}, u32[]{:S(2)}) collective-permute-start(bf16[128,1024]{1,0:T(8,128)(2,1)} %get-tuple-element.12), channel_id=1, source_target_pairs={{0,1},{1,0},{2,3},{3,2},{4,5},{5,4},{6,7},{7,6},{8,9},{9,8},{10,11... | collective-permute-start | bytes 786440 | tf_op jit(solution)/shard_map/ppermute | solution.py:209
  (5 other events, 51.8 us)

commit v2 on v1

v2 whole, which is shorter than its diff:
```python
import functools

import jax
import jax.numpy as jnp
from jax import lax
from jax.experimental import pallas as pl
from jax.experimental.pallas import tpu as pltpu
from jax.sharding import PartitionSpec as P

QUERY_HEADS = 64
KEY_VALUE_HEADS = 8
HEAD_SIZE = 128
MASK_BLOCK_SIZE = 128
GROUP = QUERY_HEADS // KEY_VALUE_HEADS
LOG2E = 1.4426950408889634


def attend_kernel(plan, table, *refs):
    relay, columns, cores, kv_first, kv_heads, own, sibling, slots, copies, offsets, widths, aliased = plan
    refs = list(refs)
    own_queries = refs.pop(0) if own else None
    sibling_queries = refs.pop(0) if sibling else None
    pieces = [refs.pop(0) for _ in slots]
    copied = [refs.pop(0) for _ in copies]
    if aliased:
        refs.pop(0)
    out = refs.pop(0) if own else None
    sibling_out = refs.pop(0) if sibling else None
    rows_held, own_held, own_made, sibling_held, sibling_made, sems, out_sems = refs
    vertical_at, vertical_count_at, slash_at, slash_count_at, rank_at, core_at = offsets
    vertical_width, slash_width = widths
    chip_rows = cores * MASK_BLOCK_SIZE
    width = GROUP * HEAD_SIZE
    half = KEY_VALUE_HEADS // cores
    rank = table[rank_at]
    core = table[core_at]
    other = cores - 1 - core

    moves = []
    for at, (piece, slot) in enumerate(zip(pieces, slots)):
        held = rows_held.at[pl.ds(slot * chip_rows, piece.shape[0])]
        moves.append(pltpu.make_async_copy(piece, held, sems.at[at]))
    if own:
        lanes = pl.ds(pl.multiple_of((core * half + kv_first) * width, width), kv_heads * width)
        moves.append(pltpu.make_async_copy(own_queries.at[:, lanes], own_held, sems.at[len(slots)]))
    if sibling:
        lanes = pl.ds(kv_first * width, kv_heads * width)
        moves.append(pltpu.make_async_copy(sibling_queries.at[:, lanes], sibling_held, sems.at[len(slots) + 1]))
    for move in moves:
        move.start()
    placed = []
    for at, (ref, first) in enumerate(zip(copied, copies)):
        lanes = pl.ds(pl.multiple_of((other * half + first) * width, width), ref.shape[1])
        placed.append(pltpu.make_async_copy(ref, out.at[:, lanes], sems.at[len(slots) + 2 + at]))
    for move in placed:
        move.start()
    for move in moves:
        move.wait()

    square = (MASK_BLOCK_SIZE, MASK_BLOCK_SIZE)
    causal = lax.broadcasted_iota(jnp.int32, square, 0) >= lax.broadcasted_iota(jnp.int32, square, 1)
    ones = jnp.ones(square, jnp.bfloat16)
    factor = HEAD_SIZE**-0.5 * LOG2E
    own_row = (0 if relay else rank) * chip_rows

    def row_of(block):
        chip = block // cores
        if relay:
            slot = (rank // columns - chip // columns) * columns + jnp.bitwise_xor(rank % columns, chip % columns)
        else:
            slot = chip
        return (slot * cores + jnp.bitwise_xor(block % cores, core)) * MASK_BLOCK_SIZE

    def unit(queries, block, diagonal_row, head, kv):
        rows = [diagonal_row]
        active = [None]
        verticals = []
        for entry in range(vertical_width):
            vertical = table[vertical_at + head * vertical_width + entry]
            live = entry < table[vertical_count_at + head]
            verticals.append((vertical, live))
            use = live & (vertical < block)
            rows.append(row_of(jnp.where(use, vertical, block)))
            active.append(use)
        for entry in range(slash_width):
            target = block - table[slash_at + head * slash_width + entry]
            use = (entry < table[slash_count_at + head]) & (target >= 0)
            for vertical, live in verticals:
                use = use & jnp.logical_not(live & (vertical == target))
            rows.append(row_of(jnp.where(use, target, block)))
            active.append(use)
        rows = [pl.ds(pl.multiple_of(row, MASK_BLOCK_SIZE), MASK_BLOCK_SIZE) for row in rows]
        key_lanes = pl.ds(pl.multiple_of(kv * HEAD_SIZE, HEAD_SIZE), HEAD_SIZE)
        value_lanes = pl.ds(pl.multiple_of((kv_heads + kv) * HEAD_SIZE, HEAD_SIZE), HEAD_SIZE)
        keys = jnp.concatenate([rows_held[row, key_lanes] for row in rows], axis=0)
        values = jnp.concatenate(
            [jnp.concatenate([rows_held[row, value_lanes], ones], axis=1) for row in rows], axis=0
        )
        scores = lax.dot_general(queries, keys, (((1,), (1,)), ((), ())), preferred_element_type=jnp.float32)
        tiles = []
        for index, use in enumerate(active):
            tile = scores[:, index * MASK_BLOCK_SIZE : (index + 1) * MASK_BLOCK_SIZE]
            tiles.append(jnp.where(causal if use is None else use, tile, -jnp.inf))
        peak = functools.reduce(jnp.maximum, tiles)
        peak = jnp.max(peak, axis=1, keepdims=True)
        weights = [jnp.exp2((tile - peak) * factor).astype(jnp.bfloat16) for tile in tiles]
        sums = jnp.dot(jnp.concatenate(weights, axis=1), values, preferred_element_type=jnp.float32)
        return (sums[:, :HEAD_SIZE] / sums[:, HEAD_SIZE:]).astype(jnp.bfloat16)

    def results(kv):
        lanes = pl.ds(pl.multiple_of(kv * width, width), width)
        made = []
        if own:
            target = pl.ds(pl.multiple_of((core * half + kv_first + kv) * width, width), width)
            made.append(pltpu.make_async_copy(own_made.at[:, lanes], out.at[:, target], out_sems.at[kv, 0]))
        if sibling:
            made.append(pltpu.make_async_copy(sibling_made.at[:, lanes], sibling_out.at[:, lanes], out_sems.at[kv, 1]))
        return made

    def of_head(kv, carry):
        for slot in range(GROUP):
            head = (core * half + kv_first + kv) * GROUP + slot
            lanes = pl.ds(pl.multiple_of(kv * width + slot * HEAD_SIZE, HEAD_SIZE), HEAD_SIZE)
            if own:
                own_made[:, lanes] = unit(own_held[:, lanes], rank * cores + core, own_row, head, kv)
            if sibling:
                sibling_made[:, lanes] = unit(
                    sibling_held[:, lanes], rank * cores + other, own_row + MASK_BLOCK_SIZE, head, kv
                )
        for move in results(kv):
            move.start()
        return carry

    lax.fori_loop(0, kv_heads, of_head, 0)
    for kv in range(kv_heads):
        for move in results(kv):
            move.wait()
    for move in placed:
        move.wait()


def attend(table, common, kv_first, kv_heads, queries, sibling_queries, pieces, slots, copies=(), into=None):
    relay, columns, cores, offsets, widths = common
    own, sibling = queries is not None, sibling_queries is not None
    some = queries if own else sibling_queries
    tokens = some.shape[0]
    width = kv_heads * GROUP * HEAD_SIZE
    plan = (relay, columns, cores, kv_first, kv_heads, own, sibling, tuple(slots), tuple(first for _, first in copies))
    plan += (offsets, widths, into is not None)
    operands = [array for array in (queries, sibling_queries) if array is not None]
    operands += list(pieces) + [array for array, _ in copies]
    aliases = {}
    if into is not None:
        aliases = {1 + len(operands): 0}
        operands.append(into)
    shapes = []
    if own:
        shapes.append(jax.ShapeDtypeStruct((tokens, QUERY_HEADS * HEAD_SIZE), jnp.bfloat16))
    if sibling:
        shapes.append(jax.ShapeDtypeStruct((tokens, width), jnp.bfloat16))
    anywhere = pl.BlockSpec(memory_space=pl.ANY)
    held = pltpu.VMEM((tokens, width), jnp.bfloat16)
    small = pltpu.VMEM((16, HEAD_SIZE), jnp.bfloat16)
    rows = sum(piece.shape[0] for piece in pieces)
    return pl.pallas_call(
        functools.partial(attend_kernel, plan),
        grid_spec=pltpu.PrefetchScalarGridSpec(
            num_scalar_prefetch=1,
            grid=(),
            in_specs=[anywhere] * len(operands),
            out_specs=[anywhere] * len(shapes),
            scratch_shapes=[pltpu.VMEM((rows, 2 * kv_heads * HEAD_SIZE), jnp.bfloat16)]
            + [held if own else small] * 2
            + [held if sibling else small] * 2
            + [
                pltpu.SemaphoreType.DMA((len(pieces) + 2 + max(1, len(copies)),)),
                pltpu.SemaphoreType.DMA((kv_heads, 2)),
            ],
        ),
        out_shape=shapes,
        input_output_aliases=aliases,
        name="attend",
    )(table, *operands)


def shards(queries, keys, values, vertical_blocks, vertical_count, slash_offsets, slash_count):
    tokens = queries.shape[0]
    ranks = lax.axis_size("seq")
    cores = lax.axis_size("tp")
    assert tokens == MASK_BLOCK_SIZE and cores == 2
    rank = lax.axis_index("seq")
    core = lax.axis_index("tp")
    other = cores - 1 - core
    columns = 2
    relay = ranks == 8
    lines = ranks // columns
    half = KEY_VALUE_HEADS // cores
    group_width = GROUP * HEAD_SIZE
    swap = [(0, 1), (1, 0)]
    chunks = ((0, half // 2), (half // 2, half - half // 2))

    parts = [vertical_blocks, vertical_count, slash_offsets, slash_count, rank, core]
    sizes = [part.size for part in parts]
    offsets = tuple(sum(sizes[:n]) for n in range(len(sizes)))
    table = jnp.concatenate([part.astype(jnp.int32).reshape(-1) for part in parts])
    common = (relay, columns, cores, offsets, (vertical_blocks.shape[1], slash_offsets.shape[1]))

    def taken(of_core, first, count):
        start = (of_core * half + first) * HEAD_SIZE
        return jnp.concatenate(
            [lax.dynamic_slice_in_dim(array, start, count * HEAD_SIZE, 1) for array in (keys, values)], axis=1
        )

    local = []
    for (first, count) in chunks:
        got = lax.ppermute(taken(other, first, count), "tp", swap)
        local.append(jnp.concatenate([taken(core, first, count), got], axis=0))
    sibling_queries = lax.ppermute(
        lax.dynamic_slice_in_dim(queries, other * half * group_width, half * group_width, 1), "tp", swap
    )

    if relay:

        def along(array, step):
            pairs = [
                (line * columns + column, (line + 1) * columns + column)
                for line in range(step - 1, lines - 1)
                for column in range(columns)
            ]
            return lax.ppermute(array, "seq", pairs)

        def across(array, step):
            pairs = [
                (line * columns + column, line * columns + 1 - column)
                for line in range(step, lines)
                for column in range(columns)
            ]
            return lax.ppermute(array, "seq", pairs)

        gathered = []
        for name, piece in zip("ab", local):
            line_pieces = [piece]
            for step in range(1, lines):
                line_pieces.append(along(line_pieces[-1], step))
            last = lines if name == "a" else lines - 1
            cross_pieces = [across(line_pieces[step], step) for step in range(last)]
            if name == "b":
                pairs = [(column, (lines - 1) * columns + column) for column in range(columns)]
                cross_pieces.append(lax.ppermute(cross_pieces[0], "seq", pairs))
            gathered.append(line_pieces + cross_pieces)
        slots = [step * columns for step in range(lines)] + [step * columns + 1 for step in range(lines)]
    else:
        gathered = [[lax.all_gather(piece, "seq", axis=0, tiled=True)] for piece in local]
        slots = [0]

    (first_a, count_a), (first_b, count_b) = chunks
    out, sibling_a = attend(table, common, first_a, count_a, queries, sibling_queries, gathered[0], slots)
    got_a = lax.ppermute(sibling_a, "tp", swap)
    (sibling_b,) = attend(table, common, first_b, count_b, None, sibling_queries, gathered[1], slots)
    got_b = lax.ppermute(sibling_b, "tp", swap)
    (out,) = attend(
        table, common, first_b, count_b, queries, None, gathered[1], slots, [(got_a, first_a)], out
    )
    return lax.dynamic_update_slice_in_dim(out, got_b, (other * half + first_b) * group_width, 1)


def solution(mesh):
    return jax.shard_map(
        shards,
        mesh=mesh,
        in_specs=(
            P(("groups", "seq", "tp"), None),
            P(("groups", "seq", "tp"), None),
            P(("groups", "seq", "tp"), None),
            P(),
            P(),
            P(),
            P(),
        ),
        out_specs=P(("groups", "seq", "tp"), None),
        check_vma=False,
    )
```

time: 101 us -> 93.4 us (0.925)
  the two profiles are of different devices: /device:TPU:31 before, /device:TPU:17 now
where the time goes in v2:
time: 93.4 us; the launch traced here: 92.8 us
  starting transfers between devices  43.1 us (46%)
  Pallas kernels  32.5 us (35%)
  waiting for transfers between devices  9.92 us (11%)
  local copies, waits for them, and re-layouts  6.75 us (7%)
    pallas_call x3, Pallas kernels, attend(): pl.pallas_call(functools.partial(attend_kernel, plan), grid_spec=pltpu.Pr...  32.5 us
    ppermute x6, starting transfers between devices, along(): return lax.ppermute(array, 'seq', pairs)  19.3 us
    ppermute x7, starting transfers between devices, across(): return lax.ppermute(array, 'seq', pairs)  13.5 us
    ppermute x6, waiting for transfers between devices, along(): return lax.ppermute(array, 'seq', pairs)  9.01 us
    ppermute x1, starting transfers between devices, shards(): got_a = lax.ppermute(sibling_a, 'tp', swap)  7.91 us
    unnamed x42, local copies, waits for them, and re-layouts  2.57 us
  transfers between devices with their start and end apart: 19, of which 5 were waited for; matrix products, arithmetic and copies ran while one was open for 3% of the time, Pallas kernels for 35%

profile of v2, /device:TPU:17, one launch (start us, length us, event | category | flops | bytes accessed | tf_op | source)
XLA Modules:
  0.0 92.8 jit_solution(17760596362830907720)
XLA Ops:
  0.0 1.1 %constant_dynamic-slice_fusion.2 = (bf16[128,256]{1,0:T(8,128)(2,1)S(1)}, bf16[128,256]{1,0:T(8,128)(2,1)S(1)}, bf16[128,256]{1,0:T(8,128)(2,1)S(1)}, bf16[128,2...) fusion(bf16[128,1024]{1,0:T(8,128)(2,1)} %param.9, ...), kind=kLoop, calls=%fused_computation.7 | loop fusion | bytes 1048592 | tf_op jit(solution)/shard_map/dynamic_slice | solution.py:211
  1.9 1.3 %constant_dynamic-slice_fusion.4 = bf16[128,4096]{1,0:T(8,128)(2,1)S(1)} fusion(bf16[128,8192]{1,0:T(8,128)(2,1)} %refs_0_.3, s32[]{:T(128)S(6)} %select_n.24), kind=kLoop, calls=%fused_computation.9 | loop fusion | bytes 2097156 | tf_op jit(solution)/shard_map/dynamic_slice | solution.py:219
  3.3 3.2 %collective-permute-start.10 = (bf16[256,512]{1,0:T(8,128)(2,1)S(1)}, bf16[256,512]{1,0:T(8,128)(2,1)S(1)}, u32[]{:S(2)}, u32[]{:S(2)}) collective-permute-start(bf16[256,512]{1,0:T(8,128)(2,1)S(1)} %pad_maximum_fusion.1.refs_2_), channel_id=1, source_target_pairs={{0,4},{2,6},{4,8},{6,10},{8,12},{10,14},{1,5},{3,7},{5,9},{7,11},{... | collective-permute-start | bytes 786440 | tf_op jit(solution)/shard_map/ppermute | solution.py:230
  6.6 0.8 collective-permute-start
  7.4 5.2 %collective-permute-done.10.refs_3_ = bf16[256,512]{1,0:T(8,128)(2,1)S(1)} collective-permute-done((bf16[256,512]{1,0:T(8,128)(2,1)S(1)}, bf16[256,512]{1,0:T(8,128)(2,1)S(1)}, u32[]{:S(2)}, u32[]{:S(2)}) %collective-permute-start.10) | collective-permute-done | bytes 262176 | tf_op jit(solution)/shard_map/ppermute | solution.py:230
  12.6 3.2 %collective-permute-start.11 = (bf16[256,512]{1,0:T(8,128)(2,1)S(1)}, bf16[256,512]{1,0:T(8,128)(2,1)S(1)}, u32[]{:S(2)}, u32[]{:S(2)}) collective-permute-start(bf16[256,512]{1,0:T(8,128)(2,1)S(1)} %collective-permute-done.10.refs_3_), channel_id=1, source_target_pairs={{4,8},{6,10},{8,12},{10,14},{5,9},{7,11},{9,13},{11,15},{20,24},{2... | collective-permute-start | bytes 786440 | tf_op jit(solution)/shard_map/ppermute | solution.py:230
  15.9 1.9 %collective-permute-start.1 = (bf16[256,512]{1,0:T(8,128)(2,1)S(1)}, bf16[256,512]{1,0:T(8,128)(2,1)S(1)}, u32[]{:S(2)}, u32[]{:S(2)}) collective-permute-start(bf16[256,512]{1,0:T(8,128)(2,1)S(1)} %pad_maximum_fusion.refs_1_), channel_id=1, source_target_pairs={{0,4},{2,6},{4,8},{6,10},{8,12},{10,14},{1,5},{3,7},{5,9},{7,11},{... | collective-permute-start | bytes 786440 | tf_op jit(solution)/shard_map/ppermute | solution.py:230
  17.8 1.3 %collective-permute-start.4 = (bf16[256,512]{1,0:T(8,128)(2,1)S(1)}, bf16[256,512]{1,0:T(8,128)(2,1)S(1)}, u32[]{:S(2)}, u32[]{:S(2)}) collective-permute-start(bf16[256,512]{1,0:T(8,128)(2,1)S(1)} %pad_maximum_fusion.refs_1_), channel_id=1, source_target_pairs={{0,2},{2,0},{4,6},{6,4},{8,10},{10,8},{12,14},{14,12},{1,3},{3,1},... | collective-permute-start | bytes 786440 | tf_op jit(solution)/shard_map/ppermute | solution.py:238
  19.3 1.7 %collective-permute-done.11.refs_4_ = bf16[256,512]{1,0:T(8,128)(2,1)S(1)} collective-permute-done((bf16[256,512]{1,0:T(8,128)(2,1)S(1)}, bf16[256,512]{1,0:T(8,128)(2,1)S(1)}, u32[]{:S(2)}, u32[]{:S(2)}) %collective-permute-start.11) | collective-permute-done | bytes 262176 | tf_op jit(solution)/shard_map/ppermute | solution.py:230
  21.0 3.9 %collective-permute-start.12 = (bf16[256,512]{1,0:T(8,128)(2,1)S(1)}, bf16[256,512]{1,0:T(8,128)(2,1)}, u32[]{:S(2)}, u32[]{:S(2)}) collective-permute-start(bf16[256,512]{1,0:T(8,128)(2,1)S(1)} %collective-permute-done.11.refs_4_), channel_id=1, source_target_pairs={{8,12},{10,14},{9,13},{11,15},{24,28},{26,30},{25,29},{27,31}} | collective-permute-start | bytes 786440 | tf_op jit(solution)/shard_map/ppermute | solution.py:230
  24.9 1.7 %collective-permute-done.1.refs_2_ = bf16[256,512]{1,0:T(8,128)(2,1)S(1)} collective-permute-done((bf16[256,512]{1,0:T(8,128)(2,1)S(1)}, bf16[256,512]{1,0:T(8,128)(2,1)S(1)}, u32[]{:S(2)}, u32[]{:S(2)}) %collective-permute-start.1) | collective-permute-done | bytes 262176 | tf_op jit(solution)/shard_map/ppermute | solution.py:230
  26.6 3.2 %collective-permute-start.2 = (bf16[256,512]{1,0:T(8,128)(2,1)S(1)}, bf16[256,512]{1,0:T(8,128)(2,1)S(1)}, u32[]{:S(2)}, u32[]{:S(2)}) collective-permute-start(bf16[256,512]{1,0:T(8,128)(2,1)S(1)} %collective-permute-done.1.refs_2_), channel_id=1, source_target_pairs={{4,8},{6,10},{8,12},{10,14},{5,9},{7,11},{9,13},{11,15},{20,24},{2... | collective-permute-start | bytes 786440 | tf_op jit(solution)/shard_map/ppermute | solution.py:230
  29.9 3.1 %collective-permute-start.14 = (bf16[256,512]{1,0:T(8,128)(2,1)S(1)}, bf16[256,512]{1,0:T(8,128)(2,1)S(1)}, u32[]{:S(2)}, u32[]{:S(2)}) collective-permute-start(bf16[256,512]{1,0:T(8,128)(2,1)S(1)} %collective-permute-done.10.refs_3_), channel_id=1, source_target_pairs={{4,6},{6,4},{8,10},{10,8},{12,14},{14,12},{5,7},{7,5},{9,11},{11,9... | collective-permute-start | bytes 786440 | tf_op jit(solution)/shard_map/ppermute | solution.py:238
  33.0 2.1 %collective-permute-start.15 = (bf16[256,512]{1,0:T(8,128)(2,1)S(1)}, bf16[256,512]{1,0:T(8,128)(2,1)S(1)}, u32[]{:S(2)}, u32[]{:S(2)}) collective-permute-start(bf16[256,512]{1,0:T(8,128)(2,1)S(1)} %collective-permute-done.11.refs_4_), channel_id=1, source_target_pairs={{8,10},{10,8},{12,14},{14,12},{9,11},{11,9},{13,15},{15,13},{24,26... | collective-permute-start | bytes 786440 | tf_op jit(solution)/shard_map/ppermute | solution.py:238
  35.2 1.4 %collective-permute-start.16 = (bf16[256,512]{1,0:T(8,128)(2,1)}, bf16[256,512]{1,0:T(8,128)(2,1)}, u32[]{:S(2)}, u32[]{:S(2)}) collective-permute-start(bf16[256,512]{1,0:T(8,128)(2,1)} %collective-permute-done.12.refs_5_), channel_id=1, source_target_pairs={{12,14},{14,12},{13,15},{15,13},{28,30},{30,28},{29,31},{31,29}} | collective-permute-start | bytes 786440 | tf_op jit(solution)/shard_map/ppermute | solution.py:238
  37.0 3.1 %collective-permute-start.5 = (bf16[256,512]{1,0:T(8,128)(2,1)S(1)}, bf16[256,512]{1,0:T(8,128)(2,1)S(1)}, u32[]{:S(2)}, u32[]{:S(2)}) collective-permute-start(bf16[256,512]{1,0:T(8,128)(2,1)S(1)} %collective-permute-done.1.refs_2_), channel_id=1, source_target_pairs={{4,6},{6,4},{8,10},{10,8},{12,14},{14,12},{5,7},{7,5},{9,11},{11,9... | collective-permute-start | bytes 786440 | tf_op jit(solution)/shard_map/ppermute | solution.py:238
  40.8 0.9 collective-permute-done.15.refs_8_
  41.7 3.9 %collective-permute-start.3 = (bf16[256,512]{1,0:T(8,128)(2,1)S(1)}, bf16[256,512]{1,0:T(8,128)(2,1)S(1)}, u32[]{:S(2)}, u32[]{:S(2)}) collective-permute-start(bf16[256,512]{1,0:T(8,128)(2,1)S(1)} %collective-permute-done.2.refs_3_), channel_id=1, source_target_pairs={{8,12},{10,14},{9,13},{11,15},{24,28},{26,30},{25,29},{27,31}} | collective-permute-start | bytes 786440 | tf_op jit(solution)/shard_map/ppermute | solution.py:230
  45.6 2.1 %collective-permute-start.6 = (bf16[256,512]{1,0:T(8,128)(2,1)S(1)}, bf16[256,512]{1,0:T(8,128)(2,1)S(1)}, u32[]{:S(2)}, u32[]{:S(2)}) collective-permute-start(bf16[256,512]{1,0:T(8,128)(2,1)S(1)} %collective-permute-done.2.refs_3_), channel_id=1, source_target_pairs={{8,10},{10,8},{12,14},{14,12},{9,11},{11,9},{13,15},{15,13},{24,26... | collective-permute-start | bytes 786440 | tf_op jit(solution)/shard_map/ppermute | solution.py:238
  49.0 8.4 %attend.3 = (bf16[128,8192]{1,0:T(8,128)(2,1)}, bf16[128,2048]{1,0:T(8,128)(2,1)}) custom-call(s32[386]{0:T(512)} %concatenate.21.table, bf16[128,8192]{1,0:T(8,128)(2,1)} %refs_0_.3, bf16[128,4096]{1,0:T(8,128)(2,1)} %copy-done, bf16[256,512]{1,0:T(8,128)(2,1)} %copy-done.9, bf16[256,512]{1,0:T(8,128)(2,1)} %copy-done.11, bf16[256,512]{1,0:T(8,128)(2,1)} %copy-done.12, ...), custom_call_target="tpu_custom_call" | custom-call | tf_op jit(solution)/shard_map/attend/pallas_call | solution.py:165
  57.5 7.9 %collective-permute-start.17 = (bf16[128,2048]{1,0:T(8,128)(2,1)}, bf16[128,2048]{1,0:T(8,128)(2,1)S(1)}, u32[]{:S(2)}, u32[]{:S(2)}) collective-permute-start(bf16[128,2048]{1,0:T(8,128)(2,1)} %get-tuple-element.7), channel_id=1, source_target_pairs={{0,1},{1,0},{2,3},{3,2},{4,5},{5,4},{6,7},{7,6},{8,9},{9,8},{10,11... | collective-permute-start | bytes 1572872 | tf_op jit(solution)/shard_map/ppermute | solution.py:258
  67.0 6.2 %attend.5 = bf16[128,2048]{1,0:T(8,128)(2,1)} custom-call(s32[386]{0:T(512)} %concatenate.21.table, bf16[128,4096]{1,0:T(8,128)(2,1)} %copy-done, bf16[256,512]{1,0:T(8,128)(2,1)} %copy-done.1, bf16[256,512]{1,0:T(8,128)(2,1)} %copy-done.2, bf16[256,512]{1,0:T(8,128)(2,1)} %copy-done.4, bf16[256,512]{1,0:T(8,128)(2,1)} %copy-done.7, ...), custom_call_target="tpu_custom_call" | custom-call | tf_op jit(solution)/shard_map/attend/pallas_call | solution.py:165
  74.1 17.8 %attend.4 = bf16[128,8192]{1,0:T(8,128)(2,1)} custom-call(s32[386]{0:T(512)} %concatenate.21.table, bf16[128,8192]{1,0:T(8,128)(2,1)} %refs_0_.3, bf16[256,512]{1,0:T(8,128)(2,1)} %copy-done.1, bf16[256,512]{1,0:T(8,128)(2,1)} %copy-done.2, bf16[256,512]{1,0:T(8,128)(2,1)} %copy-done.4, bf16[256,512]{1,0:T(8,128)(2,1)} %copy-done.7, ...), custom_call_target="tpu_custom_call", output_to_operand_aliasing={{}: (11, {})} | custom-call | tf_op jit(solution)/shard_map/attend/pallas_call | solution.py:165
  91.9 0.8 constant_dynamic-update-slice_fusion
  (69 shorter events, 5.8 us)
Async XLA Ops:
  1.1 46.7 %copy-start.16 = (s32[64,2]{0,1:T(2,128)S(1)}, s32[64,2]{0,1:T(2,128)}, u32[]{:S(2)}) copy-start(s32[64,2]{0,1:T(2,128)} %param.10) | copy-start | bytes 1540
  1.1 46.9 %copy-start.17 = (s32[64,2]{0,1:T(2,128)S(1)}, s32[64,2]{0,1:T(2,128)}, u32[]{:S(2)}) copy-start(s32[64,2]{0,1:T(2,128)} %param.12) | copy-start | bytes 1540
  1.1 47.2 %copy-start.18 = (s32[64]{0:T(128)S(1)}, s32[64]{0:T(128)}, u32[]{:S(2)}) copy-start(s32[64]{0:T(128)} %param.11) | copy-start | bytes 772
  1.1 47.2 %copy-start.19 = (s32[64]{0:T(128)S(1)}, s32[64]{0:T(128)}, u32[]{:S(2)}) copy-start(s32[64]{0:T(128)} %param.13) | copy-start | bytes 772
  1.2 2.1 %collective-permute-start.9 = (bf16[128,512]{1,0:T(8,128)(2,1)S(1)}, bf16[128,512]{1,0:T(8,128)(2,1)S(1)}, u32[]{:S(2)}, u32[]{:S(2)}) collective-permute-start(bf16[128,512]{1,0:T(8,128)(2,1)S(1)} %pad_maximum_fusion.3), channel_id=1, source_target_pairs={{0,1},{1,0},{2,3},{3,2},{4,5},{5,4},{6,7},{7,6},{8,9},{9,8},{10,11... | collective-permute-start | bytes 393224 | tf_op jit(solution)/shard_map/ppermute | solution.py:216
  3.2 42.4 %collective-permute-start.8 = (bf16[128,4096]{1,0:T(8,128)(2,1)S(1)}, bf16[128,4096]{1,0:T(8,128)(2,1)S(1)}, u32[]{:S(2)}, u32[]{:S(2)}) collective-permute-start(bf16[128,4096]{1,0:T(8,128)(2,1)S(1)} %constant_dynamic-slice_fusion.4), channel_id=1, source_target_pairs={{0,1},{1,0},{2,3},{3,2},{4,5},{5,4},{6,7},{7,6},{8,9},{9,8},{10,11... | collective-permute-start | bytes 3145736 | tf_op jit(solution)/shard_map/ppermute | solution.py:218
  3.3 9.3 %collective-permute-start.10 = (bf16[256,512]{1,0:T(8,128)(2,1)S(1)}, bf16[256,512]{1,0:T(8,128)(2,1)S(1)}, u32[]{:S(2)}, u32[]{:S(2)}) collective-permute-start(bf16[256,512]{1,0:T(8,128)(2,1)S(1)} %pad_maximum_fusion.1.refs_2_), channel_id=1, source_target_pairs={{0,4},{2,6},{4,8},{6,10},{8,12},{10,14},{1,5},{3,7},{5,9},{7,11},{... | collective-permute-start | bytes 786440 | tf_op jit(solution)/shard_map/ppermute | solution.py:230
  6.6 9.2 %collective-permute-start = (bf16[128,512]{1,0:T(8,128)(2,1)S(1)}, bf16[128,512]{1,0:T(8,128)(2,1)S(1)}, u32[]{:S(2)}, u32[]{:S(2)}) collective-permute-start(bf16[128,512]{1,0:T(8,128)(2,1)S(1)} %pad_maximum_fusion.2), channel_id=1, source_target_pairs={{0,1},{1,0},{2,3},{3,2},{4,5},{5,4},{6,7},{7,6},{8,9},{9,8},{10,11... | collective-permute-start | bytes 393224 | tf_op jit(solution)/shard_map/ppermute | solution.py:216
  12.6 8.4 %collective-permute-start.11 = (bf16[256,512]{1,0:T(8,128)(2,1)S(1)}, bf16[256,512]{1,0:T(8,128)(2,1)S(1)}, u32[]{:S(2)}, u32[]{:S(2)}) collective-permute-start(bf16[256,512]{1,0:T(8,128)(2,1)S(1)} %collective-permute-done.10.refs_3_), channel_id=1, source_target_pairs={{4,8},{6,10},{8,12},{10,14},{5,9},{7,11},{9,13},{11,15},{20,24},{2... | collective-permute-start | bytes 786440 | tf_op jit(solution)/shard_map/ppermute | solution.py:230
  15.8 49.6 %copy-start.1 = (bf16[256,512]{1,0:T(8,128)(2,1)}, bf16[256,512]{1,0:T(8,128)(2,1)S(1)}, u32[]{:S(2)}) copy-start(bf16[256,512]{1,0:T(8,128)(2,1)S(1)} %pad_maximum_fusion.refs_1_) | copy-start | bytes 786436
  15.9 10.8 %collective-permute-start.1 = (bf16[256,512]{1,0:T(8,128)(2,1)S(1)}, bf16[256,512]{1,0:T(8,128)(2,1)S(1)}, u32[]{:S(2)}, u32[]{:S(2)}) collective-permute-start(bf16[256,512]{1,0:T(8,128)(2,1)S(1)} %pad_maximum_fusion.refs_1_), channel_id=1, source_target_pairs={{0,4},{2,6},{4,8},{6,10},{8,12},{10,14},{1,5},{3,7},{5,9},{7,11},{... | collective-permute-start | bytes 786440 | tf_op jit(solution)/shard_map/ppermute | solution.py:230
  17.8 12.1 %collective-permute-start.4 = (bf16[256,512]{1,0:T(8,128)(2,1)S(1)}, bf16[256,512]{1,0:T(8,128)(2,1)S(1)}, u32[]{:S(2)}, u32[]{:S(2)}) collective-permute-start(bf16[256,512]{1,0:T(8,128)(2,1)S(1)} %pad_maximum_fusion.refs_1_), channel_id=1, source_target_pairs={{0,2},{2,0},{4,6},{6,4},{8,10},{10,8},{12,14},{14,12},{1,3},{3,1},... | collective-permute-start | bytes 786440 | tf_op jit(solution)/shard_map/ppermute | solution.py:238
  19.1 13.9 %collective-permute-start.13 = (bf16[256,512]{1,0:T(8,128)(2,1)S(1)}, bf16[256,512]{1,0:T(8,128)(2,1)S(1)}, u32[]{:S(2)}, u32[]{:S(2)}) collective-permute-start(bf16[256,512]{1,0:T(8,128)(2,1)S(1)} %pad_maximum_fusion.1.refs_2_), channel_id=1, source_target_pairs={{0,2},{2,0},{4,6},{6,4},{8,10},{10,8},{12,14},{14,12},{1,3},{3,1},... | collective-permute-start | bytes 786440 | tf_op jit(solution)/shard_map/ppermute | solution.py:238
  21.0 14.2 %collective-permute-start.12 = (bf16[256,512]{1,0:T(8,128)(2,1)S(1)}, bf16[256,512]{1,0:T(8,128)(2,1)}, u32[]{:S(2)}, u32[]{:S(2)}) collective-permute-start(bf16[256,512]{1,0:T(8,128)(2,1)S(1)} %collective-permute-done.11.refs_4_), channel_id=1, source_target_pairs={{8,12},{10,14},{9,13},{11,15},{24,28},{26,30},{25,29},{27,31}} | collective-permute-start | bytes 786440 | tf_op jit(solution)/shard_map/ppermute | solution.py:230
  26.6 10.3 %collective-permute-start.2 = (bf16[256,512]{1,0:T(8,128)(2,1)S(1)}, bf16[256,512]{1,0:T(8,128)(2,1)S(1)}, u32[]{:S(2)}, u32[]{:S(2)}) collective-permute-start(bf16[256,512]{1,0:T(8,128)(2,1)S(1)} %collective-permute-done.1.refs_2_), channel_id=1, source_target_pairs={{4,8},{6,10},{8,12},{10,14},{5,9},{7,11},{9,13},{11,15},{20,24},{2... | collective-permute-start | bytes 786440 | tf_op jit(solution)/shard_map/ppermute | solution.py:230
  29.9 10.3 %collective-permute-start.14 = (bf16[256,512]{1,0:T(8,128)(2,1)S(1)}, bf16[256,512]{1,0:T(8,128)(2,1)S(1)}, u32[]{:S(2)}, u32[]{:S(2)}) collective-permute-start(bf16[256,512]{1,0:T(8,128)(2,1)S(1)} %collective-permute-done.10.refs_3_), channel_id=1, source_target_pairs={{4,6},{6,4},{8,10},{10,8},{12,14},{14,12},{5,7},{7,5},{9,11},{11,9... | collective-permute-start | bytes 786440 | tf_op jit(solution)/shard_map/ppermute | solution.py:238
  33.0 8.7 %collective-permute-start.15 = (bf16[256,512]{1,0:T(8,128)(2,1)S(1)}, bf16[256,512]{1,0:T(8,128)(2,1)S(1)}, u32[]{:S(2)}, u32[]{:S(2)}) collective-permute-start(bf16[256,512]{1,0:T(8,128)(2,1)S(1)} %collective-permute-done.11.refs_4_), channel_id=1, source_target_pairs={{8,10},{10,8},{12,14},{14,12},{9,11},{11,9},{13,15},{15,13},{24,26... | collective-permute-start | bytes 786440 | tf_op jit(solution)/shard_map/ppermute | solution.py:238
  35.2 13.8 %collective-permute-start.16 = (bf16[256,512]{1,0:T(8,128)(2,1)}, bf16[256,512]{1,0:T(8,128)(2,1)}, u32[]{:S(2)}, u32[]{:S(2)}) collective-permute-start(bf16[256,512]{1,0:T(8,128)(2,1)} %collective-permute-done.12.refs_5_), channel_id=1, source_target_pairs={{12,14},{14,12},{13,15},{15,13},{28,30},{30,28},{29,31},{31,29}} | collective-permute-start | bytes 786440 | tf_op jit(solution)/shard_map/ppermute | solution.py:238
  37.0 28.4 %collective-permute-start.5 = (bf16[256,512]{1,0:T(8,128)(2,1)S(1)}, bf16[256,512]{1,0:T(8,128)(2,1)S(1)}, u32[]{:S(2)}, u32[]{:S(2)}) collective-permute-start(bf16[256,512]{1,0:T(8,128)(2,1)S(1)} %collective-permute-done.1.refs_2_), channel_id=1, source_target_pairs={{4,6},{6,4},{8,10},{10,8},{12,14},{14,12},{5,7},{7,5},{9,11},{11,9... | collective-permute-start | bytes 786440 | tf_op jit(solution)/shard_map/ppermute | solution.py:238
  40.1 25.2 %collective-permute-start.7 = (bf16[256,512]{1,0:T(8,128)(2,1)S(1)}, bf16[256,512]{1,0:T(8,128)(2,1)S(1)}, u32[]{:S(2)}, u32[]{:S(2)}) collective-permute-start(bf16[256,512]{1,0:T(8,128)(2,1)S(1)} %collective-permute-done.4.refs_5_), channel_id=1, source_target_pairs={{0,12},{2,14},{1,13},{3,15},{16,28},{18,30},{17,29},{19,31}} | collective-permute-start | bytes 786440 | tf_op jit(solution)/shard_map/ppermute | solution.py:249
  41.7 23.7 %collective-permute-start.3 = (bf16[256,512]{1,0:T(8,128)(2,1)S(1)}, bf16[256,512]{1,0:T(8,128)(2,1)S(1)}, u32[]{:S(2)}, u32[]{:S(2)}) collective-permute-start(bf16[256,512]{1,0:T(8,128)(2,1)S(1)} %collective-permute-done.2.refs_3_), channel_id=1, source_target_pairs={{8,12},{10,14},{9,13},{11,15},{24,28},{26,30},{25,29},{27,31}} | collective-permute-start | bytes 786440 | tf_op jit(solution)/shard_map/ppermute | solution.py:230
  45.6 19.8 %collective-permute-start.6 = (bf16[256,512]{1,0:T(8,128)(2,1)S(1)}, bf16[256,512]{1,0:T(8,128)(2,1)S(1)}, u32[]{:S(2)}, u32[]{:S(2)}) collective-permute-start(bf16[256,512]{1,0:T(8,128)(2,1)S(1)} %collective-permute-done.2.refs_3_), channel_id=1, source_target_pairs={{8,10},{10,8},{12,14},{14,12},{9,11},{11,9},{13,15},{15,13},{24,26... | collective-permute-start | bytes 786440 | tf_op jit(solution)/shard_map/ppermute | solution.py:238
  57.5 15.8 %collective-permute-start.17 = (bf16[128,2048]{1,0:T(8,128)(2,1)}, bf16[128,2048]{1,0:T(8,128)(2,1)S(1)}, u32[]{:S(2)}, u32[]{:S(2)}) collective-permute-start(bf16[128,2048]{1,0:T(8,128)(2,1)} %get-tuple-element.7), channel_id=1, source_target_pairs={{0,1},{1,0},{2,3},{3,2},{4,5},{5,4},{6,7},{7,6},{8,9},{9,8},{10,11... | collective-permute-start | bytes 1572872 | tf_op jit(solution)/shard_map/ppermute | solution.py:258
  73.2 18.7 %collective-permute-start.18 = (bf16[128,2048]{1,0:T(8,128)(2,1)}, bf16[128,2048]{1,0:T(8,128)(2,1)S(1)}, u32[]{:S(2)}, u32[]{:S(2)}) collective-permute-start(bf16[128,2048]{1,0:T(8,128)(2,1)} %attend.5), channel_id=1, source_target_pairs={{0,1},{1,0},{2,3},{3,2},{4,5},{5,4},{6,7},{7,6},{8,9},{9,8},{10,11... | collective-permute-start | bytes 1572872 | tf_op jit(solution)/shard_map/ppermute | solution.py:260
  (15 other events, 235.4 us)

commit v3 on v2

--- a/solution.py
+++ b/solution.py
@@ -256,12 +256,13 @@
     (first_a, count_a), (first_b, count_b) = chunks
     out, sibling_a = attend(table, common, first_a, count_a, queries, sibling_queries, gathered[0], slots)
     got_a = lax.ppermute(sibling_a, "tp", swap)
-    (sibling_b,) = attend(table, common, first_b, count_b, None, sibling_queries, gathered[1], slots)
+    out, sibling_b = attend(
+        table, common, first_b, count_b, queries, sibling_queries, gathered[1], slots, into=out
+    )
     got_b = lax.ppermute(sibling_b, "tp", swap)
-    (out,) = attend(
-        table, common, first_b, count_b, queries, None, gathered[1], slots, [(got_a, first_a)], out
-    )
-    return lax.dynamic_update_slice_in_dim(out, got_b, (other * half + first_b) * group_width, 1)
+    for got, first in ((got_a, first_a), (got_b, first_b)):
+        out = lax.dynamic_update_slice_in_dim(out, got, (other * half + first) * group_width, 1)
+    return out
 
 
 def solution(mesh):

time: 93.4 us -> 78.1 us (0.84)
  Pallas kernels: 32.5 us -> 16.9 us
  local copies, waits for them, and re-layouts: 6.75 us -> 5.25 us
  waiting for transfers between devices: 9.92 us -> 11.2 us
    pallas_call x3 -> x2, Pallas kernels: 32.5 us -> 16.9 us  [attend(): pl.pallas_call(functools.partial(attend_kernel, plan), grid_spec=pltpu.Pr...]
    unnamed x42 -> x34, local copies, waits for them, and re-layouts: 2.57 us -> 0.26 us
    ppermute x1, waiting for transfers between devices: 0.01 us -> 1.26 us  [shards(): got_b = lax.ppermute(sibling_b, 'tp', swap)]
  transfers between devices with their start and end apart: 19 -> 19, of which waited for: 5 -> 6; matrix products, arithmetic and copies ran while one was open for 3% -> 4% of each run, Pallas kernels for 35% -> 22%
where the time goes in v3:
time: 78.1 us; the launch traced here: 77.6 us
  starting transfers between devices  43.8 us (56%)
  Pallas kernels  16.9 us (22%)
  waiting for transfers between devices  11.2 us (14%)
  local copies, waits for them, and re-layouts  5.25 us (7%)
    ppermute x6, starting transfers between devices, along(): return lax.ppermute(array, 'seq', pairs)  19 us
    pallas_call x2, Pallas kernels, attend(): pl.pallas_call(functools.partial(attend_kernel, plan), grid_spec=pltpu.Pr...  16.9 us
    ppermute x7, starting transfers between devices, across(): return lax.ppermute(array, 'seq', pairs)  13.7 us
    ppermute x6, waiting for transfers between devices, along(): return lax.ppermute(array, 'seq', pairs)  9.7 us
    ppermute x1, starting transfers between devices, shards(): got_a = lax.ppermute(sibling_a, 'tp', swap)  7.91 us
    dynamic_update_slice x2, local copies, waits for them, and re-layouts, shards(): lax.dynamic_update_slice_in_dim(out, got, (other * half + first) * group_...  1.66 us
    ppermute x2, starting transfers between devices, shards(): got = lax.ppermute(taken(other, first, count), 'tp', swap)  1.57 us
  transfers between devices with their start and end apart: 19, of which 6 were waited for; matrix products, arithmetic and copies ran while one was open for 4% of the time, Pallas kernels for 22%

profile of v3, /device:TPU:17, one launch (start us, length us, event | category | flops | bytes accessed | tf_op | source)
XLA Modules:
  0.0 77.6 jit_solution(8058728529941212883)
XLA Ops:
  0.0 1.1 %constant_dynamic-slice_fusion.2 = (bf16[128,256]{1,0:T(8,128)(2,1)S(1)}, bf16[128,256]{1,0:T(8,128)(2,1)S(1)}, bf16[128,256]{1,0:T(8,128)(2,1)S(1)}, bf16[128,2...) fusion(bf16[128,1024]{1,0:T(8,128)(2,1)} %param.9, ...), kind=kLoop, calls=%fused_computation.8 | loop fusion | bytes 1048592 | tf_op jit(solution)/shard_map/dynamic_slice | solution.py:211
  1.9 1.3 %constant_dynamic-slice_fusion.8 = bf16[128,4096]{1,0:T(8,128)(2,1)S(1)} fusion(bf16[128,8192]{1,0:T(8,128)(2,1)} %refs_0_.3, s32[]{:T(128)S(6)} %select_n.23), kind=kLoop, calls=%fused_computation.14 | loop fusion | bytes 2097156 | tf_op jit(solution)/shard_map/dynamic_slice | solution.py:219
  3.3 3.2 %collective-permute-start.10 = (bf16[256,512]{1,0:T(8,128)(2,1)S(1)}, bf16[256,512]{1,0:T(8,128)(2,1)S(1)}, u32[]{:S(2)}, u32[]{:S(2)}) collective-permute-start(bf16[256,512]{1,0:T(8,128)(2,1)S(1)} %pad_maximum_fusion.1.refs_2_), channel_id=1, source_target_pairs={{0,4},{2,6},{4,8},{6,10},{8,12},{10,14},{1,5},{3,7},{5,9},{7,11},{... | collective-permute-start | bytes 786440 | tf_op jit(solution)/shard_map/ppermute | solution.py:230
  6.6 0.8 %collective-permute-start.1 = (bf16[128,512]{1,0:T(8,128)(2,1)S(1)}, bf16[128,512]{1,0:T(8,128)(2,1)S(1)}, u32[]{:S(2)}, u32[]{:S(2)}) collective-permute-start(bf16[128,512]{1,0:T(8,128)(2,1)S(1)} %pad_maximum_fusion.2), channel_id=1, source_target_pairs={{0,1},{1,0},{2,3},{3,2},{4,5},{5,4},{6,7},{7,6},{8,9},{9,8},{10,11... | collective-permute-start | bytes 393224 | tf_op jit(solution)/shard_map/ppermute | solution.py:216
  7.4 5.2 %collective-permute-done.10.refs_3_ = bf16[256,512]{1,0:T(8,128)(2,1)S(1)} collective-permute-done((bf16[256,512]{1,0:T(8,128)(2,1)S(1)}, bf16[256,512]{1,0:T(8,128)(2,1)S(1)}, u32[]{:S(2)}, u32[]{:S(2)}) %collective-permute-start.10) | collective-permute-done | bytes 262176 | tf_op jit(solution)/shard_map/ppermute | solution.py:230
  12.6 3.2 %collective-permute-start.11 = (bf16[256,512]{1,0:T(8,128)(2,1)S(1)}, bf16[256,512]{1,0:T(8,128)(2,1)S(1)}, u32[]{:S(2)}, u32[]{:S(2)}) collective-permute-start(bf16[256,512]{1,0:T(8,128)(2,1)S(1)} %collective-permute-done.10.refs_3_), channel_id=1, source_target_pairs={{4,8},{6,10},{8,12},{10,14},{5,9},{7,11},{9,13},{11,15},{20,24},{2... | collective-permute-start | bytes 786440 | tf_op jit(solution)/shard_map/ppermute | solution.py:230
  15.9 1.9 %collective-permute-start.2 = (bf16[256,512]{1,0:T(8,128)(2,1)S(1)}, bf16[256,512]{1,0:T(8,128)(2,1)S(1)}, u32[]{:S(2)}, u32[]{:S(2)}) collective-permute-start(bf16[256,512]{1,0:T(8,128)(2,1)S(1)} %pad_maximum_fusion.refs_2_), channel_id=1, source_target_pairs={{0,4},{2,6},{4,8},{6,10},{8,12},{10,14},{1,5},{3,7},{5,9},{7,11},{... | collective-permute-start | bytes 786440 | tf_op jit(solution)/shard_map/ppermute | solution.py:230
  17.8 1.3 %collective-permute-start.5 = (bf16[256,512]{1,0:T(8,128)(2,1)S(1)}, bf16[256,512]{1,0:T(8,128)(2,1)S(1)}, u32[]{:S(2)}, u32[]{:S(2)}) collective-permute-start(bf16[256,512]{1,0:T(8,128)(2,1)S(1)} %pad_maximum_fusion.refs_2_), channel_id=1, source_target_pairs={{0,2},{2,0},{4,6},{6,4},{8,10},{10,8},{12,14},{14,12},{1,3},{3,1},... | collective-permute-start | bytes 786440 | tf_op jit(solution)/shard_map/ppermute | solution.py:238
  19.3 1.7 %collective-permute-done.11.refs_4_ = bf16[256,512]{1,0:T(8,128)(2,1)S(1)} collective-permute-done((bf16[256,512]{1,0:T(8,128)(2,1)S(1)}, bf16[256,512]{1,0:T(8,128)(2,1)S(1)}, u32[]{:S(2)}, u32[]{:S(2)}) %collective-permute-start.11) | collective-permute-done | bytes 262176 | tf_op jit(solution)/shard_map/ppermute | solution.py:230
  21.0 3.2 %collective-permute-start.12 = (bf16[256,512]{1,0:T(8,128)(2,1)S(1)}, bf16[256,512]{1,0:T(8,128)(2,1)S(1)}, u32[]{:S(2)}, u32[]{:S(2)}) collective-permute-start(bf16[256,512]{1,0:T(8,128)(2,1)S(1)} %collective-permute-done.11.refs_4_), channel_id=1, source_target_pairs={{8,12},{10,14},{9,13},{11,15},{24,28},{26,30},{25,29},{27,31}} | collective-permute-start | bytes 786440 | tf_op jit(solution)/shard_map/ppermute | solution.py:230
  24.2 2.4 %collective-permute-done.2.refs_3_ = bf16[256,512]{1,0:T(8,128)(2,1)S(1)} collective-permute-done((bf16[256,512]{1,0:T(8,128)(2,1)S(1)}, bf16[256,512]{1,0:T(8,128)(2,1)S(1)}, u32[]{:S(2)}, u32[]{:S(2)}) %collective-permute-start.2) | collective-permute-done | bytes 262176 | tf_op jit(solution)/shard_map/ppermute | solution.py:230
  26.6 3.2 %collective-permute-start.3 = (bf16[256,512]{1,0:T(8,128)(2,1)S(1)}, bf16[256,512]{1,0:T(8,128)(2,1)S(1)}, u32[]{:S(2)}, u32[]{:S(2)}) collective-permute-start(bf16[256,512]{1,0:T(8,128)(2,1)S(1)} %collective-permute-done.2.refs_3_), channel_id=1, source_target_pairs={{4,8},{6,10},{8,12},{10,14},{5,9},{7,11},{9,13},{11,15},{20,24},{2... | collective-permute-start | bytes 786440 | tf_op jit(solution)/shard_map/ppermute | solution.py:230
  29.9 3.1 %collective-permute-start.14 = (bf16[256,512]{1,0:T(8,128)(2,1)S(1)}, bf16[256,512]{1,0:T(8,128)(2,1)S(1)}, u32[]{:S(2)}, u32[]{:S(2)}) collective-permute-start(bf16[256,512]{1,0:T(8,128)(2,1)S(1)} %collective-permute-done.10.refs_3_), channel_id=1, source_target_pairs={{4,6},{6,4},{8,10},{10,8},{12,14},{14,12},{5,7},{7,5},{9,11},{11,9... | collective-permute-start | bytes 786440 | tf_op jit(solution)/shard_map/ppermute | solution.py:238
  33.0 2.1 %collective-permute-start.15 = (bf16[256,512]{1,0:T(8,128)(2,1)S(1)}, bf16[256,512]{1,0:T(8,128)(2,1)S(1)}, u32[]{:S(2)}, u32[]{:S(2)}) collective-permute-start(bf16[256,512]{1,0:T(8,128)(2,1)S(1)} %collective-permute-done.11.refs_4_), channel_id=1, source_target_pairs={{8,10},{10,8},{12,14},{14,12},{9,11},{11,9},{13,15},{15,13},{24,26... | collective-permute-start | bytes 786440 | tf_op jit(solution)/shard_map/ppermute | solution.py:238
  35.2 1.4 %collective-permute-start.16 = (bf16[256,512]{1,0:T(8,128)(2,1)S(1)}, bf16[256,512]{1,0:T(8,128)(2,1)}, u32[]{:S(2)}, u32[]{:S(2)}) collective-permute-start(bf16[256,512]{1,0:T(8,128)(2,1)S(1)} %collective-permute-done.12.refs_5_), channel_id=1, source_target_pairs={{12,14},{14,12},{13,15},{15,13},{28,30},{30,28},{29,31},{31,29}} | collective-permute-start | bytes 786440 | tf_op jit(solution)/shard_map/ppermute | solution.py:238
  37.0 3.1 %collective-permute-start.6 = (bf16[256,512]{1,0:T(8,128)(2,1)S(1)}, bf16[256,512]{1,0:T(8,128)(2,1)}, u32[]{:S(2)}, u32[]{:S(2)}) collective-permute-start(bf16[256,512]{1,0:T(8,128)(2,1)S(1)} %collective-permute-done.2.refs_3_), channel_id=1, source_target_pairs={{4,6},{6,4},{8,10},{10,8},{12,14},{14,12},{5,7},{7,5},{9,11},{11,9... | collective-permute-start | bytes 786440 | tf_op jit(solution)/shard_map/ppermute | solution.py:238
  40.1 1.4 %collective-permute-start.8 = (bf16[256,512]{1,0:T(8,128)(2,1)S(1)}, bf16[256,512]{1,0:T(8,128)(2,1)}, u32[]{:S(2)}, u32[]{:S(2)}) collective-permute-start(bf16[256,512]{1,0:T(8,128)(2,1)S(1)} %collective-permute-done.5.refs_6_), channel_id=1, source_target_pairs={{0,12},{2,14},{1,13},{3,15},{16,28},{18,30},{17,29},{19,31}} | collective-permute-start | bytes 786440 | tf_op jit(solution)/shard_map/ppermute | solution.py:249
  41.7 2.4 %collective-permute-start.7 = (bf16[256,512]{1,0:T(8,128)(2,1)S(1)}, bf16[256,512]{1,0:T(8,128)(2,1)}, u32[]{:S(2)}, u32[]{:S(2)}) collective-permute-start(bf16[256,512]{1,0:T(8,128)(2,1)S(1)} %collective-permute-done.3.refs_4_), channel_id=1, source_target_pairs={{8,10},{10,8},{12,14},{14,12},{9,11},{11,9},{13,15},{15,13},{24,26... | collective-permute-start | bytes 786440 | tf_op jit(solution)/shard_map/ppermute | solution.py:238
  44.1 4.3 %collective-permute-start.4 = (bf16[256,512]{1,0:T(8,128)(2,1)S(1)}, bf16[256,512]{1,0:T(8,128)(2,1)}, u32[]{:S(2)}, u32[]{:S(2)}) collective-permute-start(bf16[256,512]{1,0:T(8,128)(2,1)S(1)} %collective-permute-done.3.refs_4_), channel_id=1, source_target_pairs={{8,12},{10,14},{9,13},{11,15},{24,28},{26,30},{25,29},{27,31}} | collective-permute-start | bytes 786440 | tf_op jit(solution)/shard_map/ppermute | solution.py:230
  49.7 8.4 %attend.2 = (bf16[128,8192]{1,0:T(8,128)(2,1)}, bf16[128,2048]{1,0:T(8,128)(2,1)}) custom-call(s32[386]{0:T(512)} %concatenate.21.table, bf16[128,8192]{1,0:T(8,128)(2,1)} %refs_0_.3, bf16[128,4096]{1,0:T(8,128)(2,1)} %copy-done, bf16[256,512]{1,0:T(8,128)(2,1)} %copy-done.2, bf16[256,512]{1,0:T(8,128)(2,1)} %copy-done.4, bf16[256,512]{1,0:T(8,128)(2,1)} %copy-done.6, ...), custom_call_target="tpu_custom_call" | custom-call | tf_op jit(solution)/shard_map/attend/pallas_call | solution.py:165
  58.1 7.9 %collective-permute-start.17 = (bf16[128,2048]{1,0:T(8,128)(2,1)}, bf16[128,2048]{1,0:T(8,128)(2,1)S(1)}, u32[]{:S(2)}, u32[]{:S(2)}) collective-permute-start(bf16[128,2048]{1,0:T(8,128)(2,1)} %get-tuple-element.11), channel_id=1, source_target_pairs={{0,1},{1,0},{2,3},{3,2},{4,5},{5,4},{6,7},{7,6},{8,9},{9,8},{10,11... | collective-permute-start | bytes 1572872 | tf_op jit(solution)/shard_map/ppermute | solution.py:258
  66.1 8.5 %attend.3 = (bf16[128,8192]{1,0:T(8,128)(2,1)}, bf16[128,2048]{1,0:T(8,128)(2,1)}) custom-call(s32[386]{0:T(512)} %concatenate.21.table, bf16[128,8192]{1,0:T(8,128)(2,1)} %refs_0_.3, bf16[128,4096]{1,0:T(8,128)(2,1)} %copy-done, bf16[256,512]{1,0:T(8,128)(2,1)} %copy-done.1, bf16[256,512]{1,0:T(8,128)(2,1)} %copy-done.3, ...), custom_call_target="tpu_custom_call", output_to_operand_aliasing={{0}: (11, {})} | custom-call | tf_op jit(solution)/shard_map/attend/pallas_call | solution.py:165
  74.6 0.8 %constant_dynamic-update-slice_fusion.1 = bf16[128,8192]{1,0:T(8,128)(2,1)} fusion(bf16[128,8192]{1,0:T(8,128)(2,1)} %get-tuple-element.10, bf16[128,2048]{1,0:T(8,128)(2,1)S(1)} %collective-permute-done.17, s32[]{:T(128)S(6)} %select_n.23), kind=kLoop, calls=%fused_computation.5 | loop fusion | bytes 1048580 | tf_op jit(solution)/shard_map/dynamic_update_slice | solution.py:264
  75.5 1.3 %collective-permute-done.18 = bf16[128,2048]{1,0:T(8,128)(2,1)S(1)} collective-permute-done((bf16[128,2048]{1,0:T(8,128)(2,1)}, bf16[128,2048]{1,0:T(8,128)(2,1)S(1)}, u32[]{:S(2)}, u32[]{:S(2)}) %collective-permute-start.18) | collective-permute-done | bytes 524320 | tf_op jit(solution)/shard_map/ppermute | solution.py:262
  (61 shorter events, 3.9 us)
Async XLA Ops:
  1.1 47.3 %copy-start.12 = (s32[64,2]{0,1:T(2,128)S(1)}, s32[64,2]{0,1:T(2,128)}, u32[]{:S(2)}) copy-start(s32[64,2]{0,1:T(2,128)} %param.10) | copy-start | bytes 1540
  1.1 47.6 %copy-start.13 = (s32[64,2]{0,1:T(2,128)S(1)}, s32[64,2]{0,1:T(2,128)}, u32[]{:S(2)}) copy-start(s32[64,2]{0,1:T(2,128)} %param.12) | copy-start | bytes 1540
  1.1 47.8 %copy-start.14 = (s32[64]{0:T(128)S(1)}, s32[64]{0:T(128)}, u32[]{:S(2)}) copy-start(s32[64]{0:T(128)} %param.11) | copy-start | bytes 772
  1.1 47.8 %copy-start.15 = (s32[64]{0:T(128)S(1)}, s32[64]{0:T(128)}, u32[]{:S(2)}) copy-start(s32[64]{0:T(128)} %param.13) | copy-start | bytes 772
  1.2 2.1 %collective-permute-start.9 = (bf16[128,512]{1,0:T(8,128)(2,1)S(1)}, bf16[128,512]{1,0:T(8,128)(2,1)S(1)}, u32[]{:S(2)}, u32[]{:S(2)}) collective-permute-start(bf16[128,512]{1,0:T(8,128)(2,1)S(1)} %pad_maximum_fusion.3), channel_id=1, source_target_pairs={{0,1},{1,0},{2,3},{3,2},{4,5},{5,4},{6,7},{7,6},{8,9},{9,8},{10,11... | collective-permute-start | bytes 393224 | tf_op jit(solution)/shard_map/ppermute | solution.py:216
  3.2 40.9 %collective-permute-start = (bf16[128,4096]{1,0:T(8,128)(2,1)S(1)}, bf16[128,4096]{1,0:T(8,128)(2,1)S(1)}, u32[]{:S(2)}, u32[]{:S(2)}) collective-permute-start(bf16[128,4096]{1,0:T(8,128)(2,1)S(1)} %constant_dynamic-slice_fusion.8), channel_id=1, source_target_pairs={{0,1},{1,0},{2,3},{3,2},{4,5},{5,4},{6,7},{7,6},{8,9},{9,8},{10,11... | collective-permute-start | bytes 3145736 | tf_op jit(solution)/shard_map/ppermute | solution.py:218
  3.3 9.3 %collective-permute-start.10 = (bf16[256,512]{1,0:T(8,128)(2,1)S(1)}, bf16[256,512]{1,0:T(8,128)(2,1)S(1)}, u32[]{:S(2)}, u32[]{:S(2)}) collective-permute-start(bf16[256,512]{1,0:T(8,128)(2,1)S(1)} %pad_maximum_fusion.1.refs_2_), channel_id=1, source_target_pairs={{0,4},{2,6},{4,8},{6,10},{8,12},{10,14},{1,5},{3,7},{5,9},{7,11},{... | collective-permute-start | bytes 786440 | tf_op jit(solution)/shard_map/ppermute | solution.py:230
  6.6 9.2 %collective-permute-start.1 = (bf16[128,512]{1,0:T(8,128)(2,1)S(1)}, bf16[128,512]{1,0:T(8,128)(2,1)S(1)}, u32[]{:S(2)}, u32[]{:S(2)}) collective-permute-start(bf16[128,512]{1,0:T(8,128)(2,1)S(1)} %pad_maximum_fusion.2), channel_id=1, source_target_pairs={{0,1},{1,0},{2,3},{3,2},{4,5},{5,4},{6,7},{7,6},{8,9},{9,8},{10,11... | collective-permute-start | bytes 393224 | tf_op jit(solution)/shard_map/ppermute | solution.py:216
  12.6 8.4 %collective-permute-start.11 = (bf16[256,512]{1,0:T(8,128)(2,1)S(1)}, bf16[256,512]{1,0:T(8,128)(2,1)S(1)}, u32[]{:S(2)}, u32[]{:S(2)}) collective-permute-start(bf16[256,512]{1,0:T(8,128)(2,1)S(1)} %collective-permute-done.10.refs_3_), channel_id=1, source_target_pairs={{4,8},{6,10},{8,12},{10,14},{5,9},{7,11},{9,13},{11,15},{20,24},{2... | collective-permute-start | bytes 786440 | tf_op jit(solution)/shard_map/ppermute | solution.py:230
  15.8 50.2 %copy-start.1 = (bf16[256,512]{1,0:T(8,128)(2,1)}, bf16[256,512]{1,0:T(8,128)(2,1)S(1)}, u32[]{:S(2)}) copy-start(bf16[256,512]{1,0:T(8,128)(2,1)S(1)} %pad_maximum_fusion.refs_2_) | copy-start | bytes 786436
  15.9 10.8 %collective-permute-start.2 = (bf16[256,512]{1,0:T(8,128)(2,1)S(1)}, bf16[256,512]{1,0:T(8,128)(2,1)S(1)}, u32[]{:S(2)}, u32[]{:S(2)}) collective-permute-start(bf16[256,512]{1,0:T(8,128)(2,1)S(1)} %pad_maximum_fusion.refs_2_), channel_id=1, source_target_pairs={{0,4},{2,6},{4,8},{6,10},{8,12},{10,14},{1,5},{3,7},{5,9},{7,11},{... | collective-permute-start | bytes 786440 | tf_op jit(solution)/shard_map/ppermute | solution.py:230
  17.8 12.1 %collective-permute-start.5 = (bf16[256,512]{1,0:T(8,128)(2,1)S(1)}, bf16[256,512]{1,0:T(8,128)(2,1)S(1)}, u32[]{:S(2)}, u32[]{:S(2)}) collective-permute-start(bf16[256,512]{1,0:T(8,128)(2,1)S(1)} %pad_maximum_fusion.refs_2_), channel_id=1, source_target_pairs={{0,2},{2,0},{4,6},{6,4},{8,10},{10,8},{12,14},{14,12},{1,3},{3,1},... | collective-permute-start | bytes 786440 | tf_op jit(solution)/shard_map/ppermute | solution.py:238
  19.1 13.9 %collective-permute-start.13 = (bf16[256,512]{1,0:T(8,128)(2,1)S(1)}, bf16[256,512]{1,0:T(8,128)(2,1)S(1)}, u32[]{:S(2)}, u32[]{:S(2)}) collective-permute-start(bf16[256,512]{1,0:T(8,128)(2,1)S(1)} %pad_maximum_fusion.1.refs_2_), channel_id=1, source_target_pairs={{0,2},{2,0},{4,6},{6,4},{8,10},{10,8},{12,14},{14,12},{1,3},{3,1},... | collective-permute-start | bytes 786440 | tf_op jit(solution)/shard_map/ppermute | solution.py:238
  21.0 14.2 %collective-permute-start.12 = (bf16[256,512]{1,0:T(8,128)(2,1)S(1)}, bf16[256,512]{1,0:T(8,128)(2,1)S(1)}, u32[]{:S(2)}, u32[]{:S(2)}) collective-permute-start(bf16[256,512]{1,0:T(8,128)(2,1)S(1)} %collective-permute-done.11.refs_4_), channel_id=1, source_target_pairs={{8,12},{10,14},{9,13},{11,15},{24,28},{26,30},{25,29},{27,31}} | collective-permute-start | bytes 786440 | tf_op jit(solution)/shard_map/ppermute | solution.py:230
  26.6 10.3 %collective-permute-start.3 = (bf16[256,512]{1,0:T(8,128)(2,1)S(1)}, bf16[256,512]{1,0:T(8,128)(2,1)S(1)}, u32[]{:S(2)}, u32[]{:S(2)}) collective-permute-start(bf16[256,512]{1,0:T(8,128)(2,1)S(1)} %collective-permute-done.2.refs_3_), channel_id=1, source_target_pairs={{4,8},{6,10},{8,12},{10,14},{5,9},{7,11},{9,13},{11,15},{20,24},{2... | collective-permute-start | bytes 786440 | tf_op jit(solution)/shard_map/ppermute | solution.py:230
  29.9 10.3 %collective-permute-start.14 = (bf16[256,512]{1,0:T(8,128)(2,1)S(1)}, bf16[256,512]{1,0:T(8,128)(2,1)S(1)}, u32[]{:S(2)}, u32[]{:S(2)}) collective-permute-start(bf16[256,512]{1,0:T(8,128)(2,1)S(1)} %collective-permute-done.10.refs_3_), channel_id=1, source_target_pairs={{4,6},{6,4},{8,10},{10,8},{12,14},{14,12},{5,7},{7,5},{9,11},{11,9... | collective-permute-start | bytes 786440 | tf_op jit(solution)/shard_map/ppermute | solution.py:238
  33.0 8.7 %collective-permute-start.15 = (bf16[256,512]{1,0:T(8,128)(2,1)S(1)}, bf16[256,512]{1,0:T(8,128)(2,1)S(1)}, u32[]{:S(2)}, u32[]{:S(2)}) collective-permute-start(bf16[256,512]{1,0:T(8,128)(2,1)S(1)} %collective-permute-done.11.refs_4_), channel_id=1, source_target_pairs={{8,10},{10,8},{12,14},{14,12},{9,11},{11,9},{13,15},{15,13},{24,26... | collective-permute-start | bytes 786440 | tf_op jit(solution)/shard_map/ppermute | solution.py:238
  35.2 14.4 %collective-permute-start.16 = (bf16[256,512]{1,0:T(8,128)(2,1)S(1)}, bf16[256,512]{1,0:T(8,128)(2,1)}, u32[]{:S(2)}, u32[]{:S(2)}) collective-permute-start(bf16[256,512]{1,0:T(8,128)(2,1)S(1)} %collective-permute-done.12.refs_5_), channel_id=1, source_target_pairs={{12,14},{14,12},{13,15},{15,13},{28,30},{30,28},{29,31},{31,29}} | collective-permute-start | bytes 786440 | tf_op jit(solution)/shard_map/ppermute | solution.py:238
  37.0 29.1 %collective-permute-start.6 = (bf16[256,512]{1,0:T(8,128)(2,1)S(1)}, bf16[256,512]{1,0:T(8,128)(2,1)}, u32[]{:S(2)}, u32[]{:S(2)}) collective-permute-start(bf16[256,512]{1,0:T(8,128)(2,1)S(1)} %collective-permute-done.2.refs_3_), channel_id=1, source_target_pairs={{4,6},{6,4},{8,10},{10,8},{12,14},{14,12},{5,7},{7,5},{9,11},{11,9... | collective-permute-start | bytes 786440 | tf_op jit(solution)/shard_map/ppermute | solution.py:238
  40.1 25.9 %collective-permute-start.8 = (bf16[256,512]{1,0:T(8,128)(2,1)S(1)}, bf16[256,512]{1,0:T(8,128)(2,1)}, u32[]{:S(2)}, u32[]{:S(2)}) collective-permute-start(bf16[256,512]{1,0:T(8,128)(2,1)S(1)} %collective-permute-done.5.refs_6_), channel_id=1, source_target_pairs={{0,12},{2,14},{1,13},{3,15},{16,28},{18,30},{17,29},{19,31}} | collective-permute-start | bytes 786440 | tf_op jit(solution)/shard_map/ppermute | solution.py:249
  41.7 24.3 %collective-permute-start.7 = (bf16[256,512]{1,0:T(8,128)(2,1)S(1)}, bf16[256,512]{1,0:T(8,128)(2,1)}, u32[]{:S(2)}, u32[]{:S(2)}) collective-permute-start(bf16[256,512]{1,0:T(8,128)(2,1)S(1)} %collective-permute-done.3.refs_4_), channel_id=1, source_target_pairs={{8,10},{10,8},{12,14},{14,12},{9,11},{11,9},{13,15},{15,13},{24,26... | collective-permute-start | bytes 786440 | tf_op jit(solution)/shard_map/ppermute | solution.py:238
  44.1 21.9 %collective-permute-start.4 = (bf16[256,512]{1,0:T(8,128)(2,1)S(1)}, bf16[256,512]{1,0:T(8,128)(2,1)}, u32[]{:S(2)}, u32[]{:S(2)}) collective-permute-start(bf16[256,512]{1,0:T(8,128)(2,1)S(1)} %collective-permute-done.3.refs_4_), channel_id=1, source_target_pairs={{8,12},{10,14},{9,13},{11,15},{24,28},{26,30},{25,29},{27,31}} | collective-permute-start | bytes 786440 | tf_op jit(solution)/shard_map/ppermute | solution.py:230
  58.1 16.5 %collective-permute-start.17 = (bf16[128,2048]{1,0:T(8,128)(2,1)}, bf16[128,2048]{1,0:T(8,128)(2,1)S(1)}, u32[]{:S(2)}, u32[]{:S(2)}) collective-permute-start(bf16[128,2048]{1,0:T(8,128)(2,1)} %get-tuple-element.11), channel_id=1, source_target_pairs={{0,1},{1,0},{2,3},{3,2},{4,5},{5,4},{6,7},{7,6},{8,9},{9,8},{10,11... | collective-permute-start | bytes 1572872 | tf_op jit(solution)/shard_map/ppermute | solution.py:258
  74.5 2.2 %collective-permute-start.18 = (bf16[128,2048]{1,0:T(8,128)(2,1)}, bf16[128,2048]{1,0:T(8,128)(2,1)S(1)}, u32[]{:S(2)}, u32[]{:S(2)}) collective-permute-start(bf16[128,2048]{1,0:T(8,128)(2,1)} %get-tuple-element.12), channel_id=1, source_target_pairs={{0,1},{1,0},{2,3},{3,2},{4,5},{5,4},{6,7},{7,6},{8,9},{9,8},{10,11... | collective-permute-start | bytes 1572872 | tf_op jit(solution)/shard_map/ppermute | solution.py:262
  (11 other events, 259.7 us)

commit v4 on v3

--- a/solution.py
+++ b/solution.py
@@ -16,12 +16,11 @@
 
 
 def attend_kernel(plan, table, *refs):
-    relay, columns, cores, kv_first, kv_heads, own, sibling, slots, copies, offsets, widths, aliased = plan
+    relay, columns, cores, kv_first, kv_heads, own, sibling, slots, offsets, widths, aliased = plan
     refs = list(refs)
     own_queries = refs.pop(0) if own else None
     sibling_queries = refs.pop(0) if sibling else None
     pieces = [refs.pop(0) for _ in slots]
-    copied = [refs.pop(0) for _ in copies]
     if aliased:
         refs.pop(0)
     out = refs.pop(0) if own else None
@@ -48,12 +47,6 @@
         moves.append(pltpu.make_async_copy(sibling_queries.at[:, lanes], sibling_held, sems.at[len(slots) + 1]))
     for move in moves:
         move.start()
-    placed = []
-    for at, (ref, first) in enumerate(zip(copied, copies)):
-        lanes = pl.ds(pl.multiple_of((other * half + first) * width, width), ref.shape[1])
-        placed.append(pltpu.make_async_copy(ref, out.at[:, lanes], sems.at[len(slots) + 2 + at]))
-    for move in placed:
-        move.start()
     for move in moves:
         move.wait()
 
@@ -71,41 +64,20 @@
             slot = chip
         return (slot * cores + jnp.bitwise_xor(block % cores, core)) * MASK_BLOCK_SIZE
 
-    def unit(queries, block, diagonal_row, head, kv):
-        rows = [diagonal_row]
-        active = [None]
-        verticals = []
-        for entry in range(vertical_width):
-            vertical = table[vertical_at + head * vertical_width + entry]
-            live = entry < table[vertical_count_at + head]
-            verticals.append((vertical, live))
-            use = live & (vertical < block)
-            rows.append(row_of(jnp.where(use, vertical, block)))
-            active.append(use)
-        for entry in range(slash_width):
-            target = block - table[slash_at + head * slash_width + entry]
-            use = (entry < table[slash_count_at + head]) & (target >= 0)
-            for vertical, live in verticals:
-                use = use & jnp.logical_not(live & (vertical == target))
-            rows.append(row_of(jnp.where(use, target, block)))
-            active.append(use)
-        rows = [pl.ds(pl.multiple_of(row, MASK_BLOCK_SIZE), MASK_BLOCK_SIZE) for row in rows]
-        key_lanes = pl.ds(pl.multiple_of(kv * HEAD_SIZE, HEAD_SIZE), HEAD_SIZE)
-        value_lanes = pl.ds(pl.multiple_of((kv_heads + kv) * HEAD_SIZE, HEAD_SIZE), HEAD_SIZE)
-        keys = jnp.concatenate([rows_held[row, key_lanes] for row in rows], axis=0)
-        values = jnp.concatenate(
-            [jnp.concatenate([rows_held[row, value_lanes], ones], axis=1) for row in rows], axis=0
+    def tile_rows(row):
+        return pl.ds(pl.multiple_of(row, MASK_BLOCK_SIZE), MASK_BLOCK_SIZE)
+
+    def product(left, rights):
+        return lax.dot_general(
+            left, jnp.concatenate(rights, axis=0), (((1,), (1,)), ((), ())), preferred_element_type=jnp.float32
         )
-        scores = lax.dot_general(queries, keys, (((1,), (1,)), ((), ())), preferred_element_type=jnp.float32)
-        tiles = []
-        for index, use in enumerate(active):
-            tile = scores[:, index * MASK_BLOCK_SIZE : (index + 1) * MASK_BLOCK_SIZE]
-            tiles.append(jnp.where(causal if use is None else use, tile, -jnp.inf))
-        peak = functools.reduce(jnp.maximum, tiles)
-        peak = jnp.max(peak, axis=1, keepdims=True)
-        weights = [jnp.exp2((tile - peak) * factor).astype(jnp.bfloat16) for tile in tiles]
-        sums = jnp.dot(jnp.concatenate(weights, axis=1), values, preferred_element_type=jnp.float32)
-        return (sums[:, :HEAD_SIZE] / sums[:, HEAD_SIZE:]).astype(jnp.bfloat16)
+
+    def weighted(weights, rights):
+        right = jnp.concatenate([jnp.concatenate([value, ones], axis=1) for value in rights], axis=0)
+        return jnp.dot(weights, right, preferred_element_type=jnp.float32)
+
+    def part(array, index, axis):
+        return lax.slice_in_dim(array, index * MASK_BLOCK_SIZE, (index + 1) * MASK_BLOCK_SIZE, axis=axis)
 
     def results(kv):
         lanes = pl.ds(pl.multiple_of(kv * width, width), width)
@@ -118,37 +90,85 @@
         return made
 
     def of_head(kv, carry):
+        key_lanes = pl.ds(pl.multiple_of(kv * HEAD_SIZE, HEAD_SIZE), HEAD_SIZE)
+        value_lanes = pl.ds(pl.multiple_of((kv_heads + kv) * HEAD_SIZE, HEAD_SIZE), HEAD_SIZE)
+        sides = []
+        if own:
+            sides.append((own_held, own_made, rank * cores + core, own_row))
+        if sibling:
+            sides.append((sibling_held, sibling_made, rank * cores + other, own_row + MASK_BLOCK_SIZE))
+
+        def lanes_of(slot):
+            return pl.ds(pl.multiple_of(kv * width + slot * HEAD_SIZE, HEAD_SIZE), HEAD_SIZE)
+
+        def key(row):
+            return rows_held[tile_rows(row), key_lanes]
+
+        def value(row):
+            return rows_held[tile_rows(row), value_lanes]
+
+        diagonal = [
+            product(jnp.concatenate([held[:, lanes_of(slot)] for slot in range(GROUP)], axis=0), [key(row)])
+            for held, _, _, row in sides
+        ]
+        pending = []
         for slot in range(GROUP):
             head = (core * half + kv_first + kv) * GROUP + slot
-            lanes = pl.ds(pl.multiple_of(kv * width + slot * HEAD_SIZE, HEAD_SIZE), HEAD_SIZE)
-            if own:
-                own_made[:, lanes] = unit(own_held[:, lanes], rank * cores + core, own_row, head, kv)
-            if sibling:
-                sibling_made[:, lanes] = unit(
-                    sibling_held[:, lanes], rank * cores + other, own_row + MASK_BLOCK_SIZE, head, kv
-                )
-        for move in results(kv):
-            move.start()
+            queries = [held[:, lanes_of(slot)] for held, _, _, _ in sides]
+            verticals = []
+            for entry in range(vertical_width):
+                vertical = table[vertical_at + head * vertical_width + entry]
+                live = entry < table[vertical_count_at + head]
+                verticals.append((vertical, live, row_of(jnp.minimum(vertical, rank * cores))))
+            vertical_scores = product(jnp.concatenate(queries, axis=0), [key(row) for _, _, row in verticals])
+            made = []
+            for side, (_, _, block, diagonal_row) in enumerate(sides):
+                slashes = []
+                for entry in range(slash_width):
+                    target = block - table[slash_at + head * slash_width + entry]
+                    use = (entry < table[slash_count_at + head]) & (target >= 0)
+                    for vertical, live, _ in verticals:
+                        use = use & jnp.logical_not(live & (vertical == target))
+                    slashes.append((use, row_of(jnp.where(use, target, block))))
+                slash_scores = product(queries[side], [key(row) for _, row in slashes])
+                tiles = [jnp.where(causal, part(diagonal[side], slot, 0), -jnp.inf)]
+                across = part(vertical_scores, side, 0)
+                for index, (vertical, live, _) in enumerate(verticals):
+                    tiles.append(jnp.where(live & (vertical < block), part(across, index, 1), -jnp.inf))
+                for index, (use, _) in enumerate(slashes):
+                    tiles.append(jnp.where(use, part(slash_scores, index, 1), -jnp.inf))
+                peak = jnp.max(functools.reduce(jnp.maximum, tiles), axis=1, keepdims=True)
+                weights = [jnp.exp2((tile - peak) * factor).astype(jnp.bfloat16) for tile in tiles]
+                last = 1 + len(verticals)
+                total = weighted(jnp.concatenate(weights[last:], axis=1), [value(row) for _, row in slashes])
+                made.append((weights[0], jnp.concatenate(weights[1:last], axis=1), total))
+            vertical_sums = weighted(
+                jnp.concatenate([one[1] for one in made], axis=0), [value(row) for _, _, row in verticals]
+            )
+            pending.append([(one[0], one[2] + part(vertical_sums, side, 0)) for side, one in enumerate(made)])
+        for side, (_, to, _, diagonal_row) in enumerate(sides):
+            sums = weighted(jnp.concatenate([one[side][0] for one in pending], axis=0), [value(diagonal_row)])
+            for slot in range(GROUP):
+                whole = part(sums, slot, 0) + pending[slot][side][1]
+                to[:, lanes_of(slot)] = (whole[:, :HEAD_SIZE] / whole[:, HEAD_SIZE:]).astype(jnp.bfloat16)
+            results(kv)[side].start()
         return carry
 
     lax.fori_loop(0, kv_heads, of_head, 0)
     for kv in range(kv_heads):
         for move in results(kv):
             move.wait()
-    for move in placed:
-        move.wait()
-
-
-def attend(table, common, kv_first, kv_heads, queries, sibling_queries, pieces, slots, copies=(), into=None):
+
+
+def attend(table, common, kv_first, kv_heads, queries, sibling_queries, pieces, slots, into=None):
     relay, columns, cores, offsets, widths = common
     own, sibling = queries is not None, sibling_queries is not None
     some = queries if own else sibling_queries
     tokens = some.shape[0]
     width = kv_heads * GROUP * HEAD_SIZE
-    plan = (relay, columns, cores, kv_first, kv_heads, own, sibling, tuple(slots), tuple(first for _, first in copies))
-    plan += (offsets, widths, into is not None)
+    plan = (relay, columns, cores, kv_first, kv_heads, own, sibling, tuple(slots), offsets, widths, into is not None)
     operands = [array for array in (queries, sibling_queries) if array is not None]
-    operands += list(pieces) + [array for array, _ in copies]
+    operands += list(pieces)
     aliases = {}
     if into is not None:
         aliases = {1 + len(operands): 0}
@@ -173,7 +193,7 @@
             + [held if own else small] * 2
             + [held if sibling else small] * 2
             + [
-                pltpu.SemaphoreType.DMA((len(pieces) + 2 + max(1, len(copies)),)),
+                pltpu.SemaphoreType.DMA((len(pieces) + 2,)),
                 pltpu.SemaphoreType.DMA((kv_heads, 2)),
             ],
         ),
@@ -213,6 +233,8 @@
 
     local = []
     for (first, count) in chunks:
+        if local:
+            keys, values, _ = lax.optimization_barrier((keys, values, local[0]))
         got = lax.ppermute(taken(other, first, count), "tp", swap)
         local.append(jnp.concatenate([taken(core, first, count), got], axis=0))
     sibling_queries = lax.ppermute(

time: 78.1 us -> 73.1 us (0.936)
  the two profiles are of different devices: /device:TPU:17 before, /device:TPU:0 now
where the time goes in v4:
time: 73.1 us; the launch traced here: 72.6 us
  starting transfers between devices  41 us (56%)
  Pallas kernels  16.2 us (22%)
  waiting for transfers between devices  9.11 us (12%)
  local copies, waits for them, and re-layouts  5.92 us (8%)
    ppermute x6, starting transfers between devices, along(): return lax.ppermute(array, 'seq', pairs)  16.3 us
    pallas_call x2, Pallas kernels, attend(): pl.pallas_call(functools.partial(attend_kernel, plan), grid_spec=pltpu.Pr...  16.2 us
    ppermute x1, starting transfers between devices, shards(): cross_pieces.append(lax.ppermute(cross_pieces[0], 'seq', pairs))  15.8 us
    ppermute x7, starting transfers between devices, across(): return lax.ppermute(array, 'seq', pairs)  7.57 us
    ppermute x6, waiting for transfers between devices, along(): return lax.ppermute(array, 'seq', pairs)  7.23 us
    dynamic_update_slice x2, local copies, waits for them, and re-layouts, shards(): lax.dynamic_update_slice_in_dim(out, got, (other * half + first) * group_...  1.65 us
  transfers between devices with their start and end apart: 19, of which 4 were waited for; matrix products, arithmetic and copies ran while one was open for 5% of the time, Pallas kernels for 22%

profile of v4, /device:TPU:0, one launch (start us, length us, event | category | flops | bytes accessed | tf_op | source)
XLA Modules:
  0.0 72.6 jit_solution(415283242562489626)
XLA Ops:
  0.0 1.0 %constant_dynamic-slice_fusion.6 = (bf16[128,256]{1,0:T(8,128)(2,1)S(1)}, bf16[128,256]{1,0:T(8,128)(2,1)S(1)}, bf16[128,256]{1,0:T(8,128)(2,1)S(1)}, bf16[128,256]{1,0:T(8,128)(2,1)S(1)}) fusion(bf16[128,1024]{1,0:T(8,128)(2,1)} %param.9, s32[]{:T(128)S(6)} %select_n.24, s32[]{:T(128)S(6)} %select_n.25, bf16[128,1024]{1,0:T(8,128)(2,1)} %param.8), kind=kLoop, calls=%fused_computation.12 | loop fusion | bytes 524296 | tf_op jit(solution)/shard_map/dynamic_slice | solution.py:231
  1.6 1.3 %constant_dynamic-slice_fusion.8 = bf16[128,4096]{1,0:T(8,128)(2,1)S(1)} fusion(bf16[128,8192]{1,0:T(8,128)(2,1)} %refs_0_.3, s32[]{:T(128)S(6)} %select_n.23), kind=kLoop, calls=%fused_computation.14 | loop fusion | bytes 2097156 | tf_op jit(solution)/shard_map/dynamic_slice | solution.py:241
  3.1 5.0 %collective-permute-start.10 = (bf16[256,512]{1,0:T(8,128)(2,1)S(1)}, bf16[256,512]{1,0:T(8,128)(2,1)S(1)}, u32[]{:S(2)}, u32[]{:S(2)}) collective-permute-start(bf16[256,512]{1,0:T(8,128)(2,1)S(1)} %pad_maximum_fusion.refs_2_), channel_id=1, source_target_pairs={{0,4},{2,6},{4,8},{6,10},{8,12},{10,14},{1,5},{3,7},{5,9},{7,11},{... | collective-permute-start | bytes 786440 | tf_op jit(solution)/shard_map/ppermute | solution.py:252
  8.2 5.5 %collective-permute-done.10.refs_3_ = bf16[256,512]{1,0:T(8,128)(2,1)S(1)} collective-permute-done((bf16[256,512]{1,0:T(8,128)(2,1)S(1)}, bf16[256,512]{1,0:T(8,128)(2,1)S(1)}, u32[]{:S(2)}, u32[]{:S(2)}) %collective-permute-start.10) | collective-permute-done | bytes 262176 | tf_op jit(solution)/shard_map/ppermute | solution.py:252
  14.4 1.6 %collective-permute-start.13 = (bf16[256,512]{1,0:T(8,128)(2,1)S(1)}, bf16[256,512]{1,0:T(8,128)(2,1)S(1)}, u32[]{:S(2)}, u32[]{:S(2)}) collective-permute-start(bf16[256,512]{1,0:T(8,128)(2,1)S(1)} %pad_maximum_fusion.refs_2_), channel_id=1, source_target_pairs={{0,2},{2,0},{4,6},{6,4},{8,10},{10,8},{12,14},{14,12},{1,3},{3,1},... | collective-permute-start | bytes 786440 | tf_op jit(solution)/shard_map/ppermute | solution.py:260
  16.1 7.2 %collective-permute-start.3 = (bf16[256,512]{1,0:T(8,128)(2,1)S(1)}, bf16[256,512]{1,0:T(8,128)(2,1)S(1)}, u32[]{:S(2)}, u32[]{:S(2)}) collective-permute-start(bf16[256,512]{1,0:T(8,128)(2,1)S(1)} %pad_maximum_fusion.1.refs_2_), channel_id=1, source_target_pairs={{0,4},{2,6},{4,8},{6,10},{8,12},{10,14},{1,5},{3,7},{5,9},{7,11},{... | collective-permute-start | bytes 786440 | tf_op jit(solution)/shard_map/ppermute | solution.py:252
  23.9 1.4 %collective-permute-start.12 = (bf16[256,512]{1,0:T(8,128)(2,1)S(1)}, bf16[256,512]{1,0:T(8,128)(2,1)}, u32[]{:S(2)}, u32[]{:S(2)}) collective-permute-start(bf16[256,512]{1,0:T(8,128)(2,1)S(1)} %collective-permute-done.11.refs_4_), channel_id=1, source_target_pairs={{8,12},{10,14},{9,13},{11,15},{24,28},{26,30},{25,29},{27,31}} | collective-permute-start | bytes 786440 | tf_op jit(solution)/shard_map/ppermute | solution.py:252
  25.3 0.7 collective-permute-start.14
  25.9 1.7 %collective-permute-done.3.refs_3_ = bf16[256,512]{1,0:T(8,128)(2,1)S(1)} collective-permute-done((bf16[256,512]{1,0:T(8,128)(2,1)S(1)}, bf16[256,512]{1,0:T(8,128)(2,1)S(1)}, u32[]{:S(2)}, u32[]{:S(2)}) %collective-permute-start.3) | collective-permute-done | bytes 262176 | tf_op jit(solution)/shard_map/ppermute | solution.py:252
  27.6 1.4 %collective-permute-start.4 = (bf16[256,512]{1,0:T(8,128)(2,1)S(1)}, bf16[256,512]{1,0:T(8,128)(2,1)}, u32[]{:S(2)}, u32[]{:S(2)}) collective-permute-start(bf16[256,512]{1,0:T(8,128)(2,1)S(1)} %collective-permute-done.3.refs_3_), channel_id=1, source_target_pairs={{4,8},{6,10},{8,12},{10,14},{5,9},{7,11},{9,13},{11,15},{20,24},{2... | collective-permute-start | bytes 786440 | tf_op jit(solution)/shard_map/ppermute | solution.py:252
  29.0 0.9 %collective-permute-done.6.refs_6_ = bf16[256,512]{1,0:T(8,128)(2,1)S(1)} collective-permute-done((bf16[256,512]{1,0:T(8,128)(2,1)S(1)}, bf16[256,512]{1,0:T(8,128)(2,1)S(1)}, u32[]{:S(2)}, u32[]{:S(2)}) %collective-permute-start.6) | collective-permute-done | bytes 262176 | tf_op jit(solution)/shard_map/ppermute | solution.py:260
  29.9 0.7 collective-permute-start.15
  30.6 1.4 %collective-permute-start.16 = (bf16[256,512]{1,0:T(8,128)(2,1)}, bf16[256,512]{1,0:T(8,128)(2,1)}, u32[]{:S(2)}, u32[]{:S(2)}) collective-permute-start(bf16[256,512]{1,0:T(8,128)(2,1)} %collective-permute-done.12.refs_5_), channel_id=1, source_target_pairs={{12,14},{14,12},{13,15},{15,13},{28,30},{30,28},{29,31},{31,29}} | collective-permute-start | bytes 786440 | tf_op jit(solution)/shard_map/ppermute | solution.py:260
  32.0 1.3 %collective-permute-start.7 = (bf16[256,512]{1,0:T(8,128)(2,1)S(1)}, bf16[256,512]{1,0:T(8,128)(2,1)}, u32[]{:S(2)}, u32[]{:S(2)}) collective-permute-start(bf16[256,512]{1,0:T(8,128)(2,1)S(1)} %collective-permute-done.3.refs_3_), channel_id=1, source_target_pairs={{4,6},{6,4},{8,10},{10,8},{12,14},{14,12},{5,7},{7,5},{9,11},{11,9... | collective-permute-start | bytes 786440 | tf_op jit(solution)/shard_map/ppermute | solution.py:260
  33.3 15.8 %collective-permute-start.9 = (bf16[256,512]{1,0:T(8,128)(2,1)S(1)}, bf16[256,512]{1,0:T(8,128)(2,1)}, u32[]{:S(2)}, u32[]{:S(2)}) collective-permute-start(bf16[256,512]{1,0:T(8,128)(2,1)S(1)} %collective-permute-done.6.refs_6_), channel_id=1, source_target_pairs={{0,12},{2,14},{1,13},{3,15},{16,28},{18,30},{17,29},{19,31}} | collective-permute-start | bytes 786440 | tf_op jit(solution)/shard_map/ppermute | solution.py:271
  49.2 1.4 %collective-permute-start.8 = (bf16[256,512]{1,0:T(8,128)(2,1)}, bf16[256,512]{1,0:T(8,128)(2,1)}, u32[]{:S(2)}, u32[]{:S(2)}) collective-permute-start(bf16[256,512]{1,0:T(8,128)(2,1)} %collective-permute-done.4.refs_4_), channel_id=1, source_target_pairs={{8,10},{10,8},{12,14},{14,12},{9,11},{11,9},{13,15},{15,13},{24,26... | collective-permute-start | bytes 786440 | tf_op jit(solution)/shard_map/ppermute | solution.py:260
  50.6 0.7 collective-permute-start.5
  51.8 0.7 concatenate.21.table
  52.5 8.1 %attend.2 = (bf16[128,8192]{1,0:T(8,128)(2,1)}, bf16[128,2048]{1,0:T(8,128)(2,1)}) custom-call(s32[386]{0:T(512)} %concatenate.21.table, bf16[128,8192]{1,0:T(8,128)(2,1)} %refs_0_.3, bf16[128,4096]{1,0:T(8,128)(2,1)} %copy-done, bf16[256,512]{1,0:T(8,128)(2,1)} %copy-done.1, bf16[256,512]{1,0:T(8,128)(2,1)} %copy-done.3, bf16[256,512]{1,0:T(8,128)(2,1)} %copy-done.6, ...), custom_call_target="tpu_custom_call" | custom-call | tf_op jit(solution)/shard_map/attend/pallas_call | solution.py:185
  60.7 0.7 copy-done.10
  61.4 8.1 %attend.3 = (bf16[128,8192]{1,0:T(8,128)(2,1)}, bf16[128,2048]{1,0:T(8,128)(2,1)}) custom-call(s32[386]{0:T(512)} %concatenate.21.table, bf16[128,8192]{1,0:T(8,128)(2,1)} %refs_0_.3, bf16[128,4096]{1,0:T(8,128)(2,1)} %copy-done, bf16[256,512]{1,0:T(8,128)(2,1)} %copy-done.2, bf16[256,512]{1,0:T(8,128)(2,1)} %copy-done.4, ...), custom_call_target="tpu_custom_call", output_to_operand_aliasing={{0}: (11, {})} | custom-call | tf_op jit(solution)/shard_map/attend/pallas_call | solution.py:185
  70.1 0.8 %constant_dynamic-update-slice_fusion.1 = bf16[128,8192]{1,0:T(8,128)(2,1)} fusion(bf16[128,8192]{1,0:T(8,128)(2,1)} %get-tuple-element.14, bf16[128,2048]{1,0:T(8,128)(2,1)S(1)} %collective-permute-done.17, s32[]{:T(128)S(6)} %select_n.23), kind=kLoop, calls=%fused_computation.5 | loop fusion | bytes 1048580 | tf_op jit(solution)/shard_map/dynamic_update_slice | solution.py:286
  70.9 0.9 %collective-permute-done.18 = bf16[128,2048]{1,0:T(8,128)(2,1)S(1)} collective-permute-done((bf16[128,2048]{1,0:T(8,128)(2,1)}, bf16[128,2048]{1,0:T(8,128)(2,1)S(1)}, u32[]{:S(2)}, u32[]{:S(2)}) %collective-permute-start.18) | collective-permute-done | bytes 524320 | tf_op jit(solution)/shard_map/ppermute | solution.py:284
  71.8 0.8 %constant_dynamic-update-slice_fusion = bf16[128,8192]{1,0:T(8,128)(2,1)} fusion(bf16[128,8192]{1,0:T(8,128)(2,1)} %constant_dynamic-update-slice_fusion.1, bf16[128,2048]{1,0:T(8,128)(2,1)S(1)} %collective-permute-done.18, s32[]{:T(128)S(6)} %select_n.28), kind=kLoop, calls=%fused_computation.4 | loop fusion | bytes 1048580 | tf_op jit(solution)/shard_map/dynamic_update_slice | solution.py:286
  (65 shorter events, 3.3 us)
Async XLA Ops:
  1.0 50.2 %copy-start.13 = (s32[64,2]{0,1:T(2,128)S(1)}, s32[64,2]{0,1:T(2,128)}, u32[]{:S(2)}) copy-start(s32[64,2]{0,1:T(2,128)} %param.10) | copy-start | bytes 1540
  1.0 50.5 %copy-start.14 = (s32[64,2]{0,1:T(2,128)S(1)}, s32[64,2]{0,1:T(2,128)}, u32[]{:S(2)}) copy-start(s32[64,2]{0,1:T(2,128)} %param.12) | copy-start | bytes 1540
  1.1 50.7 %copy-start.15 = (s32[64]{0:T(128)S(1)}, s32[64]{0:T(128)}, u32[]{:S(2)}) copy-start(s32[64]{0:T(128)} %param.11) | copy-start | bytes 772
  1.1 50.7 %copy-start.16 = (s32[64]{0:T(128)S(1)}, s32[64]{0:T(128)}, u32[]{:S(2)}) copy-start(s32[64]{0:T(128)} %param.13) | copy-start | bytes 772
  1.1 1.9 %collective-permute-start.1 = (bf16[128,512]{1,0:T(8,128)(2,1)S(1)}, bf16[128,512]{1,0:T(8,128)(2,1)S(1)}, u32[]{:S(2)}, u32[]{:S(2)}) collective-permute-start(bf16[128,512]{1,0:T(8,128)(2,1)S(1)} %pad_maximum_fusion.2), channel_id=1, source_target_pairs={{0,1},{1,0},{2,3},{3,2},{4,5},{5,4},{6,7},{7,6},{8,9},{9,8},{10,11... | collective-permute-start | bytes 393224 | tf_op jit(solution)/shard_map/ppermute | solution.py:238
  2.9 47.6 %collective-permute-start = (bf16[128,4096]{1,0:T(8,128)(2,1)S(1)}, bf16[128,4096]{1,0:T(8,128)(2,1)S(1)}, u32[]{:S(2)}, u32[]{:S(2)}) collective-permute-start(bf16[128,4096]{1,0:T(8,128)(2,1)S(1)} %constant_dynamic-slice_fusion.8), channel_id=1, source_target_pairs={{0,1},{1,0},{2,3},{3,2},{4,5},{5,4},{6,7},{7,6},{8,9},{9,8},{10,11... | collective-permute-start | bytes 3145736 | tf_op jit(solution)/shard_map/ppermute | solution.py:240
  3.1 49.4 %copy-start.1 = (bf16[256,512]{1,0:T(8,128)(2,1)}, bf16[256,512]{1,0:T(8,128)(2,1)S(1)}, u32[]{:S(2)}) copy-start(bf16[256,512]{1,0:T(8,128)(2,1)S(1)} %pad_maximum_fusion.refs_2_) | copy-start | bytes 786436
  3.1 10.7 %collective-permute-start.10 = (bf16[256,512]{1,0:T(8,128)(2,1)S(1)}, bf16[256,512]{1,0:T(8,128)(2,1)S(1)}, u32[]{:S(2)}, u32[]{:S(2)}) collective-permute-start(bf16[256,512]{1,0:T(8,128)(2,1)S(1)} %pad_maximum_fusion.refs_2_), channel_id=1, source_target_pairs={{0,4},{2,6},{4,8},{6,10},{8,12},{10,14},{1,5},{3,7},{5,9},{7,11},{... | collective-permute-start | bytes 786440 | tf_op jit(solution)/shard_map/ppermute | solution.py:252
  8.1 7.9 %collective-permute-start.2 = (bf16[128,512]{1,0:T(8,128)(2,1)S(1)}, bf16[128,512]{1,0:T(8,128)(2,1)S(1)}, u32[]{:S(2)}, u32[]{:S(2)}) collective-permute-start(bf16[128,512]{1,0:T(8,128)(2,1)S(1)} %pad_maximum_fusion.3), channel_id=1, source_target_pairs={{0,1},{1,0},{2,3},{3,2},{4,5},{5,4},{6,7},{7,6},{8,9},{9,8},{10,11... | collective-permute-start | bytes 393224 | tf_op jit(solution)/shard_map/ppermute | solution.py:238
  13.8 10.1 %collective-permute-start.11 = (bf16[256,512]{1,0:T(8,128)(2,1)S(1)}, bf16[256,512]{1,0:T(8,128)(2,1)S(1)}, u32[]{:S(2)}, u32[]{:S(2)}) collective-permute-start(bf16[256,512]{1,0:T(8,128)(2,1)S(1)} %collective-permute-done.10.refs_3_), channel_id=1, source_target_pairs={{4,8},{6,10},{8,12},{10,14},{5,9},{7,11},{9,13},{11,15},{20,24},{2... | collective-permute-start | bytes 786440 | tf_op jit(solution)/shard_map/ppermute | solution.py:252
  14.4 10.8 %collective-permute-start.13 = (bf16[256,512]{1,0:T(8,128)(2,1)S(1)}, bf16[256,512]{1,0:T(8,128)(2,1)S(1)}, u32[]{:S(2)}, u32[]{:S(2)}) collective-permute-start(bf16[256,512]{1,0:T(8,128)(2,1)S(1)} %pad_maximum_fusion.refs_2_), channel_id=1, source_target_pairs={{0,2},{2,0},{4,6},{6,4},{8,10},{10,8},{12,14},{14,12},{1,3},{3,1},... | collective-permute-start | bytes 786440 | tf_op jit(solution)/shard_map/ppermute | solution.py:260
  16.1 11.5 %collective-permute-start.3 = (bf16[256,512]{1,0:T(8,128)(2,1)S(1)}, bf16[256,512]{1,0:T(8,128)(2,1)S(1)}, u32[]{:S(2)}, u32[]{:S(2)}) collective-permute-start(bf16[256,512]{1,0:T(8,128)(2,1)S(1)} %pad_maximum_fusion.1.refs_2_), channel_id=1, source_target_pairs={{0,4},{2,6},{4,8},{6,10},{8,12},{10,14},{1,5},{3,7},{5,9},{7,11},{... | collective-permute-start | bytes 786440 | tf_op jit(solution)/shard_map/ppermute | solution.py:252
  23.3 6.6 %collective-permute-start.6 = (bf16[256,512]{1,0:T(8,128)(2,1)S(1)}, bf16[256,512]{1,0:T(8,128)(2,1)S(1)}, u32[]{:S(2)}, u32[]{:S(2)}) collective-permute-start(bf16[256,512]{1,0:T(8,128)(2,1)S(1)} %pad_maximum_fusion.1.refs_2_), channel_id=1, source_target_pairs={{0,2},{2,0},{4,6},{6,4},{8,10},{10,8},{12,14},{14,12},{1,3},{3,1},... | collective-permute-start | bytes 786440 | tf_op jit(solution)/shard_map/ppermute | solution.py:260
  23.9 6.7 %collective-permute-start.12 = (bf16[256,512]{1,0:T(8,128)(2,1)S(1)}, bf16[256,512]{1,0:T(8,128)(2,1)}, u32[]{:S(2)}, u32[]{:S(2)}) collective-permute-start(bf16[256,512]{1,0:T(8,128)(2,1)S(1)} %collective-permute-done.11.refs_4_), channel_id=1, source_target_pairs={{8,12},{10,14},{9,13},{11,15},{24,28},{26,30},{25,29},{27,31}} | collective-permute-start | bytes 786440 | tf_op jit(solution)/shard_map/ppermute | solution.py:252
  25.3 6.7 %collective-permute-start.14 = (bf16[256,512]{1,0:T(8,128)(2,1)S(1)}, bf16[256,512]{1,0:T(8,128)(2,1)S(1)}, u32[]{:S(2)}, u32[]{:S(2)}) collective-permute-start(bf16[256,512]{1,0:T(8,128)(2,1)S(1)} %collective-permute-done.10.refs_3_), channel_id=1, source_target_pairs={{4,6},{6,4},{8,10},{10,8},{12,14},{14,12},{5,7},{7,5},{9,11},{11,9... | collective-permute-start | bytes 786440 | tf_op jit(solution)/shard_map/ppermute | solution.py:260
  27.6 5.7 %collective-permute-start.4 = (bf16[256,512]{1,0:T(8,128)(2,1)S(1)}, bf16[256,512]{1,0:T(8,128)(2,1)}, u32[]{:S(2)}, u32[]{:S(2)}) collective-permute-start(bf16[256,512]{1,0:T(8,128)(2,1)S(1)} %collective-permute-done.3.refs_3_), channel_id=1, source_target_pairs={{4,8},{6,10},{8,12},{10,14},{5,9},{7,11},{9,13},{11,15},{20,24},{2... | collective-permute-start | bytes 786440 | tf_op jit(solution)/shard_map/ppermute | solution.py:252
  29.9 19.3 %collective-permute-start.15 = (bf16[256,512]{1,0:T(8,128)(2,1)S(1)}, bf16[256,512]{1,0:T(8,128)(2,1)S(1)}, u32[]{:S(2)}, u32[]{:S(2)}) collective-permute-start(bf16[256,512]{1,0:T(8,128)(2,1)S(1)} %collective-permute-done.11.refs_4_), channel_id=1, source_target_pairs={{8,10},{10,8},{12,14},{14,12},{9,11},{11,9},{13,15},{15,13},{24,26... | collective-permute-start | bytes 786440 | tf_op jit(solution)/shard_map/ppermute | solution.py:260
  30.6 21.9 %collective-permute-start.16 = (bf16[256,512]{1,0:T(8,128)(2,1)}, bf16[256,512]{1,0:T(8,128)(2,1)}, u32[]{:S(2)}, u32[]{:S(2)}) collective-permute-start(bf16[256,512]{1,0:T(8,128)(2,1)} %collective-permute-done.12.refs_5_), channel_id=1, source_target_pairs={{12,14},{14,12},{13,15},{15,13},{28,30},{30,28},{29,31},{31,29}} | collective-permute-start | bytes 786440 | tf_op jit(solution)/shard_map/ppermute | solution.py:260
  32.0 28.7 %collective-permute-start.7 = (bf16[256,512]{1,0:T(8,128)(2,1)S(1)}, bf16[256,512]{1,0:T(8,128)(2,1)}, u32[]{:S(2)}, u32[]{:S(2)}) collective-permute-start(bf16[256,512]{1,0:T(8,128)(2,1)S(1)} %collective-permute-done.3.refs_3_), channel_id=1, source_target_pairs={{4,6},{6,4},{8,10},{10,8},{12,14},{14,12},{5,7},{7,5},{9,11},{11,9... | collective-permute-start | bytes 786440 | tf_op jit(solution)/shard_map/ppermute | solution.py:260
  33.3 27.3 %collective-permute-start.9 = (bf16[256,512]{1,0:T(8,128)(2,1)S(1)}, bf16[256,512]{1,0:T(8,128)(2,1)}, u32[]{:S(2)}, u32[]{:S(2)}) collective-permute-start(bf16[256,512]{1,0:T(8,128)(2,1)S(1)} %collective-permute-done.6.refs_6_), channel_id=1, source_target_pairs={{0,12},{2,14},{1,13},{3,15},{16,28},{18,30},{17,29},{19,31}} | collective-permute-start | bytes 786440 | tf_op jit(solution)/shard_map/ppermute | solution.py:271
  49.2 11.5 %collective-permute-start.8 = (bf16[256,512]{1,0:T(8,128)(2,1)}, bf16[256,512]{1,0:T(8,128)(2,1)}, u32[]{:S(2)}, u32[]{:S(2)}) collective-permute-start(bf16[256,512]{1,0:T(8,128)(2,1)} %collective-permute-done.4.refs_4_), channel_id=1, source_target_pairs={{8,10},{10,8},{12,14},{14,12},{9,11},{11,9},{13,15},{15,13},{24,26... | collective-permute-start | bytes 786440 | tf_op jit(solution)/shard_map/ppermute | solution.py:260
  50.6 10.1 %collective-permute-start.5 = (bf16[256,512]{1,0:T(8,128)(2,1)}, bf16[256,512]{1,0:T(8,128)(2,1)S(1)}, u32[]{:S(2)}, u32[]{:S(2)}) collective-permute-start(bf16[256,512]{1,0:T(8,128)(2,1)} %collective-permute-done.4.refs_4_), channel_id=1, source_target_pairs={{8,12},{10,14},{9,13},{11,15},{24,28},{26,30},{25,29},{27,31}} | collective-permute-start | bytes 786440 | tf_op jit(solution)/shard_map/ppermute | solution.py:252
  60.6 9.5 %collective-permute-start.17 = (bf16[128,2048]{1,0:T(8,128)(2,1)}, bf16[128,2048]{1,0:T(8,128)(2,1)S(1)}, u32[]{:S(2)}, u32[]{:S(2)}) collective-permute-start(bf16[128,2048]{1,0:T(8,128)(2,1)} %get-tuple-element.15), channel_id=1, source_target_pairs={{0,1},{1,0},{2,3},{3,2},{4,5},{5,4},{6,7},{7,6},{8,9},{9,8},{10,11... | collective-permute-start | bytes 1572872 | tf_op jit(solution)/shard_map/ppermute | solution.py:280
  69.5 2.3 %collective-permute-start.18 = (bf16[128,2048]{1,0:T(8,128)(2,1)}, bf16[128,2048]{1,0:T(8,128)(2,1)S(1)}, u32[]{:S(2)}, u32[]{:S(2)}) collective-permute-start(bf16[128,2048]{1,0:T(8,128)(2,1)} %get-tuple-element.16), channel_id=1, source_target_pairs={{0,1},{1,0},{2,3},{3,2},{4,5},{5,4},{6,7},{7,6},{8,9},{9,8},{10,11... | collective-permute-start | bytes 1572872 | tf_op jit(solution)/shard_map/ppermute | solution.py:284
  (12 other events, 237.9 us)

commit v5 on v4

--- a/solution.py
+++ b/solution.py
@@ -212,8 +212,8 @@
     core = lax.axis_index("tp")
     other = cores - 1 - core
     columns = 2
-    relay = ranks == 8
     lines = ranks // columns
+    relay = lines == 4
     half = KEY_VALUE_HEADS // cores
     group_width = GROUP * HEAD_SIZE
     swap = [(0, 1), (1, 0)]
@@ -259,28 +259,35 @@
             ]
             return lax.ppermute(array, "seq", pairs)
 
-        gathered = []
-        for name, piece in zip("ab", local):
-            line_pieces = [piece]
-            for step in range(1, lines):
-                line_pieces.append(along(line_pieces[-1], step))
-            last = lines if name == "a" else lines - 1
-            cross_pieces = [across(line_pieces[step], step) for step in range(last)]
-            if name == "b":
-                pairs = [(column, (lines - 1) * columns + column) for column in range(columns)]
-                cross_pieces.append(lax.ppermute(cross_pieces[0], "seq", pairs))
-            gathered.append(line_pieces + cross_pieces)
-        slots = [step * columns for step in range(lines)] + [step * columns + 1 for step in range(lines)]
+        def from_first(array):
+            pairs = [(column, (lines - 1) * columns + column) for column in range(columns)]
+            return lax.ppermute(array, "seq", pairs)
+
+        line_slots = [step * columns for step in range(lines)]
+        a, b = [local[0]], [local[1]]
+        a.append(along(a[0], 1))
+        a.append(along(a[1], 2))
+        a.append(from_first(a[0]))
+        a += [across(a[step], step) for step in range(lines)]
+        b.append(along(b[0], 1))
+        b.append(along(b[1], 2))
+        b += [across(b[step], step) for step in range(lines - 1)]
+        both = jnp.concatenate([b[0], b[lines - 1]], axis=0)
+        both, a[5], a[7], sibling_queries = lax.optimization_barrier((both, a[5], a[7], sibling_queries))
+        b.append(from_first(both))
+        gathered = [a, b]
+        slots = [
+            line_slots + [slot + 1 for slot in line_slots],
+            line_slots[:-1] + [slot + 1 for slot in line_slots[:-1]] + line_slots[-1:],
+        ]
     else:
         gathered = [[lax.all_gather(piece, "seq", axis=0, tiled=True)] for piece in local]
-        slots = [0]
+        slots = [[0], [0]]
 
     (first_a, count_a), (first_b, count_b) = chunks
-    out, sibling_a = attend(table, common, first_a, count_a, queries, sibling_queries, gathered[0], slots)
+    out, sibling_a = attend(table, common, first_a, count_a, queries, sibling_queries, gathered[0], slots[0])
     got_a = lax.ppermute(sibling_a, "tp", swap)
-    out, sibling_b = attend(
-        table, common, first_b, count_b, queries, sibling_queries, gathered[1], slots, into=out
-    )
+    out, sibling_b = attend(table, common, first_b, count_b, queries, sibling_queries, gathered[1], slots[1], into=out)
     got_b = lax.ppermute(sibling_b, "tp", swap)
     for got, first in ((got_a, first_a), (got_b, first_b)):
         out = lax.dynamic_update_slice_in_dim(out, got, (other * half + first) * group_width, 1)

time: 73.1 us -> 80.8 us (1.11)
  the two profiles are of different devices: /device:TPU:0 before, /device:TPU:25 now
where the time goes in v5:
time: 80.8 us; the launch traced here: 80.4 us
  starting transfers between devices  30.2 us (37%)
  waiting for transfers between devices  27.3 us (34%)
  Pallas kernels  16.1 us (20%)
  local copies, waits for them, and re-layouts  6.25 us (8%)
    ppermute x4, waiting for transfers between devices, along(): return lax.ppermute(array, 'seq', pairs)  18.7 us
    ppermute x7, starting transfers between devices, across(): return lax.ppermute(array, 'seq', pairs)  17.3 us
    pallas_call x2, Pallas kernels, attend(): pl.pallas_call(functools.partial(attend_kernel, plan), grid_spec=pltpu.Pr...  16.1 us
    ppermute x2, waiting for transfers between devices, from_first(): return lax.ppermute(array, 'seq', pairs)  6.31 us
    ppermute x4, starting transfers between devices, along(): return lax.ppermute(array, 'seq', pairs)  5.16 us
    ppermute x1, starting transfers between devices, shards(): got_a = lax.ppermute(sibling_a, 'tp', swap)  3.71 us
    ppermute x2, starting transfers between devices, from_first(): return lax.ppermute(array, 'seq', pairs)  2.57 us
    dynamic_update_slice x2, local copies, waits for them, and re-layouts, shards(): lax.dynamic_update_slice_in_dim(out, got, (other * half + first) * group_...  1.66 us
  transfers between devices with their start and end apart: 18, of which 7 were waited for; matrix products, arithmetic and copies ran while one was open for 4% of the time, Pallas kernels for 20%

profile of v5, /device:TPU:25, one launch (start us, length us, event | category | flops | bytes accessed | tf_op | source)
XLA Modules:
  0.0 80.4 jit_solution(4236184999197751211)
XLA Ops:
  1.8 1.4 %constant_dynamic-slice_fusion = bf16[128,4096]{1,0:T(8,128)(2,1)S(1)} fusion(bf16[128,8192]{1,0:T(8,128)(2,1)} %refs_0_.3, s32[]{:T(128)S(6)} %select_n.27), kind=kLoop, calls=%fused_computation.7 | loop fusion | bytes 2097156 | tf_op jit(solution)/shard_map/dynamic_slice | solution.py:241
  3.9 1.3 %collective-permute-start.5 = (bf16[256,512]{1,0:T(8,128)(2,1)S(1)}, bf16[256,512]{1,0:T(8,128)(2,1)S(1)}, u32[]{:S(2)}, u32[]{:S(2)}) collective-permute-start(bf16[256,512]{1,0:T(8,128)(2,1)S(1)} %pad_maximum_fusion.1.refs_2_), channel_id=1, source_target_pairs={{0,12},{2,14},{1,13},{3,15},{16,28},{18,30},{17,29},{19,31}} | collective-permute-start | bytes 786440 | tf_op jit(solution)/shard_map/ppermute | solution.py:264
  5.2 1.3 %collective-permute-start.3 = (bf16[256,512]{1,0:T(8,128)(2,1)S(1)}, bf16[256,512]{1,0:T(8,128)(2,1)S(1)}, u32[]{:S(2)}, u32[]{:S(2)}) collective-permute-start(bf16[256,512]{1,0:T(8,128)(2,1)S(1)} %pad_maximum_fusion.1.refs_2_), channel_id=1, source_target_pairs={{0,4},{2,6},{4,8},{6,10},{8,12},{10,14},{1,5},{3,7},{5,9},{7,11},{... | collective-permute-start | bytes 786440 | tf_op jit(solution)/shard_map/ppermute | solution.py:252
  6.6 1.3 %collective-permute-start.8 = (bf16[256,512]{1,0:T(8,128)(2,1)S(1)}, bf16[256,512]{1,0:T(8,128)(2,1)}, u32[]{:S(2)}, u32[]{:S(2)}) collective-permute-start(bf16[256,512]{1,0:T(8,128)(2,1)S(1)} %pad_maximum_fusion.2.refs_2_), channel_id=1, source_target_pairs={{0,4},{2,6},{4,8},{6,10},{8,12},{10,14},{1,5},{3,7},{5,9},{7,11},{... | collective-permute-start | bytes 786440 | tf_op jit(solution)/shard_map/ppermute | solution.py:252
  7.9 1.3 %collective-permute-start.2 = (bf16[256,512]{1,0:T(8,128)(2,1)S(1)}, bf16[256,512]{1,0:T(8,128)(2,1)S(1)}, u32[]{:S(2)}, u32[]{:S(2)}) collective-permute-start(bf16[256,512]{1,0:T(8,128)(2,1)S(1)} %pad_maximum_fusion.2.refs_2_), channel_id=1, source_target_pairs={{0,2},{2,0},{4,6},{6,4},{8,10},{10,8},{12,14},{14,12},{1,3},{3,1},... | collective-permute-start | bytes 786440 | tf_op jit(solution)/shard_map/ppermute | solution.py:260
  9.2 6.3 %collective-permute-done.5.refs_5_ = bf16[256,512]{1,0:T(8,128)(2,1)S(1)} collective-permute-done((bf16[256,512]{1,0:T(8,128)(2,1)S(1)}, bf16[256,512]{1,0:T(8,128)(2,1)S(1)}, u32[]{:S(2)}, u32[]{:S(2)}) %collective-permute-start.5) | collective-permute-done | bytes 262176 | tf_op jit(solution)/shard_map/ppermute | solution.py:264
  15.5 3.1 %collective-permute-start.6 = (bf16[256,512]{1,0:T(8,128)(2,1)S(1)}, bf16[256,512]{1,0:T(8,128)(2,1)S(1)}, u32[]{:S(2)}, u32[]{:S(2)}) collective-permute-start(bf16[256,512]{1,0:T(8,128)(2,1)S(1)} %collective-permute-done.5.refs_5_), channel_id=1, source_target_pairs={{12,14},{14,12},{13,15},{15,13},{28,30},{30,28},{29,31},{31,29}} | collective-permute-start | bytes 786440 | tf_op jit(solution)/shard_map/ppermute | solution.py:260
  18.6 1.9 %collective-permute-done.3.refs_3_ = bf16[256,512]{1,0:T(8,128)(2,1)S(1)} collective-permute-done((bf16[256,512]{1,0:T(8,128)(2,1)S(1)}, bf16[256,512]{1,0:T(8,128)(2,1)S(1)}, u32[]{:S(2)}, u32[]{:S(2)}) %collective-permute-start.3) | collective-permute-done | bytes 262176 | tf_op jit(solution)/shard_map/ppermute | solution.py:252
  20.6 3.1 %collective-permute-start.4 = (bf16[256,512]{1,0:T(8,128)(2,1)S(1)}, bf16[256,512]{1,0:T(8,128)(2,1)S(1)}, u32[]{:S(2)}, u32[]{:S(2)}) collective-permute-start(bf16[256,512]{1,0:T(8,128)(2,1)S(1)} %collective-permute-done.3.refs_3_), channel_id=1, source_target_pairs={{4,6},{6,4},{8,10},{10,8},{12,14},{14,12},{5,7},{7,5},{9,11},{11,9... | collective-permute-start | bytes 786440 | tf_op jit(solution)/shard_map/ppermute | solution.py:260
  23.7 2.6 %collective-permute-done.8.refs_3_ = bf16[256,512]{1,0:T(8,128)(2,1)} collective-permute-done((bf16[256,512]{1,0:T(8,128)(2,1)S(1)}, bf16[256,512]{1,0:T(8,128)(2,1)}, u32[]{:S(2)}, u32[]{:S(2)}) %collective-permute-start.8) | collective-permute-done | bytes 262176 | tf_op jit(solution)/shard_map/ppermute | solution.py:252
  26.3 1.3 %collective-permute-start.13 = (bf16[256,512]{1,0:T(8,128)(2,1)S(1)}, bf16[256,512]{1,0:T(8,128)(2,1)}, u32[]{:S(2)}, u32[]{:S(2)}) collective-permute-start(bf16[256,512]{1,0:T(8,128)(2,1)S(1)} %collective-permute-done.3.refs_3_), channel_id=1, source_target_pairs={{4,8},{6,10},{8,12},{10,14},{5,9},{7,11},{9,13},{11,15},{20,24},{2... | collective-permute-start | bytes 786440 | tf_op jit(solution)/shard_map/ppermute | solution.py:252
  27.6 1.3 %collective-permute-start.9 = (bf16[256,512]{1,0:T(8,128)(2,1)}, bf16[256,512]{1,0:T(8,128)(2,1)}, u32[]{:S(2)}, u32[]{:S(2)}) collective-permute-start(bf16[256,512]{1,0:T(8,128)(2,1)} %collective-permute-done.8.refs_3_), channel_id=1, source_target_pairs={{4,8},{6,10},{8,12},{10,14},{5,9},{7,11},{9,13},{11,15},{20,24},{2... | collective-permute-start | bytes 786440 | tf_op jit(solution)/shard_map/ppermute | solution.py:252
  29.0 1.1 %collective-permute-done.4.refs_7_ = bf16[256,512]{1,0:T(8,128)(2,1)S(1)} collective-permute-done((bf16[256,512]{1,0:T(8,128)(2,1)S(1)}, bf16[256,512]{1,0:T(8,128)(2,1)S(1)}, u32[]{:S(2)}, u32[]{:S(2)}) %collective-permute-start.4) | collective-permute-done | bytes 262176 | tf_op jit(solution)/shard_map/ppermute | solution.py:260
  30.0 1.3 %collective-permute-start.12 = (bf16[512,512]{1,0:T(8,128)(2,1)S(1)}, bf16[512,512]{1,0:T(8,128)(2,1)S(1)}, u32[]{:S(2)}, u32[]{:S(2)}) collective-permute-start(bf16[512,512]{1,0:T(8,128)(2,1)S(1)} %pad_maximum_fusion), channel_id=1, source_target_pairs={{0,12},{2,14},{1,13},{3,15},{16,28},{18,30},{17,29},{19,31}} | collective-permute-start | bytes 1572872 | tf_op jit(solution)/shard_map/ppermute | solution.py:264
  31.3 1.3 %collective-permute-start.14 = (bf16[256,512]{1,0:T(8,128)(2,1)S(1)}, bf16[256,512]{1,0:T(8,128)(2,1)}, u32[]{:S(2)}, u32[]{:S(2)}) collective-permute-start(bf16[256,512]{1,0:T(8,128)(2,1)S(1)} %pad_maximum_fusion.1.refs_2_), channel_id=1, source_target_pairs={{0,2},{2,0},{4,6},{6,4},{8,10},{10,8},{12,14},{14,12},{1,3},{3,1},... | collective-permute-start | bytes 786440 | tf_op jit(solution)/shard_map/ppermute | solution.py:260
  32.6 2.6 %collective-permute-done.13.refs_4_ = bf16[256,512]{1,0:T(8,128)(2,1)} collective-permute-done((bf16[256,512]{1,0:T(8,128)(2,1)S(1)}, bf16[256,512]{1,0:T(8,128)(2,1)}, u32[]{:S(2)}, u32[]{:S(2)}) %collective-permute-start.13) | collective-permute-done | bytes 262176 | tf_op jit(solution)/shard_map/ppermute | solution.py:252
  35.3 3.1 %collective-permute-start.15 = (bf16[256,512]{1,0:T(8,128)(2,1)}, bf16[256,512]{1,0:T(8,128)(2,1)}, u32[]{:S(2)}, u32[]{:S(2)}) collective-permute-start(bf16[256,512]{1,0:T(8,128)(2,1)} %collective-permute-done.13.refs_4_), channel_id=1, source_target_pairs={{8,10},{10,8},{12,14},{14,12},{9,11},{11,9},{13,15},{15,13},{24,26... | collective-permute-start | bytes 786440 | tf_op jit(solution)/shard_map/ppermute | solution.py:260
  38.4 2.1 %collective-permute-start.10 = (bf16[256,512]{1,0:T(8,128)(2,1)}, bf16[256,512]{1,0:T(8,128)(2,1)S(1)}, u32[]{:S(2)}, u32[]{:S(2)}) collective-permute-start(bf16[256,512]{1,0:T(8,128)(2,1)} %collective-permute-done.8.refs_3_), channel_id=1, source_target_pairs={{4,6},{6,4},{8,10},{10,8},{12,14},{14,12},{5,7},{7,5},{9,11},{11,9... | collective-permute-start | bytes 786440 | tf_op jit(solution)/shard_map/ppermute | solution.py:260
  40.6 11.6 %collective-permute-done.9.refs_4_ = bf16[256,512]{1,0:T(8,128)(2,1)} collective-permute-done((bf16[256,512]{1,0:T(8,128)(2,1)}, bf16[256,512]{1,0:T(8,128)(2,1)}, u32[]{:S(2)}, u32[]{:S(2)}) %collective-permute-start.9) | collective-permute-done | bytes 262176 | tf_op jit(solution)/shard_map/ppermute | solution.py:252
  52.1 3.1 %collective-permute-start.11 = (bf16[256,512]{1,0:T(8,128)(2,1)}, bf16[256,512]{1,0:T(8,128)(2,1)S(1)}, u32[]{:S(2)}, u32[]{:S(2)}) collective-permute-start(bf16[256,512]{1,0:T(8,128)(2,1)} %collective-permute-done.9.refs_4_), channel_id=1, source_target_pairs={{8,10},{10,8},{12,14},{14,12},{9,11},{11,9},{13,15},{15,13},{24,26... | collective-permute-start | bytes 786440 | tf_op jit(solution)/shard_map/ppermute | solution.py:260
  56.5 8.1 %attend.2 = (bf16[128,8192]{1,0:T(8,128)(2,1)}, bf16[128,2048]{1,0:T(8,128)(2,1)}) custom-call(s32[386]{0:T(512)} %concatenate.25.table, bf16[128,8192]{1,0:T(8,128)(2,1)} %refs_0_.3, bf16[128,4096]{1,0:T(8,128)(2,1)} %copy-done, bf16[256,512]{1,0:T(8,128)(2,1)} %copy-done.1, bf16[256,512]{1,0:T(8,128)(2,1)} %copy-done.6, ...), custom_call_target="tpu_custom_call" | custom-call | tf_op jit(solution)/shard_map/attend/pallas_call | solution.py:185
  64.6 3.7 %collective-permute-start.16 = (bf16[128,2048]{1,0:T(8,128)(2,1)}, bf16[128,2048]{1,0:T(8,128)(2,1)S(1)}, u32[]{:S(2)}, u32[]{:S(2)}) collective-permute-start(bf16[128,2048]{1,0:T(8,128)(2,1)} %get-tuple-element.23), channel_id=1, source_target_pairs={{0,1},{1,0},{2,3},{3,2},{4,5},{5,4},{6,7},{7,6},{8,9},{9,8},{10,11... | collective-permute-start | bytes 1572872 | tf_op jit(solution)/shard_map/ppermute | solution.py:289
  69.3 8.1 %attend.3 = (bf16[128,8192]{1,0:T(8,128)(2,1)}, bf16[128,2048]{1,0:T(8,128)(2,1)}) custom-call(s32[386]{0:T(512)} %concatenate.25.table, bf16[128,8192]{1,0:T(8,128)(2,1)} %refs_0_.3, bf16[128,4096]{1,0:T(8,128)(2,1)} %copy-done, bf16[256,512]{1,0:T(8,128)(2,1)} %copy-done.2, ...), custom_call_target="tpu_custom_call", output_to_operand_aliasing={{0}: (10, {})} | custom-call | tf_op jit(solution)/shard_map/attend/pallas_call | solution.py:185
  78.3 1.3 %collective-permute-done.17 = bf16[128,2048]{1,0:T(8,128)(2,1)S(1)} collective-permute-done((bf16[128,2048]{1,0:T(8,128)(2,1)}, bf16[128,2048]{1,0:T(8,128)(2,1)S(1)}, u32[]{:S(2)}, u32[]{:S(2)}) %collective-permute-start.17) | collective-permute-done | bytes 524320 | tf_op jit(solution)/shard_map/ppermute | solution.py:291
  (64 shorter events, 6.5 us)
Async XLA Ops:
  1.0 2.2 %collective-permute-start = (bf16[128,512]{1,0:T(8,128)(2,1)S(1)}, bf16[128,512]{1,0:T(8,128)(2,1)S(1)}, u32[]{:S(2)}, u32[]{:S(2)}) collective-permute-start(bf16[128,512]{1,0:T(8,128)(2,1)S(1)} %pad_maximum_fusion.3), channel_id=1, source_target_pairs={{0,1},{1,0},{2,3},{3,2},{4,5},{5,4},{6,7},{7,6},{8,9},{9,8},{10,11... | collective-permute-start | bytes 393224 | tf_op jit(solution)/shard_map/ppermute | solution.py:238
  1.8 53.5 %copy-start.13 = (s32[64,2]{0,1:T(2,128)S(1)}, s32[64,2]{0,1:T(2,128)}, u32[]{:S(2)}) copy-start(s32[64,2]{0,1:T(2,128)} %param.10) | copy-start | bytes 1540
  1.8 53.7 %copy-start.14 = (s32[64,2]{0,1:T(2,128)S(1)}, s32[64,2]{0,1:T(2,128)}, u32[]{:S(2)}) copy-start(s32[64,2]{0,1:T(2,128)} %param.12) | copy-start | bytes 1540
  1.8 54.0 %copy-start.15 = (s32[64]{0:T(128)S(1)}, s32[64]{0:T(128)}, u32[]{:S(2)}) copy-start(s32[64]{0:T(128)} %param.11) | copy-start | bytes 772
  1.8 54.0 %copy-start.16 = (s32[64]{0:T(128)S(1)}, s32[64]{0:T(128)}, u32[]{:S(2)}) copy-start(s32[64]{0:T(128)} %param.13) | copy-start | bytes 772
  3.2 26.9 %collective-permute-start.7 = (bf16[128,4096]{1,0:T(8,128)(2,1)S(1)}, bf16[128,4096]{1,0:T(8,128)(2,1)S(1)}, u32[]{:S(2)}, u32[]{:S(2)}) collective-permute-start(bf16[128,4096]{1,0:T(8,128)(2,1)S(1)} %constant_dynamic-slice_fusion), channel_id=1, source_target_pairs={{0,1},{1,0},{2,3},{3,2},{4,5},{5,4},{6,7},{7,6},{8,9},{9,8},{10,11... | collective-permute-start | bytes 3145736 | tf_op jit(solution)/shard_map/ppermute | solution.py:240
  3.3 53.2 %copy-start.1 = (bf16[256,512]{1,0:T(8,128)(2,1)}, bf16[256,512]{1,0:T(8,128)(2,1)S(1)}, u32[]{:S(2)}) copy-start(bf16[256,512]{1,0:T(8,128)(2,1)S(1)} %pad_maximum_fusion.1.refs_2_) | copy-start | bytes 786436
  3.4 3.1 %collective-permute-start.1 = (bf16[128,512]{1,0:T(8,128)(2,1)S(1)}, bf16[128,512]{1,0:T(8,128)(2,1)S(1)}, u32[]{:S(2)}, u32[]{:S(2)}) collective-permute-start(bf16[128,512]{1,0:T(8,128)(2,1)S(1)} %pad_maximum_fusion.4), channel_id=1, source_target_pairs={{0,1},{1,0},{2,3},{3,2},{4,5},{5,4},{6,7},{7,6},{8,9},{9,8},{10,11... | collective-permute-start | bytes 393224 | tf_op jit(solution)/shard_map/ppermute | solution.py:238
  3.9 11.6 %collective-permute-start.5 = (bf16[256,512]{1,0:T(8,128)(2,1)S(1)}, bf16[256,512]{1,0:T(8,128)(2,1)S(1)}, u32[]{:S(2)}, u32[]{:S(2)}) collective-permute-start(bf16[256,512]{1,0:T(8,128)(2,1)S(1)} %pad_maximum_fusion.1.refs_2_), channel_id=1, source_target_pairs={{0,12},{2,14},{1,13},{3,15},{16,28},{18,30},{17,29},{19,31}} | collective-permute-start | bytes 786440 | tf_op jit(solution)/shard_map/ppermute | solution.py:264
  5.2 15.3 %collective-permute-start.3 = (bf16[256,512]{1,0:T(8,128)(2,1)S(1)}, bf16[256,512]{1,0:T(8,128)(2,1)S(1)}, u32[]{:S(2)}, u32[]{:S(2)}) collective-permute-start(bf16[256,512]{1,0:T(8,128)(2,1)S(1)} %pad_maximum_fusion.1.refs_2_), channel_id=1, source_target_pairs={{0,4},{2,6},{4,8},{6,10},{8,12},{10,14},{1,5},{3,7},{5,9},{7,11},{... | collective-permute-start | bytes 786440 | tf_op jit(solution)/shard_map/ppermute | solution.py:252
  6.6 58.0 %copy-start.2 = (bf16[256,512]{1,0:T(8,128)(2,1)}, bf16[256,512]{1,0:T(8,128)(2,1)S(1)}, u32[]{:S(2)}) copy-start(bf16[256,512]{1,0:T(8,128)(2,1)S(1)} %pad_maximum_fusion.2.refs_2_) | copy-start | bytes 786436
  6.6 19.7 %collective-permute-start.8 = (bf16[256,512]{1,0:T(8,128)(2,1)S(1)}, bf16[256,512]{1,0:T(8,128)(2,1)}, u32[]{:S(2)}, u32[]{:S(2)}) collective-permute-start(bf16[256,512]{1,0:T(8,128)(2,1)S(1)} %pad_maximum_fusion.2.refs_2_), channel_id=1, source_target_pairs={{0,4},{2,6},{4,8},{6,10},{8,12},{10,14},{1,5},{3,7},{5,9},{7,11},{... | collective-permute-start | bytes 786440 | tf_op jit(solution)/shard_map/ppermute | solution.py:252
  7.9 19.7 %collective-permute-start.2 = (bf16[256,512]{1,0:T(8,128)(2,1)S(1)}, bf16[256,512]{1,0:T(8,128)(2,1)S(1)}, u32[]{:S(2)}, u32[]{:S(2)}) collective-permute-start(bf16[256,512]{1,0:T(8,128)(2,1)S(1)} %pad_maximum_fusion.2.refs_2_), channel_id=1, source_target_pairs={{0,2},{2,0},{4,6},{6,4},{8,10},{10,8},{12,14},{14,12},{1,3},{3,1},... | collective-permute-start | bytes 786440 | tf_op jit(solution)/shard_map/ppermute | solution.py:260
  15.5 13.5 %collective-permute-start.6 = (bf16[256,512]{1,0:T(8,128)(2,1)S(1)}, bf16[256,512]{1,0:T(8,128)(2,1)S(1)}, u32[]{:S(2)}, u32[]{:S(2)}) collective-permute-start(bf16[256,512]{1,0:T(8,128)(2,1)S(1)} %collective-permute-done.5.refs_5_), channel_id=1, source_target_pairs={{12,14},{14,12},{13,15},{15,13},{28,30},{30,28},{29,31},{31,29}} | collective-permute-start | bytes 786440 | tf_op jit(solution)/shard_map/ppermute | solution.py:260
  20.6 9.4 %collective-permute-start.4 = (bf16[256,512]{1,0:T(8,128)(2,1)S(1)}, bf16[256,512]{1,0:T(8,128)(2,1)S(1)}, u32[]{:S(2)}, u32[]{:S(2)}) collective-permute-start(bf16[256,512]{1,0:T(8,128)(2,1)S(1)} %collective-permute-done.3.refs_3_), channel_id=1, source_target_pairs={{4,6},{6,4},{8,10},{10,8},{12,14},{14,12},{5,7},{7,5},{9,11},{11,9... | collective-permute-start | bytes 786440 | tf_op jit(solution)/shard_map/ppermute | solution.py:260
  26.3 9.0 %collective-permute-start.13 = (bf16[256,512]{1,0:T(8,128)(2,1)S(1)}, bf16[256,512]{1,0:T(8,128)(2,1)}, u32[]{:S(2)}, u32[]{:S(2)}) collective-permute-start(bf16[256,512]{1,0:T(8,128)(2,1)S(1)} %collective-permute-done.3.refs_3_), channel_id=1, source_target_pairs={{4,8},{6,10},{8,12},{10,14},{5,9},{7,11},{9,13},{11,15},{20,24},{2... | collective-permute-start | bytes 786440 | tf_op jit(solution)/shard_map/ppermute | solution.py:252
  27.6 24.5 %collective-permute-start.9 = (bf16[256,512]{1,0:T(8,128)(2,1)}, bf16[256,512]{1,0:T(8,128)(2,1)}, u32[]{:S(2)}, u32[]{:S(2)}) collective-permute-start(bf16[256,512]{1,0:T(8,128)(2,1)} %collective-permute-done.8.refs_3_), channel_id=1, source_target_pairs={{4,8},{6,10},{8,12},{10,14},{5,9},{7,11},{9,13},{11,15},{20,24},{2... | collective-permute-start | bytes 786440 | tf_op jit(solution)/shard_map/ppermute | solution.py:252
  30.0 38.3 %collective-permute-start.12 = (bf16[512,512]{1,0:T(8,128)(2,1)S(1)}, bf16[512,512]{1,0:T(8,128)(2,1)S(1)}, u32[]{:S(2)}, u32[]{:S(2)}) collective-permute-start(bf16[512,512]{1,0:T(8,128)(2,1)S(1)} %pad_maximum_fusion), channel_id=1, source_target_pairs={{0,12},{2,14},{1,13},{3,15},{16,28},{18,30},{17,29},{19,31}} | collective-permute-start | bytes 1572872 | tf_op jit(solution)/shard_map/ppermute | solution.py:264
  31.3 25.1 %collective-permute-start.14 = (bf16[256,512]{1,0:T(8,128)(2,1)S(1)}, bf16[256,512]{1,0:T(8,128)(2,1)}, u32[]{:S(2)}, u32[]{:S(2)}) collective-permute-start(bf16[256,512]{1,0:T(8,128)(2,1)S(1)} %pad_maximum_fusion.1.refs_2_), channel_id=1, source_target_pairs={{0,2},{2,0},{4,6},{6,4},{8,10},{10,8},{12,14},{14,12},{1,3},{3,1},... | collective-permute-start | bytes 786440 | tf_op jit(solution)/shard_map/ppermute | solution.py:260
  35.3 21.2 %collective-permute-start.15 = (bf16[256,512]{1,0:T(8,128)(2,1)}, bf16[256,512]{1,0:T(8,128)(2,1)}, u32[]{:S(2)}, u32[]{:S(2)}) collective-permute-start(bf16[256,512]{1,0:T(8,128)(2,1)} %collective-permute-done.13.refs_4_), channel_id=1, source_target_pairs={{8,10},{10,8},{12,14},{14,12},{9,11},{11,9},{13,15},{15,13},{24,26... | collective-permute-start | bytes 786440 | tf_op jit(solution)/shard_map/ppermute | solution.py:260
  38.4 29.9 %collective-permute-start.10 = (bf16[256,512]{1,0:T(8,128)(2,1)}, bf16[256,512]{1,0:T(8,128)(2,1)S(1)}, u32[]{:S(2)}, u32[]{:S(2)}) collective-permute-start(bf16[256,512]{1,0:T(8,128)(2,1)} %collective-permute-done.8.refs_3_), channel_id=1, source_target_pairs={{4,6},{6,4},{8,10},{10,8},{12,14},{14,12},{5,7},{7,5},{9,11},{11,9... | collective-permute-start | bytes 786440 | tf_op jit(solution)/shard_map/ppermute | solution.py:260
  52.1 16.2 %collective-permute-start.11 = (bf16[256,512]{1,0:T(8,128)(2,1)}, bf16[256,512]{1,0:T(8,128)(2,1)S(1)}, u32[]{:S(2)}, u32[]{:S(2)}) collective-permute-start(bf16[256,512]{1,0:T(8,128)(2,1)} %collective-permute-done.9.refs_4_), channel_id=1, source_target_pairs={{8,10},{10,8},{12,14},{14,12},{9,11},{11,9},{13,15},{15,13},{24,26... | collective-permute-start | bytes 786440 | tf_op jit(solution)/shard_map/ppermute | solution.py:260
  64.6 12.9 %collective-permute-start.16 = (bf16[128,2048]{1,0:T(8,128)(2,1)}, bf16[128,2048]{1,0:T(8,128)(2,1)S(1)}, u32[]{:S(2)}, u32[]{:S(2)}) collective-permute-start(bf16[128,2048]{1,0:T(8,128)(2,1)} %get-tuple-element.23), channel_id=1, source_target_pairs={{0,1},{1,0},{2,3},{3,2},{4,5},{5,4},{6,7},{7,6},{8,9},{9,8},{10,11... | collective-permute-start | bytes 1572872 | tf_op jit(solution)/shard_map/ppermute | solution.py:289
  77.3 2.2 %collective-permute-start.17 = (bf16[128,2048]{1,0:T(8,128)(2,1)}, bf16[128,2048]{1,0:T(8,128)(2,1)S(1)}, u32[]{:S(2)}, u32[]{:S(2)}) collective-permute-start(bf16[128,2048]{1,0:T(8,128)(2,1)} %get-tuple-element.24), channel_id=1, source_target_pairs={{0,1},{1,0},{2,3},{3,2},{4,5},{5,4},{6,7},{7,6},{8,9},{9,8},{10,11... | collective-permute-start | bytes 1572872 | tf_op jit(solution)/shard_map/ppermute | solution.py:291
  (11 other events, 115.1 us)

commit v6 on v5

--- a/solution.py
+++ b/solution.py
@@ -200,6 +200,7 @@
         out_shape=shapes,
         input_output_aliases=aliases,
         name="attend",
+        compiler_params=pltpu.CompilerParams(vmem_limit_bytes=4 * rows * kv_heads * HEAD_SIZE + 2**23),
     )(table, *operands)
 
 
@@ -232,11 +233,12 @@
         )
 
     local = []
-    for (first, count) in chunks:
-        if local:
-            keys, values, _ = lax.optimization_barrier((keys, values, local[0]))
-        got = lax.ppermute(taken(other, first, count), "tp", swap)
-        local.append(jnp.concatenate([taken(core, first, count), got], axis=0))
+    for name, (first, count) in zip("ab", chunks):
+        mine, theirs = taken(core, first, count), taken(other, first, count)
+        if name == "b":
+            mine, theirs = lax.optimization_barrier((mine, theirs))
+        got = lax.ppermute(theirs, "tp", swap)
+        local.append(jnp.concatenate([mine, got], axis=0))
     sibling_queries = lax.ppermute(
         lax.dynamic_slice_in_dim(queries, other * half * group_width, half * group_width, 1), "tp", swap
     )
@@ -273,7 +275,6 @@
         b.append(along(b[1], 2))
         b += [across(b[step], step) for step in range(lines - 1)]
         both = jnp.concatenate([b[0], b[lines - 1]], axis=0)
-        both, a[5], a[7], sibling_queries = lax.optimization_barrier((both, a[5], a[7], sibling_queries))
         b.append(from_first(both))
         gathered = [a, b]
         slots = [

time: 80.8 us -> 77.4 us (0.958)
  the two profiles are of different devices: /device:TPU:25 before, /device:TPU:0 now
where the time goes in v6:
time: 77.4 us; the launch traced here: 76.8 us
  starting transfers between devices  36.8 us (48%)
  local copies, waits for them, and re-layouts  15.2 us (20%)
  Pallas kernels  14.7 us (19%)
  waiting for transfers between devices  6.34 us (8%)
  other arithmetic  3.37 us (4%)
    ppermute x2, starting transfers between devices, from_first(): return lax.ppermute(array, 'seq', pairs)  16.8 us
    pallas_call x2, Pallas kernels, attend(): pl.pallas_call(functools.partial(attend_kernel, plan), grid_spec=pltpu.Pr...  14.7 us
    ppermute x4, starting transfers between devices, along(): return lax.ppermute(array, 'seq', pairs)  9.72 us
    ppermute x7, starting transfers between devices, across(): return lax.ppermute(array, 'seq', pairs)  8.59 us
    unnamed x47, local copies, waits for them, and re-layouts  7.91 us
    ppermute x4, waiting for transfers between devices, along(): return lax.ppermute(array, 'seq', pairs)  4.56 us
    dynamic_update_slice x2, local copies, waits for them, and re-layouts, shards(): lax.dynamic_update_slice_in_dim(out, got, (other * half + first) * group_...  2.71 us
    dynamic_slice x1, local copies, waits for them, and re-layouts, shards(): lax.dynamic_slice_in_dim(queries, other * half * group_width, half * grou...  2.44 us
  transfers between devices with their start and end apart: 18, of which 3 were waited for; matrix products, arithmetic and copies ran while one was open for 11% of the time, Pallas kernels for 19%

profile of v6, /device:TPU:0, one launch (start us, length us, event | category | flops | bytes accessed | tf_op | source)
XLA Modules:
  0.0 76.8 jit_solution(15388348770484923900)
XLA Ops:
  0.0 1.8 %constant_dynamic-slice_fusion.2 = (bf16[128,256]{1,0:T(8,128)(2,1)}, bf16[128,256]{1,0:T(8,128)(2,1)S(1)}, bf16[128,256]{1,0:T(8,128)(2,1)S(1)}, bf16[128,256]{...) fusion(bf16[128,1024]{1,0:T(8,128)(2,1)} %param.9, ...), kind=kLoop, calls=%fused_computation.11 | loop fusion | bytes 1048592 | tf_op jit(solution)/shard_map/dynamic_slice | solution.py:232
  3.2 2.4 %constant_dynamic-slice_fusion.8 = bf16[128,4096]{1,0:T(8,128)(2,1)} fusion(bf16[128,8192]{1,0:T(8,128)(2,1)} %refs_0_.3, s32[]{:T(128)S(6)} %select_n.23), kind=kLoop, calls=%fused_computation.17 | loop fusion | bytes 2097156 | tf_op jit(solution)/shard_map/dynamic_slice | solution.py:243
  6.1 2.6 %collective-permute-start.4 = (bf16[256,512]{1,0:T(8,128)(2,1)S(1)}, bf16[256,512]{1,0:T(8,128)(2,1)S(1)}, u32[]{:S(2)}, u32[]{:S(2)}) collective-permute-start(bf16[256,512]{1,0:T(8,128)(2,1)S(1)} %constant_dynamic-update-slice_fusion.refs_2_), channel_id=1, source_target_pairs={{0,2},{2,0},{4,6},{6,4},{8,10},{10,8},{12,14},{14,12},{1,3},{3,1},... | collective-permute-start | bytes 786440 | tf_op jit(solution)/shard_map/ppermute | solution.py:262
  8.7 4.2 %collective-permute-start.2 = (bf16[256,512]{1,0:T(8,128)(2,1)S(1)}, bf16[256,512]{1,0:T(8,128)(2,1)}, u32[]{:S(2)}, u32[]{:S(2)}) collective-permute-start(bf16[256,512]{1,0:T(8,128)(2,1)S(1)} %constant_dynamic-update-slice_fusion.refs_2_), channel_id=1, source_target_pairs={{0,4},{2,6},{4,8},{6,10},{8,12},{10,14},{1,5},{3,7},{5,9},{7,11},{... | collective-permute-start | bytes 786440 | tf_op jit(solution)/shard_map/ppermute | solution.py:254
  12.9 0.9 %pad_maximum_fusion.1.refs_2_ = bf16[256,512]{1,0:T(8,128)(2,1)S(1)} fusion(bf16[128,512]{1,0:T(8,128)(2,1)} %collective-permute-done.8, bf16[128,256]{1,0:T(8,128)(2,1)S(1)} %copy-done.16, bf16[128,256]{1,0:T(8,128)(2,1)S(1)} %copy-done.17), kind=kLoop, calls=%fused_computation.1 | loop fusion | flops 786432 | bytes 524288 | tf_op jit(solution)/shard_map/concatenate | solution.py:241
  13.9 2.8 %collective-permute-start.9 = (bf16[256,512]{1,0:T(8,128)(2,1)S(1)}, bf16[256,512]{1,0:T(8,128)(2,1)S(1)}, u32[]{:S(2)}, u32[]{:S(2)}) collective-permute-start(bf16[256,512]{1,0:T(8,128)(2,1)S(1)} %pad_maximum_fusion.1.refs_2_), channel_id=1, source_target_pairs={{0,4},{2,6},{4,8},{6,10},{8,12},{10,14},{1,5},{3,7},{5,9},{7,11},{... | collective-permute-start | bytes 786440 | tf_op jit(solution)/shard_map/ppermute | solution.py:254
  16.7 1.3 %collective-permute-start.11 = (bf16[256,512]{1,0:T(8,128)(2,1)S(1)}, bf16[256,512]{1,0:T(8,128)(2,1)S(1)}, u32[]{:S(2)}, u32[]{:S(2)}) collective-permute-start(bf16[256,512]{1,0:T(8,128)(2,1)S(1)} %pad_maximum_fusion.1.refs_2_), channel_id=1, source_target_pairs={{0,12},{2,14},{1,13},{3,15},{16,28},{18,30},{17,29},{19,31}} | collective-permute-start | bytes 786440 | tf_op jit(solution)/shard_map/ppermute | solution.py:266
  18.9 1.4 %collective-permute-start.3 = (bf16[256,512]{1,0:T(8,128)(2,1)}, bf16[256,512]{1,0:T(8,128)(2,1)}, u32[]{:S(2)}, u32[]{:S(2)}) collective-permute-start(bf16[256,512]{1,0:T(8,128)(2,1)} %collective-permute-done.2.refs_3_), channel_id=1, source_target_pairs={{4,8},{6,10},{8,12},{10,14},{5,9},{7,11},{9,13},{11,15},{20,24},{2... | collective-permute-start | bytes 786440 | tf_op jit(solution)/shard_map/ppermute | solution.py:254
  20.3 4.3 %collective-permute-done.9.refs_3_ = bf16[256,512]{1,0:T(8,128)(2,1)S(1)} collective-permute-done((bf16[256,512]{1,0:T(8,128)(2,1)S(1)}, bf16[256,512]{1,0:T(8,128)(2,1)S(1)}, u32[]{:S(2)}, u32[]{:S(2)}) %collective-permute-start.9) | collective-permute-done | bytes 262176 | tf_op jit(solution)/shard_map/ppermute | solution.py:254
  24.5 1.4 %collective-permute-start.10 = (bf16[256,512]{1,0:T(8,128)(2,1)S(1)}, bf16[256,512]{1,0:T(8,128)(2,1)}, u32[]{:S(2)}, u32[]{:S(2)}) collective-permute-start(bf16[256,512]{1,0:T(8,128)(2,1)S(1)} %collective-permute-done.9.refs_3_), channel_id=1, source_target_pairs={{4,8},{6,10},{8,12},{10,14},{5,9},{7,11},{9,13},{11,15},{20,24},{2... | collective-permute-start | bytes 786440 | tf_op jit(solution)/shard_map/ppermute | solution.py:254
  25.9 1.8 %pad_maximum_fusion = bf16[512,512]{1,0:T(8,128)(2,1)} fusion(bf16[256,512]{1,0:T(8,128)(2,1)S(1)} %collective-permute-done.4.refs_5_, bf16[128,512]{1,0:T(8,128)(2,1)} %copy-done.15, bf16[128,512]{1,0:T(8,128)(2,1)S(1)} %pad_maximum_fusion.2), kind=kLoop, calls=%fused_computation | loop fusion | flops 1572864 | bytes 1048576 | tf_op jit(solution)/shard_map/concatenate | solution.py:277
  27.7 1.7 %collective-permute-done.11.refs_5_ = bf16[256,512]{1,0:T(8,128)(2,1)S(1)} collective-permute-done((bf16[256,512]{1,0:T(8,128)(2,1)S(1)}, bf16[256,512]{1,0:T(8,128)(2,1)S(1)}, u32[]{:S(2)}, u32[]{:S(2)}) %collective-permute-start.11) | collective-permute-done | bytes 262176 | tf_op jit(solution)/shard_map/ppermute | solution.py:266
  32.2 15.5 %collective-permute-start.7 = (bf16[512,512]{1,0:T(8,128)(2,1)}, bf16[512,512]{1,0:T(8,128)(2,1)}, u32[]{:S(2)}, u32[]{:S(2)}) collective-permute-start(bf16[512,512]{1,0:T(8,128)(2,1)} %pad_maximum_fusion), channel_id=1, source_target_pairs={{0,12},{2,14},{1,13},{3,15},{16,28},{18,30},{17,29},{19,31}} | collective-permute-start | bytes 1572872 | tf_op jit(solution)/shard_map/ppermute | solution.py:266
  47.7 1.4 %collective-permute-start.14 = (bf16[256,512]{1,0:T(8,128)(2,1)}, bf16[256,512]{1,0:T(8,128)(2,1)}, u32[]{:S(2)}, u32[]{:S(2)}) collective-permute-start(bf16[256,512]{1,0:T(8,128)(2,1)} %collective-permute-done.10.refs_4_), channel_id=1, source_target_pairs={{8,10},{10,8},{12,14},{14,12},{9,11},{11,9},{13,15},{15,13},{24,26... | collective-permute-start | bytes 786440 | tf_op jit(solution)/shard_map/ppermute | solution.py:262
  49.8 1.4 %collective-permute-start.5 = (bf16[256,512]{1,0:T(8,128)(2,1)}, bf16[256,512]{1,0:T(8,128)(2,1)}, u32[]{:S(2)}, u32[]{:S(2)}) collective-permute-start(bf16[256,512]{1,0:T(8,128)(2,1)} %collective-permute-done.2.refs_3_), channel_id=1, source_target_pairs={{4,6},{6,4},{8,10},{10,8},{12,14},{14,12},{5,7},{7,5},{9,11},{11,9... | collective-permute-start | bytes 786440 | tf_op jit(solution)/shard_map/ppermute | solution.py:262
  51.9 1.3 %collective-permute-start.6 = (bf16[256,512]{1,0:T(8,128)(2,1)}, bf16[256,512]{1,0:T(8,128)(2,1)}, u32[]{:S(2)}, u32[]{:S(2)}) collective-permute-start(bf16[256,512]{1,0:T(8,128)(2,1)} %collective-permute-done.3.refs_4_), channel_id=1, source_target_pairs={{8,10},{10,8},{12,14},{14,12},{9,11},{11,9},{13,15},{15,13},{24,26... | collective-permute-start | bytes 786440 | tf_op jit(solution)/shard_map/ppermute | solution.py:262
  53.8 1.0 %copy-done.6 = bf16[256,512]{1,0:T(8,128)(2,1)S(1)} copy-done((bf16[256,512]{1,0:T(8,128)(2,1)S(1)}, bf16[256,512]{1,0:T(8,128)(2,1)}, u32[]{:S(2)}) %copy-start.6) | copy-done | bytes 262168
  54.8 0.9 %copy-done.8 = bf16[256,512]{1,0:T(8,128)(2,1)S(1)} copy-done((bf16[256,512]{1,0:T(8,128)(2,1)S(1)}, bf16[256,512]{1,0:T(8,128)(2,1)}, u32[]{:S(2)}) %copy-start.8) | copy-done | bytes 262168
  55.8 0.9 %copy-done.10 = bf16[256,512]{1,0:T(8,128)(2,1)S(1)} copy-done((bf16[256,512]{1,0:T(8,128)(2,1)S(1)}, bf16[256,512]{1,0:T(8,128)(2,1)}, u32[]{:S(2)}) %copy-start.10) | copy-done | bytes 262168
  56.7 0.9 %copy-done.12 = bf16[256,512]{1,0:T(8,128)(2,1)S(1)} copy-done((bf16[256,512]{1,0:T(8,128)(2,1)S(1)}, bf16[256,512]{1,0:T(8,128)(2,1)}, u32[]{:S(2)}) %copy-start.12) | copy-done | bytes 262168
  57.7 0.9 %copy-done.14 = bf16[256,512]{1,0:T(8,128)(2,1)S(1)} copy-done((bf16[256,512]{1,0:T(8,128)(2,1)S(1)}, bf16[256,512]{1,0:T(8,128)(2,1)}, u32[]{:S(2)}) %copy-start.14) | copy-done | bytes 262168
  58.6 7.2 %attend.2 = (bf16[128,8192]{1,0:T(8,128)(2,1)}, bf16[128,2048]{1,0:T(8,128)(2,1)}) custom-call(s32[386]{0:T(512)S(1)} %concatenate.25.table, bf16[128,8192]{1,0:T(8,128)(2,1)S(1)} %copy-done, bf16[128,4096]{1,0:T(8,128)(2,1)S(1)} %collective-permute-done.refs_1_, bf16[256,512]{1,0:T(8,128)(2,1)S(1)} %pad_maximum_fusion.1.refs_2_, ...), custom_call_target="tpu_custom_call" | custom-call | tf_op jit(solution)/shard_map/attend/pallas_call | solution.py:185
  66.0 7.5 %attend.3 = (bf16[128,8192]{1,0:T(8,128)(2,1)}, bf16[128,2048]{1,0:T(8,128)(2,1)}) custom-call(s32[386]{0:T(512)S(1)} %concatenate.25.table, bf16[128,8192]{1,0:T(8,128)(2,1)S(1)} %copy-done, bf16[128,4096]{1,0:T(8,128)(2,1)S(1)} %collective-permute-done.refs_1_, bf16[256,512]{1,0:T(8,128)(2,1)S(1)} %copy-done.4, ...), custom_call_target="tpu_custom_call", output_to_operand_aliasing={{0}: (10, {})} | custom-call | tf_op jit(solution)/shard_map/attend/pallas_call | solution.py:185
  74.0 1.9 %constant_dynamic-update-slice_fusion.3 = bf16[128,8192]{1,0:T(8,128)(2,1)} fusion(bf16[128,8192]{1,0:T(8,128)(2,1)} %get-tuple-element.14, bf16[128,2048]{1,0:T(8,128)(2,1)} %collective-permute-done.16, s32[]{:T(128)S(6)} %select_n.23), kind=kLoop, calls=%fused_computation.8 | loop fusion | bytes 1048580 | tf_op jit(solution)/shard_map/dynamic_update_slice | solution.py:294
  (74 shorter events, 8.9 us)
Async XLA Ops:
  1.8 11.1 %collective-permute-start.8 = (bf16[128,512]{1,0:T(8,128)(2,1)S(1)}, bf16[128,512]{1,0:T(8,128)(2,1)}, u32[]{:S(2)}, u32[]{:S(2)}) collective-permute-start(bf16[128,512]{1,0:T(8,128)(2,1)S(1)} %pad_maximum_fusion.4), channel_id=1, source_target_pairs={{0,1},{1,0},{2,3},{3,2},{4,5},{5,4},{6,7},{7,6},{8,9},{9,8},{10,11... | collective-permute-start | bytes 393224 | tf_op jit(solution)/shard_map/ppermute | solution.py:240
  3.0 3.1 %collective-permute-start.1 = (bf16[128,512]{1,0:T(8,128)(2,1)}, bf16[128,512]{1,0:T(8,128)(2,1)S(1)}, u32[]{:S(2)}, u32[]{:S(2)}) collective-permute-start(bf16[128,512]{1,0:T(8,128)(2,1)} %pad_maximum_fusion.3), channel_id=1, source_target_pairs={{0,1},{1,0},{2,3},{3,2},{4,5},{5,4},{6,7},{7,6},{8,9},{9,8},{10,11... | collective-permute-start | bytes 393224 | tf_op jit(solution)/shard_map/ppermute | solution.py:240
  3.1 50.1 %copy-start.18 = (s32[64,2]{0,1:T(2,128)S(1)}, s32[64,2]{0,1:T(2,128)}, u32[]{:S(2)}) copy-start(s32[64,2]{0,1:T(2,128)} %param.10) | copy-start | bytes 1540
  3.1 50.3 %copy-start.19 = (s32[64,2]{0,1:T(2,128)S(1)}, s32[64,2]{0,1:T(2,128)}, u32[]{:S(2)}) copy-start(s32[64,2]{0,1:T(2,128)} %param.12) | copy-start | bytes 1540
  3.1 50.6 %copy-start.20 = (s32[64]{0:T(128)S(1)}, s32[64]{0:T(128)}, u32[]{:S(2)}) copy-start(s32[64]{0:T(128)} %param.11) | copy-start | bytes 772
  3.1 50.6 %copy-start.21 = (s32[64]{0:T(128)S(1)}, s32[64]{0:T(128)}, u32[]{:S(2)}) copy-start(s32[64]{0:T(128)} %param.13) | copy-start | bytes 772
  3.1 50.7 %copy-start = (bf16[128,8192]{1,0:T(8,128)(2,1)S(1)}, bf16[128,8192]{1,0:T(8,128)(2,1)}, u32[]{:S(2)}) copy-start(bf16[128,8192]{1,0:T(8,128)(2,1)} %refs_0_.3) | copy-start | bytes 6291460
  5.6 48.2 %collective-permute-start = (bf16[128,4096]{1,0:T(8,128)(2,1)}, bf16[128,4096]{1,0:T(8,128)(2,1)S(1)}, u32[]{:S(2)}, u32[]{:S(2)}) collective-permute-start(bf16[128,4096]{1,0:T(8,128)(2,1)} %constant_dynamic-slice_fusion.8), channel_id=1, source_target_pairs={{0,1},{1,0},{2,3},{3,2},{4,5},{5,4},{6,7},{7,6},{8,9},{9,8},{10,11... | collective-permute-start | bytes 3145736 | tf_op jit(solution)/shard_map/ppermute | solution.py:242
  6.1 18.4 %copy-start.3 = (bf16[256,512]{1,0:T(8,128)(2,1)}, bf16[256,512]{1,0:T(8,128)(2,1)S(1)}, u32[]{:S(2)}) copy-start(bf16[256,512]{1,0:T(8,128)(2,1)S(1)} %constant_dynamic-update-slice_fusion.refs_2_) | copy-start | bytes 786436
  6.1 11.9 %collective-permute-start.4 = (bf16[256,512]{1,0:T(8,128)(2,1)S(1)}, bf16[256,512]{1,0:T(8,128)(2,1)S(1)}, u32[]{:S(2)}, u32[]{:S(2)}) collective-permute-start(bf16[256,512]{1,0:T(8,128)(2,1)S(1)} %constant_dynamic-update-slice_fusion.refs_2_), channel_id=1, source_target_pairs={{0,2},{2,0},{4,6},{6,4},{8,10},{10,8},{12,14},{14,12},{1,3},{3,1},... | collective-permute-start | bytes 786440 | tf_op jit(solution)/shard_map/ppermute | solution.py:262
  8.7 10.2 %collective-permute-start.2 = (bf16[256,512]{1,0:T(8,128)(2,1)S(1)}, bf16[256,512]{1,0:T(8,128)(2,1)}, u32[]{:S(2)}, u32[]{:S(2)}) collective-permute-start(bf16[256,512]{1,0:T(8,128)(2,1)S(1)} %constant_dynamic-update-slice_fusion.refs_2_), channel_id=1, source_target_pairs={{0,4},{2,6},{4,8},{6,10},{8,12},{10,14},{1,5},{3,7},{5,9},{7,11},{... | collective-permute-start | bytes 786440 | tf_op jit(solution)/shard_map/ppermute | solution.py:254
  13.9 10.7 %collective-permute-start.9 = (bf16[256,512]{1,0:T(8,128)(2,1)S(1)}, bf16[256,512]{1,0:T(8,128)(2,1)S(1)}, u32[]{:S(2)}, u32[]{:S(2)}) collective-permute-start(bf16[256,512]{1,0:T(8,128)(2,1)S(1)} %pad_maximum_fusion.1.refs_2_), channel_id=1, source_target_pairs={{0,4},{2,6},{4,8},{6,10},{8,12},{10,14},{1,5},{3,7},{5,9},{7,11},{... | collective-permute-start | bytes 786440 | tf_op jit(solution)/shard_map/ppermute | solution.py:254
  16.7 12.7 %collective-permute-start.11 = (bf16[256,512]{1,0:T(8,128)(2,1)S(1)}, bf16[256,512]{1,0:T(8,128)(2,1)S(1)}, u32[]{:S(2)}, u32[]{:S(2)}) collective-permute-start(bf16[256,512]{1,0:T(8,128)(2,1)S(1)} %pad_maximum_fusion.1.refs_2_), channel_id=1, source_target_pairs={{0,12},{2,14},{1,13},{3,15},{16,28},{18,30},{17,29},{19,31}} | collective-permute-start | bytes 786440 | tf_op jit(solution)/shard_map/ppermute | solution.py:266
  18.0 12.8 %collective-permute-start.12 = (bf16[256,512]{1,0:T(8,128)(2,1)S(1)}, bf16[256,512]{1,0:T(8,128)(2,1)S(1)}, u32[]{:S(2)}, u32[]{:S(2)}) collective-permute-start(bf16[256,512]{1,0:T(8,128)(2,1)S(1)} %pad_maximum_fusion.1.refs_2_), channel_id=1, source_target_pairs={{0,2},{2,0},{4,6},{6,4},{8,10},{10,8},{12,14},{14,12},{1,3},{3,1},... | collective-permute-start | bytes 786440 | tf_op jit(solution)/shard_map/ppermute | solution.py:262
  18.9 13.3 %collective-permute-start.3 = (bf16[256,512]{1,0:T(8,128)(2,1)}, bf16[256,512]{1,0:T(8,128)(2,1)}, u32[]{:S(2)}, u32[]{:S(2)}) collective-permute-start(bf16[256,512]{1,0:T(8,128)(2,1)} %collective-permute-done.2.refs_3_), channel_id=1, source_target_pairs={{4,8},{6,10},{8,12},{10,14},{5,9},{7,11},{9,13},{11,15},{20,24},{2... | collective-permute-start | bytes 786440 | tf_op jit(solution)/shard_map/ppermute | solution.py:254
  24.5 23.2 %collective-permute-start.10 = (bf16[256,512]{1,0:T(8,128)(2,1)S(1)}, bf16[256,512]{1,0:T(8,128)(2,1)}, u32[]{:S(2)}, u32[]{:S(2)}) collective-permute-start(bf16[256,512]{1,0:T(8,128)(2,1)S(1)} %collective-permute-done.9.refs_3_), channel_id=1, source_target_pairs={{4,8},{6,10},{8,12},{10,14},{5,9},{7,11},{9,13},{11,15},{20,24},{2... | collective-permute-start | bytes 786440 | tf_op jit(solution)/shard_map/ppermute | solution.py:254
  29.4 19.7 %collective-permute-start.15 = (bf16[256,512]{1,0:T(8,128)(2,1)S(1)}, bf16[256,512]{1,0:T(8,128)(2,1)S(1)}, u32[]{:S(2)}, u32[]{:S(2)}) collective-permute-start(bf16[256,512]{1,0:T(8,128)(2,1)S(1)} %collective-permute-done.11.refs_5_), channel_id=1, source_target_pairs={{12,14},{14,12},{13,15},{15,13},{28,30},{30,28},{29,31},{31,29}} | collective-permute-start | bytes 786440 | tf_op jit(solution)/shard_map/ppermute | solution.py:262
  31.5 19.6 %collective-permute-start.13 = (bf16[256,512]{1,0:T(8,128)(2,1)S(1)}, bf16[256,512]{1,0:T(8,128)(2,1)S(1)}, u32[]{:S(2)}, u32[]{:S(2)}) collective-permute-start(bf16[256,512]{1,0:T(8,128)(2,1)S(1)} %collective-permute-done.9.refs_3_), channel_id=1, source_target_pairs={{4,6},{6,4},{8,10},{10,8},{12,14},{14,12},{5,7},{7,5},{9,11},{11,9... | collective-permute-start | bytes 786440 | tf_op jit(solution)/shard_map/ppermute | solution.py:262
  32.2 33.8 %collective-permute-start.7 = (bf16[512,512]{1,0:T(8,128)(2,1)}, bf16[512,512]{1,0:T(8,128)(2,1)}, u32[]{:S(2)}, u32[]{:S(2)}) collective-permute-start(bf16[512,512]{1,0:T(8,128)(2,1)} %pad_maximum_fusion), channel_id=1, source_target_pairs={{0,12},{2,14},{1,13},{3,15},{16,28},{18,30},{17,29},{19,31}} | collective-permute-start | bytes 1572872 | tf_op jit(solution)/shard_map/ppermute | solution.py:266
  47.7 6.1 %collective-permute-start.14 = (bf16[256,512]{1,0:T(8,128)(2,1)}, bf16[256,512]{1,0:T(8,128)(2,1)}, u32[]{:S(2)}, u32[]{:S(2)}) collective-permute-start(bf16[256,512]{1,0:T(8,128)(2,1)} %collective-permute-done.10.refs_4_), channel_id=1, source_target_pairs={{8,10},{10,8},{12,14},{14,12},{9,11},{11,9},{13,15},{15,13},{24,26... | collective-permute-start | bytes 786440 | tf_op jit(solution)/shard_map/ppermute | solution.py:262
  49.8 16.2 %collective-permute-start.5 = (bf16[256,512]{1,0:T(8,128)(2,1)}, bf16[256,512]{1,0:T(8,128)(2,1)}, u32[]{:S(2)}, u32[]{:S(2)}) collective-permute-start(bf16[256,512]{1,0:T(8,128)(2,1)} %collective-permute-done.2.refs_3_), channel_id=1, source_target_pairs={{4,6},{6,4},{8,10},{10,8},{12,14},{14,12},{5,7},{7,5},{9,11},{11,9... | collective-permute-start | bytes 786440 | tf_op jit(solution)/shard_map/ppermute | solution.py:262
  51.9 14.1 %collective-permute-start.6 = (bf16[256,512]{1,0:T(8,128)(2,1)}, bf16[256,512]{1,0:T(8,128)(2,1)}, u32[]{:S(2)}, u32[]{:S(2)}) collective-permute-start(bf16[256,512]{1,0:T(8,128)(2,1)} %collective-permute-done.3.refs_4_), channel_id=1, source_target_pairs={{8,10},{10,8},{12,14},{14,12},{9,11},{11,9},{13,15},{15,13},{24,26... | collective-permute-start | bytes 786440 | tf_op jit(solution)/shard_map/ppermute | solution.py:262
  65.9 8.2 %collective-permute-start.16 = (bf16[128,2048]{1,0:T(8,128)(2,1)}, bf16[128,2048]{1,0:T(8,128)(2,1)}, u32[]{:S(2)}, u32[]{:S(2)}) collective-permute-start(bf16[128,2048]{1,0:T(8,128)(2,1)} %get-tuple-element.15), channel_id=1, source_target_pairs={{0,1},{1,0},{2,3},{3,2},{4,5},{5,4},{6,7},{7,6},{8,9},{9,8},{10,11... | collective-permute-start | bytes 1572872 | tf_op jit(solution)/shard_map/ppermute | solution.py:290
  73.5 2.4 %collective-permute-start.17 = (bf16[128,2048]{1,0:T(8,128)(2,1)}, bf16[128,2048]{1,0:T(8,128)(2,1)S(1)}, u32[]{:S(2)}, u32[]{:S(2)}) collective-permute-start(bf16[128,2048]{1,0:T(8,128)(2,1)} %get-tuple-element.16), channel_id=1, source_target_pairs={{0,1},{1,0},{2,3},{3,2},{4,5},{5,4},{6,7},{7,6},{8,9},{9,8},{10,11... | collective-permute-start | bytes 1572872 | tf_op jit(solution)/shard_map/ppermute | solution.py:292
  (16 other events, 78.9 us)

commit v7 on v6

--- a/solution.py
+++ b/solution.py
@@ -25,7 +25,7 @@
         refs.pop(0)
     out = refs.pop(0) if own else None
     sibling_out = refs.pop(0) if sibling else None
-    rows_held, own_held, own_made, sibling_held, sibling_made, sems, out_sems = refs
+    rows_held, own_made, sibling_made, sems, out_sems = refs
     vertical_at, vertical_count_at, slash_at, slash_count_at, rank_at, core_at = offsets
     vertical_width, slash_width = widths
     chip_rows = cores * MASK_BLOCK_SIZE
@@ -39,12 +39,6 @@
     for at, (piece, slot) in enumerate(zip(pieces, slots)):
         held = rows_held.at[pl.ds(slot * chip_rows, piece.shape[0])]
         moves.append(pltpu.make_async_copy(piece, held, sems.at[at]))
-    if own:
-        lanes = pl.ds(pl.multiple_of((core * half + kv_first) * width, width), kv_heads * width)
-        moves.append(pltpu.make_async_copy(own_queries.at[:, lanes], own_held, sems.at[len(slots)]))
-    if sibling:
-        lanes = pl.ds(kv_first * width, kv_heads * width)
-        moves.append(pltpu.make_async_copy(sibling_queries.at[:, lanes], sibling_held, sems.at[len(slots) + 1]))
     for move in moves:
         move.start()
     for move in moves:
@@ -94,13 +88,19 @@
         value_lanes = pl.ds(pl.multiple_of((kv_heads + kv) * HEAD_SIZE, HEAD_SIZE), HEAD_SIZE)
         sides = []
         if own:
-            sides.append((own_held, own_made, rank * cores + core, own_row))
+            sides.append((own_queries, own_made, rank * cores + core, own_row))
         if sibling:
-            sides.append((sibling_held, sibling_made, rank * cores + other, own_row + MASK_BLOCK_SIZE))
+            sides.append((sibling_queries, sibling_made, rank * cores + other, own_row + MASK_BLOCK_SIZE))
 
         def lanes_of(slot):
             return pl.ds(pl.multiple_of(kv * width + slot * HEAD_SIZE, HEAD_SIZE), HEAD_SIZE)
 
+        def query(held, slot):
+            start = (kv_first + kv) * width + slot * HEAD_SIZE
+            if held is own_queries:
+                start = start + core * half * width
+            return held[:, pl.ds(pl.multiple_of(start, HEAD_SIZE), HEAD_SIZE)]
+
         def key(row):
             return rows_held[tile_rows(row), key_lanes]
 
@@ -108,13 +108,13 @@
             return rows_held[tile_rows(row), value_lanes]
 
         diagonal = [
-            product(jnp.concatenate([held[:, lanes_of(slot)] for slot in range(GROUP)], axis=0), [key(row)])
+            product(jnp.concatenate([query(held, slot) for slot in range(GROUP)], axis=0), [key(row)])
             for held, _, _, row in sides
         ]
         pending = []
         for slot in range(GROUP):
             head = (core * half + kv_first + kv) * GROUP + slot
-            queries = [held[:, lanes_of(slot)] for held, _, _, _ in sides]
+            queries = [query(held, slot) for held, _, _, _ in sides]
             verticals = []
             for entry in range(vertical_width):
                 vertical = table[vertical_at + head * vertical_width + entry]
@@ -179,6 +179,7 @@
     if sibling:
         shapes.append(jax.ShapeDtypeStruct((tokens, width), jnp.bfloat16))
     anywhere = pl.BlockSpec(memory_space=pl.ANY)
+    resident = pl.BlockSpec(memory_space=pltpu.VMEM)
     held = pltpu.VMEM((tokens, width), jnp.bfloat16)
     small = pltpu.VMEM((16, HEAD_SIZE), jnp.bfloat16)
     rows = sum(piece.shape[0] for piece in pieces)
@@ -187,11 +188,11 @@
         grid_spec=pltpu.PrefetchScalarGridSpec(
             num_scalar_prefetch=1,
             grid=(),
-            in_specs=[anywhere] * len(operands),
+            in_specs=[resident] * (own + sibling) + [anywhere] * (len(operands) - own - sibling),
             out_specs=[anywhere] * len(shapes),
             scratch_shapes=[pltpu.VMEM((rows, 2 * kv_heads * HEAD_SIZE), jnp.bfloat16)]
-            + [held if own else small] * 2
-            + [held if sibling else small] * 2
+            + [held if own else small]
+            + [held if sibling else small]
             + [
                 pltpu.SemaphoreType.DMA((len(pieces) + 2,)),
                 pltpu.SemaphoreType.DMA((kv_heads, 2)),
@@ -200,7 +201,7 @@
         out_shape=shapes,
         input_output_aliases=aliases,
         name="attend",
-        compiler_params=pltpu.CompilerParams(vmem_limit_bytes=4 * rows * kv_heads * HEAD_SIZE + 2**23),
+        compiler_params=pltpu.CompilerParams(vmem_limit_bytes=4 * rows * kv_heads * HEAD_SIZE + 2**24),
     )(table, *operands)
 
 

time: 77.4 us -> 77.4 us (level)
  no operation moved by 1% of the time
where the time goes in v7:
time: 77.4 us; the launch traced here: 76.8 us
  starting transfers between devices  36.8 us (48%)
  local copies, waits for them, and re-layouts  15.2 us (20%)
  Pallas kernels  14.7 us (19%)
  waiting for transfers between devices  6.34 us (8%)
  other arithmetic  3.37 us (4%)
    ppermute x2, starting transfers between devices, from_first(): return lax.ppermute(array, 'seq', pairs)  16.8 us
    pallas_call x2, Pallas kernels, attend(): pl.pallas_call(functools.partial(attend_kernel, plan), grid_spec=pltpu.Pr...  14.7 us
    ppermute x4, starting transfers between devices, along(): return lax.ppermute(array, 'seq', pairs)  9.72 us
    ppermute x7, starting transfers between devices, across(): return lax.ppermute(array, 'seq', pairs)  8.59 us
    unnamed x47, local copies, waits for them, and re-layouts  7.91 us
    ppermute x4, waiting for transfers between devices, along(): return lax.ppermute(array, 'seq', pairs)  4.56 us
    dynamic_update_slice x2, local copies, waits for them, and re-layouts, shards(): lax.dynamic_update_slice_in_dim(out, got, (other * half + first) * group_...  2.71 us
    dynamic_slice x1, local copies, waits for them, and re-layouts, shards(): lax.dynamic_slice_in_dim(queries, other * half * group_width, half * grou...  2.44 us
  transfers between devices with their start and end apart: 18, of which 3 were waited for; matrix products, arithmetic and copies ran while one was open for 11% of the time, Pallas kernels for 19%

profile of v7, /device:TPU:0, one launch (start us, length us, event | category | flops | bytes accessed | tf_op | source)
XLA Modules:
  0.0 76.8 jit_solution(17591336447831891950)
XLA Ops:
  0.0 1.8 %constant_dynamic-slice_fusion.2 = (bf16[128,256]{1,0:T(8,128)(2,1)}, bf16[128,256]{1,0:T(8,128)(2,1)S(1)}, bf16[128,256]{1,0:T(8,128)(2,1)S(1)}, bf16[128,256]{...) fusion(bf16[128,1024]{1,0:T(8,128)(2,1)} %param.9, ...), kind=kLoop, calls=%fused_computation.11 | loop fusion | bytes 1048592 | tf_op jit(solution)/shard_map/dynamic_slice | solution.py:233
  3.2 2.4 %constant_dynamic-slice_fusion.8 = bf16[128,4096]{1,0:T(8,128)(2,1)} fusion(bf16[128,8192]{1,0:T(8,128)(2,1)} %refs_0_.3, s32[]{:T(128)S(6)} %select_n.23), kind=kLoop, calls=%fused_computation.17 | loop fusion | bytes 2097156 | tf_op jit(solution)/shard_map/dynamic_slice | solution.py:244
  6.1 2.6 %collective-permute-start.4 = (bf16[256,512]{1,0:T(8,128)(2,1)S(1)}, bf16[256,512]{1,0:T(8,128)(2,1)S(1)}, u32[]{:S(2)}, u32[]{:S(2)}) collective-permute-start(bf16[256,512]{1,0:T(8,128)(2,1)S(1)} %constant_dynamic-update-slice_fusion.refs_2_), channel_id=1, source_target_pairs={{0,2},{2,0},{4,6},{6,4},{8,10},{10,8},{12,14},{14,12},{1,3},{3,1},... | collective-permute-start | bytes 786440 | tf_op jit(solution)/shard_map/ppermute | solution.py:263
  8.7 4.2 %collective-permute-start.2 = (bf16[256,512]{1,0:T(8,128)(2,1)S(1)}, bf16[256,512]{1,0:T(8,128)(2,1)}, u32[]{:S(2)}, u32[]{:S(2)}) collective-permute-start(bf16[256,512]{1,0:T(8,128)(2,1)S(1)} %constant_dynamic-update-slice_fusion.refs_2_), channel_id=1, source_target_pairs={{0,4},{2,6},{4,8},{6,10},{8,12},{10,14},{1,5},{3,7},{5,9},{7,11},{... | collective-permute-start | bytes 786440 | tf_op jit(solution)/shard_map/ppermute | solution.py:255
  12.9 0.9 %pad_maximum_fusion.1.refs_2_ = bf16[256,512]{1,0:T(8,128)(2,1)S(1)} fusion(bf16[128,512]{1,0:T(8,128)(2,1)} %collective-permute-done.8, bf16[128,256]{1,0:T(8,128)(2,1)S(1)} %copy-done.16, bf16[128,256]{1,0:T(8,128)(2,1)S(1)} %copy-done.17), kind=kLoop, calls=%fused_computation.1 | loop fusion | flops 786432 | bytes 524288 | tf_op jit(solution)/shard_map/concatenate | solution.py:242
  13.9 2.8 %collective-permute-start.9 = (bf16[256,512]{1,0:T(8,128)(2,1)S(1)}, bf16[256,512]{1,0:T(8,128)(2,1)S(1)}, u32[]{:S(2)}, u32[]{:S(2)}) collective-permute-start(bf16[256,512]{1,0:T(8,128)(2,1)S(1)} %pad_maximum_fusion.1.refs_2_), channel_id=1, source_target_pairs={{0,4},{2,6},{4,8},{6,10},{8,12},{10,14},{1,5},{3,7},{5,9},{7,11},{... | collective-permute-start | bytes 786440 | tf_op jit(solution)/shard_map/ppermute | solution.py:255
  16.7 1.3 %collective-permute-start.11 = (bf16[256,512]{1,0:T(8,128)(2,1)S(1)}, bf16[256,512]{1,0:T(8,128)(2,1)S(1)}, u32[]{:S(2)}, u32[]{:S(2)}) collective-permute-start(bf16[256,512]{1,0:T(8,128)(2,1)S(1)} %pad_maximum_fusion.1.refs_2_), channel_id=1, source_target_pairs={{0,12},{2,14},{1,13},{3,15},{16,28},{18,30},{17,29},{19,31}} | collective-permute-start | bytes 786440 | tf_op jit(solution)/shard_map/ppermute | solution.py:267
  18.9 1.4 %collective-permute-start.3 = (bf16[256,512]{1,0:T(8,128)(2,1)}, bf16[256,512]{1,0:T(8,128)(2,1)}, u32[]{:S(2)}, u32[]{:S(2)}) collective-permute-start(bf16[256,512]{1,0:T(8,128)(2,1)} %collective-permute-done.2.refs_3_), channel_id=1, source_target_pairs={{4,8},{6,10},{8,12},{10,14},{5,9},{7,11},{9,13},{11,15},{20,24},{2... | collective-permute-start | bytes 786440 | tf_op jit(solution)/shard_map/ppermute | solution.py:255
  20.3 4.3 %collective-permute-done.9.refs_3_ = bf16[256,512]{1,0:T(8,128)(2,1)S(1)} collective-permute-done((bf16[256,512]{1,0:T(8,128)(2,1)S(1)}, bf16[256,512]{1,0:T(8,128)(2,1)S(1)}, u32[]{:S(2)}, u32[]{:S(2)}) %collective-permute-start.9) | collective-permute-done | bytes 262176 | tf_op jit(solution)/shard_map/ppermute | solution.py:255
  24.5 1.4 %collective-permute-start.10 = (bf16[256,512]{1,0:T(8,128)(2,1)S(1)}, bf16[256,512]{1,0:T(8,128)(2,1)}, u32[]{:S(2)}, u32[]{:S(2)}) collective-permute-start(bf16[256,512]{1,0:T(8,128)(2,1)S(1)} %collective-permute-done.9.refs_3_), channel_id=1, source_target_pairs={{4,8},{6,10},{8,12},{10,14},{5,9},{7,11},{9,13},{11,15},{20,24},{2... | collective-permute-start | bytes 786440 | tf_op jit(solution)/shard_map/ppermute | solution.py:255
  25.9 1.8 %pad_maximum_fusion = bf16[512,512]{1,0:T(8,128)(2,1)} fusion(bf16[256,512]{1,0:T(8,128)(2,1)S(1)} %collective-permute-done.4.refs_5_, bf16[128,512]{1,0:T(8,128)(2,1)} %copy-done.15, bf16[128,512]{1,0:T(8,128)(2,1)S(1)} %pad_maximum_fusion.2), kind=kLoop, calls=%fused_computation | loop fusion | flops 1572864 | bytes 1048576 | tf_op jit(solution)/shard_map/concatenate | solution.py:278
  27.7 1.7 %collective-permute-done.11.refs_5_ = bf16[256,512]{1,0:T(8,128)(2,1)S(1)} collective-permute-done((bf16[256,512]{1,0:T(8,128)(2,1)S(1)}, bf16[256,512]{1,0:T(8,128)(2,1)S(1)}, u32[]{:S(2)}, u32[]{:S(2)}) %collective-permute-start.11) | collective-permute-done | bytes 262176 | tf_op jit(solution)/shard_map/ppermute | solution.py:267
  32.2 15.5 %collective-permute-start.7 = (bf16[512,512]{1,0:T(8,128)(2,1)}, bf16[512,512]{1,0:T(8,128)(2,1)}, u32[]{:S(2)}, u32[]{:S(2)}) collective-permute-start(bf16[512,512]{1,0:T(8,128)(2,1)} %pad_maximum_fusion), channel_id=1, source_target_pairs={{0,12},{2,14},{1,13},{3,15},{16,28},{18,30},{17,29},{19,31}} | collective-permute-start | bytes 1572872 | tf_op jit(solution)/shard_map/ppermute | solution.py:267
  47.7 1.4 %collective-permute-start.14 = (bf16[256,512]{1,0:T(8,128)(2,1)}, bf16[256,512]{1,0:T(8,128)(2,1)}, u32[]{:S(2)}, u32[]{:S(2)}) collective-permute-start(bf16[256,512]{1,0:T(8,128)(2,1)} %collective-permute-done.10.refs_4_), channel_id=1, source_target_pairs={{8,10},{10,8},{12,14},{14,12},{9,11},{11,9},{13,15},{15,13},{24,26... | collective-permute-start | bytes 786440 | tf_op jit(solution)/shard_map/ppermute | solution.py:263
  49.8 1.4 %collective-permute-start.5 = (bf16[256,512]{1,0:T(8,128)(2,1)}, bf16[256,512]{1,0:T(8,128)(2,1)}, u32[]{:S(2)}, u32[]{:S(2)}) collective-permute-start(bf16[256,512]{1,0:T(8,128)(2,1)} %collective-permute-done.2.refs_3_), channel_id=1, source_target_pairs={{4,6},{6,4},{8,10},{10,8},{12,14},{14,12},{5,7},{7,5},{9,11},{11,9... | collective-permute-start | bytes 786440 | tf_op jit(solution)/shard_map/ppermute | solution.py:263
  51.9 1.3 %collective-permute-start.6 = (bf16[256,512]{1,0:T(8,128)(2,1)}, bf16[256,512]{1,0:T(8,128)(2,1)}, u32[]{:S(2)}, u32[]{:S(2)}) collective-permute-start(bf16[256,512]{1,0:T(8,128)(2,1)} %collective-permute-done.3.refs_4_), channel_id=1, source_target_pairs={{8,10},{10,8},{12,14},{14,12},{9,11},{11,9},{13,15},{15,13},{24,26... | collective-permute-start | bytes 786440 | tf_op jit(solution)/shard_map/ppermute | solution.py:263
  53.8 1.0 %copy-done.6 = bf16[256,512]{1,0:T(8,128)(2,1)S(1)} copy-done((bf16[256,512]{1,0:T(8,128)(2,1)S(1)}, bf16[256,512]{1,0:T(8,128)(2,1)}, u32[]{:S(2)}) %copy-start.6) | copy-done | bytes 262168
  54.8 0.9 %copy-done.8 = bf16[256,512]{1,0:T(8,128)(2,1)S(1)} copy-done((bf16[256,512]{1,0:T(8,128)(2,1)S(1)}, bf16[256,512]{1,0:T(8,128)(2,1)}, u32[]{:S(2)}) %copy-start.8) | copy-done | bytes 262168
  55.8 0.9 %copy-done.10 = bf16[256,512]{1,0:T(8,128)(2,1)S(1)} copy-done((bf16[256,512]{1,0:T(8,128)(2,1)S(1)}, bf16[256,512]{1,0:T(8,128)(2,1)}, u32[]{:S(2)}) %copy-start.10) | copy-done | bytes 262168
  56.7 0.9 %copy-done.12 = bf16[256,512]{1,0:T(8,128)(2,1)S(1)} copy-done((bf16[256,512]{1,0:T(8,128)(2,1)S(1)}, bf16[256,512]{1,0:T(8,128)(2,1)}, u32[]{:S(2)}) %copy-start.12) | copy-done | bytes 262168
  57.7 0.9 %copy-done.14 = bf16[256,512]{1,0:T(8,128)(2,1)S(1)} copy-done((bf16[256,512]{1,0:T(8,128)(2,1)S(1)}, bf16[256,512]{1,0:T(8,128)(2,1)}, u32[]{:S(2)}) %copy-start.14) | copy-done | bytes 262168
  58.6 7.2 %attend.2 = (bf16[128,8192]{1,0:T(8,128)(2,1)}, bf16[128,2048]{1,0:T(8,128)(2,1)}) custom-call(s32[386]{0:T(512)S(1)} %concatenate.25.table, bf16[128,8192]{1,0:T(8,128)(2,1)S(1)} %copy-done, bf16[128,4096]{1,0:T(8,128)(2,1)S(1)} %collective-permute-done.refs_1_, bf16[256,512]{1,0:T(8,128)(2,1)S(1)} %pad_maximum_fusion.1.refs_2_, ...), custom_call_target="tpu_custom_call" | custom-call | tf_op jit(solution)/shard_map/attend/pallas_call | solution.py:186
  66.0 7.5 %attend.3 = (bf16[128,8192]{1,0:T(8,128)(2,1)}, bf16[128,2048]{1,0:T(8,128)(2,1)}) custom-call(s32[386]{0:T(512)S(1)} %concatenate.25.table, bf16[128,8192]{1,0:T(8,128)(2,1)S(1)} %copy-done, bf16[128,4096]{1,0:T(8,128)(2,1)S(1)} %collective-permute-done.refs_1_, bf16[256,512]{1,0:T(8,128)(2,1)S(1)} %copy-done.4, ...), custom_call_target="tpu_custom_call", output_to_operand_aliasing={{0}: (10, {})} | custom-call | tf_op jit(solution)/shard_map/attend/pallas_call | solution.py:186
  74.0 1.9 %constant_dynamic-update-slice_fusion.3 = bf16[128,8192]{1,0:T(8,128)(2,1)} fusion(bf16[128,8192]{1,0:T(8,128)(2,1)} %get-tuple-element.14, bf16[128,2048]{1,0:T(8,128)(2,1)} %collective-permute-done.16, s32[]{:T(128)S(6)} %select_n.23), kind=kLoop, calls=%fused_computation.8 | loop fusion | bytes 1048580 | tf_op jit(solution)/shard_map/dynamic_update_slice | solution.py:295
  (74 shorter events, 8.9 us)
Async XLA Ops:
  1.8 11.1 %collective-permute-start.8 = (bf16[128,512]{1,0:T(8,128)(2,1)S(1)}, bf16[128,512]{1,0:T(8,128)(2,1)}, u32[]{:S(2)}, u32[]{:S(2)}) collective-permute-start(bf16[128,512]{1,0:T(8,128)(2,1)S(1)} %pad_maximum_fusion.4), channel_id=1, source_target_pairs={{0,1},{1,0},{2,3},{3,2},{4,5},{5,4},{6,7},{7,6},{8,9},{9,8},{10,11... | collective-permute-start | bytes 393224 | tf_op jit(solution)/shard_map/ppermute | solution.py:241
  3.0 3.1 %collective-permute-start.1 = (bf16[128,512]{1,0:T(8,128)(2,1)}, bf16[128,512]{1,0:T(8,128)(2,1)S(1)}, u32[]{:S(2)}, u32[]{:S(2)}) collective-permute-start(bf16[128,512]{1,0:T(8,128)(2,1)} %pad_maximum_fusion.3), channel_id=1, source_target_pairs={{0,1},{1,0},{2,3},{3,2},{4,5},{5,4},{6,7},{7,6},{8,9},{9,8},{10,11... | collective-permute-start | bytes 393224 | tf_op jit(solution)/shard_map/ppermute | solution.py:241
  3.1 50.1 %copy-start.18 = (s32[64,2]{0,1:T(2,128)S(1)}, s32[64,2]{0,1:T(2,128)}, u32[]{:S(2)}) copy-start(s32[64,2]{0,1:T(2,128)} %param.10) | copy-start | bytes 1540
  3.1 50.3 %copy-start.19 = (s32[64,2]{0,1:T(2,128)S(1)}, s32[64,2]{0,1:T(2,128)}, u32[]{:S(2)}) copy-start(s32[64,2]{0,1:T(2,128)} %param.12) | copy-start | bytes 1540
  3.1 50.6 %copy-start.20 = (s32[64]{0:T(128)S(1)}, s32[64]{0:T(128)}, u32[]{:S(2)}) copy-start(s32[64]{0:T(128)} %param.11) | copy-start | bytes 772
  3.1 50.6 %copy-start.21 = (s32[64]{0:T(128)S(1)}, s32[64]{0:T(128)}, u32[]{:S(2)}) copy-start(s32[64]{0:T(128)} %param.13) | copy-start | bytes 772
  3.1 50.7 %copy-start = (bf16[128,8192]{1,0:T(8,128)(2,1)S(1)}, bf16[128,8192]{1,0:T(8,128)(2,1)}, u32[]{:S(2)}) copy-start(bf16[128,8192]{1,0:T(8,128)(2,1)} %refs_0_.3) | copy-start | bytes 6291460
  5.6 48.2 %collective-permute-start = (bf16[128,4096]{1,0:T(8,128)(2,1)}, bf16[128,4096]{1,0:T(8,128)(2,1)S(1)}, u32[]{:S(2)}, u32[]{:S(2)}) collective-permute-start(bf16[128,4096]{1,0:T(8,128)(2,1)} %constant_dynamic-slice_fusion.8), channel_id=1, source_target_pairs={{0,1},{1,0},{2,3},{3,2},{4,5},{5,4},{6,7},{7,6},{8,9},{9,8},{10,11... | collective-permute-start | bytes 3145736 | tf_op jit(solution)/shard_map/ppermute | solution.py:243
  6.1 18.4 %copy-start.3 = (bf16[256,512]{1,0:T(8,128)(2,1)}, bf16[256,512]{1,0:T(8,128)(2,1)S(1)}, u32[]{:S(2)}) copy-start(bf16[256,512]{1,0:T(8,128)(2,1)S(1)} %constant_dynamic-update-slice_fusion.refs_2_) | copy-start | bytes 786436
  6.1 11.9 %collective-permute-start.4 = (bf16[256,512]{1,0:T(8,128)(2,1)S(1)}, bf16[256,512]{1,0:T(8,128)(2,1)S(1)}, u32[]{:S(2)}, u32[]{:S(2)}) collective-permute-start(bf16[256,512]{1,0:T(8,128)(2,1)S(1)} %constant_dynamic-update-slice_fusion.refs_2_), channel_id=1, source_target_pairs={{0,2},{2,0},{4,6},{6,4},{8,10},{10,8},{12,14},{14,12},{1,3},{3,1},... | collective-permute-start | bytes 786440 | tf_op jit(solution)/shard_map/ppermute | solution.py:263
  8.7 10.2 %collective-permute-start.2 = (bf16[256,512]{1,0:T(8,128)(2,1)S(1)}, bf16[256,512]{1,0:T(8,128)(2,1)}, u32[]{:S(2)}, u32[]{:S(2)}) collective-permute-start(bf16[256,512]{1,0:T(8,128)(2,1)S(1)} %constant_dynamic-update-slice_fusion.refs_2_), channel_id=1, source_target_pairs={{0,4},{2,6},{4,8},{6,10},{8,12},{10,14},{1,5},{3,7},{5,9},{7,11},{... | collective-permute-start | bytes 786440 | tf_op jit(solution)/shard_map/ppermute | solution.py:255
  13.9 10.7 %collective-permute-start.9 = (bf16[256,512]{1,0:T(8,128)(2,1)S(1)}, bf16[256,512]{1,0:T(8,128)(2,1)S(1)}, u32[]{:S(2)}, u32[]{:S(2)}) collective-permute-start(bf16[256,512]{1,0:T(8,128)(2,1)S(1)} %pad_maximum_fusion.1.refs_2_), channel_id=1, source_target_pairs={{0,4},{2,6},{4,8},{6,10},{8,12},{10,14},{1,5},{3,7},{5,9},{7,11},{... | collective-permute-start | bytes 786440 | tf_op jit(solution)/shard_map/ppermute | solution.py:255
  16.7 12.7 %collective-permute-start.11 = (bf16[256,512]{1,0:T(8,128)(2,1)S(1)}, bf16[256,512]{1,0:T(8,128)(2,1)S(1)}, u32[]{:S(2)}, u32[]{:S(2)}) collective-permute-start(bf16[256,512]{1,0:T(8,128)(2,1)S(1)} %pad_maximum_fusion.1.refs_2_), channel_id=1, source_target_pairs={{0,12},{2,14},{1,13},{3,15},{16,28},{18,30},{17,29},{19,31}} | collective-permute-start | bytes 786440 | tf_op jit(solution)/shard_map/ppermute | solution.py:267
  18.0 12.8 %collective-permute-start.12 = (bf16[256,512]{1,0:T(8,128)(2,1)S(1)}, bf16[256,512]{1,0:T(8,128)(2,1)S(1)}, u32[]{:S(2)}, u32[]{:S(2)}) collective-permute-start(bf16[256,512]{1,0:T(8,128)(2,1)S(1)} %pad_maximum_fusion.1.refs_2_), channel_id=1, source_target_pairs={{0,2},{2,0},{4,6},{6,4},{8,10},{10,8},{12,14},{14,12},{1,3},{3,1},... | collective-permute-start | bytes 786440 | tf_op jit(solution)/shard_map/ppermute | solution.py:263
  18.9 13.3 %collective-permute-start.3 = (bf16[256,512]{1,0:T(8,128)(2,1)}, bf16[256,512]{1,0:T(8,128)(2,1)}, u32[]{:S(2)}, u32[]{:S(2)}) collective-permute-start(bf16[256,512]{1,0:T(8,128)(2,1)} %collective-permute-done.2.refs_3_), channel_id=1, source_target_pairs={{4,8},{6,10},{8,12},{10,14},{5,9},{7,11},{9,13},{11,15},{20,24},{2... | collective-permute-start | bytes 786440 | tf_op jit(solution)/shard_map/ppermute | solution.py:255
  24.5 23.2 %collective-permute-start.10 = (bf16[256,512]{1,0:T(8,128)(2,1)S(1)}, bf16[256,512]{1,0:T(8,128)(2,1)}, u32[]{:S(2)}, u32[]{:S(2)}) collective-permute-start(bf16[256,512]{1,0:T(8,128)(2,1)S(1)} %collective-permute-done.9.refs_3_), channel_id=1, source_target_pairs={{4,8},{6,10},{8,12},{10,14},{5,9},{7,11},{9,13},{11,15},{20,24},{2... | collective-permute-start | bytes 786440 | tf_op jit(solution)/shard_map/ppermute | solution.py:255
  29.4 19.7 %collective-permute-start.15 = (bf16[256,512]{1,0:T(8,128)(2,1)S(1)}, bf16[256,512]{1,0:T(8,128)(2,1)S(1)}, u32[]{:S(2)}, u32[]{:S(2)}) collective-permute-start(bf16[256,512]{1,0:T(8,128)(2,1)S(1)} %collective-permute-done.11.refs_5_), channel_id=1, source_target_pairs={{12,14},{14,12},{13,15},{15,13},{28,30},{30,28},{29,31},{31,29}} | collective-permute-start | bytes 786440 | tf_op jit(solution)/shard_map/ppermute | solution.py:263
  31.5 19.6 %collective-permute-start.13 = (bf16[256,512]{1,0:T(8,128)(2,1)S(1)}, bf16[256,512]{1,0:T(8,128)(2,1)S(1)}, u32[]{:S(2)}, u32[]{:S(2)}) collective-permute-start(bf16[256,512]{1,0:T(8,128)(2,1)S(1)} %collective-permute-done.9.refs_3_), channel_id=1, source_target_pairs={{4,6},{6,4},{8,10},{10,8},{12,14},{14,12},{5,7},{7,5},{9,11},{11,9... | collective-permute-start | bytes 786440 | tf_op jit(solution)/shard_map/ppermute | solution.py:263
  32.2 33.7 %collective-permute-start.7 = (bf16[512,512]{1,0:T(8,128)(2,1)}, bf16[512,512]{1,0:T(8,128)(2,1)}, u32[]{:S(2)}, u32[]{:S(2)}) collective-permute-start(bf16[512,512]{1,0:T(8,128)(2,1)} %pad_maximum_fusion), channel_id=1, source_target_pairs={{0,12},{2,14},{1,13},{3,15},{16,28},{18,30},{17,29},{19,31}} | collective-permute-start | bytes 1572872 | tf_op jit(solution)/shard_map/ppermute | solution.py:267
  47.7 6.1 %collective-permute-start.14 = (bf16[256,512]{1,0:T(8,128)(2,1)}, bf16[256,512]{1,0:T(8,128)(2,1)}, u32[]{:S(2)}, u32[]{:S(2)}) collective-permute-start(bf16[256,512]{1,0:T(8,128)(2,1)} %collective-permute-done.10.refs_4_), channel_id=1, source_target_pairs={{8,10},{10,8},{12,14},{14,12},{9,11},{11,9},{13,15},{15,13},{24,26... | collective-permute-start | bytes 786440 | tf_op jit(solution)/shard_map/ppermute | solution.py:263
  49.8 16.1 %collective-permute-start.5 = (bf16[256,512]{1,0:T(8,128)(2,1)}, bf16[256,512]{1,0:T(8,128)(2,1)}, u32[]{:S(2)}, u32[]{:S(2)}) collective-permute-start(bf16[256,512]{1,0:T(8,128)(2,1)} %collective-permute-done.2.refs_3_), channel_id=1, source_target_pairs={{4,6},{6,4},{8,10},{10,8},{12,14},{14,12},{5,7},{7,5},{9,11},{11,9... | collective-permute-start | bytes 786440 | tf_op jit(solution)/shard_map/ppermute | solution.py:263
  51.9 14.1 %collective-permute-start.6 = (bf16[256,512]{1,0:T(8,128)(2,1)}, bf16[256,512]{1,0:T(8,128)(2,1)}, u32[]{:S(2)}, u32[]{:S(2)}) collective-permute-start(bf16[256,512]{1,0:T(8,128)(2,1)} %collective-permute-done.3.refs_4_), channel_id=1, source_target_pairs={{8,10},{10,8},{12,14},{14,12},{9,11},{11,9},{13,15},{15,13},{24,26... | collective-permute-start | bytes 786440 | tf_op jit(solution)/shard_map/ppermute | solution.py:263
  65.8 8.2 %collective-permute-start.16 = (bf16[128,2048]{1,0:T(8,128)(2,1)}, bf16[128,2048]{1,0:T(8,128)(2,1)}, u32[]{:S(2)}, u32[]{:S(2)}) collective-permute-start(bf16[128,2048]{1,0:T(8,128)(2,1)} %get-tuple-element.15), channel_id=1, source_target_pairs={{0,1},{1,0},{2,3},{3,2},{4,5},{5,4},{6,7},{7,6},{8,9},{9,8},{10,11... | collective-permute-start | bytes 1572872 | tf_op jit(solution)/shard_map/ppermute | solution.py:291
  73.5 2.4 %collective-permute-start.17 = (bf16[128,2048]{1,0:T(8,128)(2,1)}, bf16[128,2048]{1,0:T(8,128)(2,1)S(1)}, u32[]{:S(2)}, u32[]{:S(2)}) collective-permute-start(bf16[128,2048]{1,0:T(8,128)(2,1)} %get-tuple-element.16), channel_id=1, source_target_pairs={{0,1},{1,0},{2,3},{3,2},{4,5},{5,4},{6,7},{7,6},{8,9},{9,8},{10,11... | collective-permute-start | bytes 1572872 | tf_op jit(solution)/shard_map/ppermute | solution.py:293
  (16 other events, 78.9 us)
